TPU v7x, 32 devices: a whole 2x2x4 slice. The times are simulated.
32 devices in a mesh: section: 4 (over x, core), dp: 8 (over z, y).
Axes of the slice: x: 2, y: 2, z: 4, core: 2. Of those that a mesh axis runs over, the one named last changes fastest.
Arguments:
- tokens: bfloat16 [16, 1024, 768], P('dp'), may hold values from -6 to 6
- doc_ids: int32 [16, 1024], P('dp'), may hold values from 0 to 3, never falling along the last dimension, each value on 1 to 512 neighbouring positions
- reset_flags: int32 [16, 1], P('dp'), may hold values 0 or 1
- first_weights: bfloat16 [4, 768, 3072], P('section'), may hold values from -2 to 2
- down_halves: bfloat16 [4, 1536, 768], P('section'), may hold values from -0.109375 to 0.109375
- norm_gain: float32 [4, 768], P('section'), may hold values from 0.5 to 1.5
- norm_bias: float32 [4, 768], P('section'), may hold values from -2.5 to 2.5
- cotangent: bfloat16 [16, 1024, 768], P('dp'), may hold values from -6 to 6
Outputs:
- section_out: bfloat16 [4, 16, 1024, 768], P('section', 'dp')
- section_in_grad: bfloat16 [4, 16, 1024, 768], P('section', 'dp')
- first_grad: float32 [4, 768, 3072], P('section')
- down_grad: float32 [4, 1536, 768], P('section')
- gain_grad: float32 [4, 768], P('section')
- bias_grad: float32 [4, 768], P('section')
Inputs may be any that keep to these rules, and one draw needn't show every extreme that they name: doc_ids never fall along a sequence.
All inputs are finite; a program needn't handle non-finite values. No bound on the sum of `reset_flags` on one device may be relied on, other than what follows from the above.
Results may differ from a plain program's by a relative error of at most 0.023.
Values may be sent and summed in bfloat16 or wider, within the bound.
A program may use at most 192 MiB of HBM per device.

v0:
```python
from functools import partial

import jax
import jax.numpy as jnp
from jax import lax
from jax.sharding import PartitionSpec as P

H = 12
M = 20
NSEG = 2


NORM_EPSILON = 1e-05
MASKED_SCORE = -1000000000.0


def from_behind(shard, axis, by):
    devices = lax.axis_size(axis)
    pairs = [(i, i + by) for i in range(devices) if 0 <= i + by < devices]
    return lax.ppermute(shard, axis, pairs)


def shortened(shard):
    return jax.tree.map(lambda a: a.astype(jnp.bfloat16) if a.dtype == jnp.float32 else a, shard)


def norm_rows(summed, norm_scale, norm_shift):
    row_mean = jnp.mean(summed, axis=-1, keepdims=True)
    centered = summed - row_mean
    row_var = jnp.mean(centered * centered, axis=-1, keepdims=True)
    inv_std = lax.rsqrt(row_var + NORM_EPSILON)
    normed = centered * inv_std
    return (normed * norm_scale + norm_shift, normed, inv_std)


def norm_back(grad_out, normed, inv_std, norm_scale):
    scaled = grad_out * norm_scale
    row_term = jnp.mean(scaled, axis=-1, keepdims=True)
    row_cross = jnp.mean(scaled * normed, axis=-1, keepdims=True)
    return inv_std * (scaled - row_term - normed * row_cross)


def allowed_mask(doc_rows, memory_rows):
    marks = jnp.concatenate([jnp.full((memory_rows,), -1, jnp.int32), doc_rows])
    is_memory = lax.iota(jnp.int32, memory_rows + doc_rows.shape[0]) < memory_rows
    return is_memory[:, None] | is_memory[None, :] | (marks[:, None] == marks[None, :])


def split_heads(block_part, head_count):
    return block_part.reshape(block_part.shape[0], head_count, block_part.shape[1] // head_count)


def attention_scores(queries, keys, allowed):
    score_scale = queries.shape[2] ** (-0.5)
    scores = (
        jnp.einsum("rhd,khd->hrk", queries, keys, preferred_element_type=jnp.float32) * score_scale
    )
    return jnp.where(allowed[None], scores, MASKED_SCORE)


def attention_core(projected, allowed, head_count):
    row_count = projected.shape[0]
    feature_width = projected.shape[1] // 3
    queries = split_heads(projected[:, :feature_width], head_count)
    keys = split_heads(projected[:, feature_width : 2 * feature_width], head_count)
    values = split_heads(projected[:, 2 * feature_width :], head_count)
    scores = attention_scores(queries, keys, allowed)
    row_peak = jnp.max(scores, axis=2, keepdims=True)
    log_total = row_peak + jnp.log(jnp.sum(jnp.exp(scores - row_peak), axis=2, keepdims=True))
    attn_probs = jnp.exp(scores - log_total).astype(jnp.bfloat16)
    context = jnp.einsum("hrk,khd->rhd", attn_probs, values, preferred_element_type=jnp.float32)
    return (context.reshape(row_count, feature_width).astype(jnp.bfloat16), log_total[:, :, 0])


def attention_forward(inputs, first_matrix, norm_scale, norm_shift, allowed, head_count):
    feature_width = inputs.shape[1]
    projected = jnp.dot(
        inputs, first_matrix[:, : 3 * feature_width], preferred_element_type=jnp.float32
    ).astype(jnp.bfloat16)
    context, log_total = attention_core(projected, allowed, head_count)
    branch = jnp.dot(
        context, first_matrix[:, 3 * feature_width :], preferred_element_type=jnp.float32
    )
    outputs, normed, inv_std = norm_rows(
        inputs.astype(jnp.float32) + branch, norm_scale, norm_shift
    )
    return (outputs.astype(jnp.bfloat16), projected, context, log_total, normed, inv_std)


def attention_backward(
    inputs,
    grad_in,
    first_matrix,
    norm_scale,
    allowed,
    projected,
    context,
    log_total,
    normed,
    inv_std,
    head_count,
):
    row_count, feature_width = inputs.shape
    out_matrix = first_matrix[:, 3 * feature_width :]
    grad_out = grad_in.astype(jnp.float32)
    scale_part = jnp.sum(grad_out * normed, axis=0)
    shift_part = jnp.sum(grad_out, axis=0)
    grad_sum = norm_back(grad_out, normed, inv_std, norm_scale)
    grad_branch = grad_sum.astype(jnp.bfloat16)
    out_part = jnp.einsum("rd,re->de", context, grad_branch, preferred_element_type=jnp.float32)
    grad_context = jnp.einsum(
        "re,de->rd", grad_branch, out_matrix, preferred_element_type=jnp.float32
    ).astype(jnp.bfloat16)
    queries = split_heads(projected[:, :feature_width], head_count)
    keys = split_heads(projected[:, feature_width : 2 * feature_width], head_count)
    values = split_heads(projected[:, 2 * feature_width :], head_count)
    score_scale = queries.shape[2] ** (-0.5)
    attn_probs = jnp.exp(attention_scores(queries, keys, allowed) - log_total[:, :, None])
    grad_heads = split_heads(grad_context, head_count)
    grad_probs = jnp.einsum("rhd,khd->hrk", grad_heads, values, preferred_element_type=jnp.float32)
    grad_values = jnp.einsum(
        "hrk,rhd->khd",
        attn_probs.astype(jnp.bfloat16),
        grad_heads,
        preferred_element_type=jnp.float32,
    )
    row_inner = jnp.sum(grad_probs * attn_probs, axis=2, keepdims=True)
    grad_scores = (attn_probs * (grad_probs - row_inner)).astype(jnp.bfloat16)
    grad_queries = (
        jnp.einsum("hrk,khd->rhd", grad_scores, keys, preferred_element_type=jnp.float32)
        * score_scale
    )
    grad_keys = (
        jnp.einsum("hrk,rhd->khd", grad_scores, queries, preferred_element_type=jnp.float32)
        * score_scale
    )
    grad_projected = jnp.concatenate(
        [
            grad_queries.reshape(row_count, feature_width),
            grad_keys.reshape(row_count, feature_width),
            grad_values.reshape(row_count, feature_width),
        ],
        axis=1,
    ).astype(jnp.bfloat16)
    projected_part = jnp.einsum(
        "rd,re->de", inputs, grad_projected, preferred_element_type=jnp.float32
    )
    grad_inputs = (
        jnp.einsum(
            "re,de->rd",
            grad_projected,
            first_matrix[:, : 3 * feature_width],
            preferred_element_type=jnp.float32,
        )
        + grad_sum
    )
    return (
        grad_inputs.astype(jnp.bfloat16),
        jnp.concatenate([projected_part, out_part], axis=1),
        scale_part,
        shift_part,
    )


def feed_forward(inputs, up_matrix, down_matrix, norm_scale, norm_shift):
    pre_act = jnp.dot(inputs, up_matrix, preferred_element_type=jnp.float32)
    hidden = jax.nn.gelu(pre_act, approximate=False).astype(jnp.bfloat16)
    branch = jnp.dot(hidden, down_matrix, preferred_element_type=jnp.float32)
    outputs, normed, inv_std = norm_rows(
        inputs.astype(jnp.float32) + branch, norm_scale, norm_shift
    )
    return (outputs.astype(jnp.bfloat16), pre_act, normed, inv_std)


def feed_backward(inputs, grad_in, up_matrix, down_matrix, norm_scale, pre_act, normed, inv_std):
    hidden = jax.nn.gelu(pre_act, approximate=False).astype(jnp.bfloat16)
    grad_out = grad_in.astype(jnp.float32)
    scale_part = jnp.sum(grad_out * normed, axis=0)
    shift_part = jnp.sum(grad_out, axis=0)
    grad_sum = norm_back(grad_out, normed, inv_std, norm_scale)
    grad_branch = grad_sum.astype(jnp.bfloat16)
    down_part = jnp.einsum("rf,rd->fd", hidden, grad_branch, preferred_element_type=jnp.float32)
    grad_hidden = jnp.einsum(
        "rd,fd->rf", grad_branch, down_matrix, preferred_element_type=jnp.float32
    )
    gelu_back = jax.vjp(partial(jax.nn.gelu, approximate=False), pre_act)[1]
    grad_pre = gelu_back(grad_hidden)[0].astype(jnp.bfloat16)
    up_part = jnp.einsum("rd,rf->df", inputs, grad_pre, preferred_element_type=jnp.float32)
    grad_inputs = (
        jnp.einsum("rf,df->rd", grad_pre, up_matrix, preferred_element_type=jnp.float32) + grad_sum
    )
    return (grad_inputs.astype(jnp.bfloat16), up_part, down_part, scale_part, shift_part)


def locate_item(item_index, period, seq_count, seg_count):
    block_index = item_index // period
    sequence = item_index % period
    active = (item_index >= 0) & (block_index < seg_count) & (sequence < seq_count)
    return (jnp.clip(block_index, 0, seg_count - 1), jnp.clip(sequence, 0, seq_count - 1), active)


def store_item(buffer, position, content, active):
    previous = lax.dynamic_index_in_dim(buffer, position, 0, keepdims=False)
    return lax.dynamic_update_index_in_dim(
        buffer, jnp.where(active, content, previous), position, 0
    )


def store_rows(buffer, sequence, row_start, content, active):
    previous = lax.dynamic_slice(buffer, (sequence, row_start, 0), (1,) + content.shape)[0]
    return lax.dynamic_update_slice(
        buffer, jnp.where(active, content, previous)[None], (sequence, row_start, 0)
    )


def shards(
    tokens, doc_ids, reset_flags, first_weights, down_halves, norm_gain, norm_bias, cotangent
):
    section_count = lax.axis_size("section")
    section_index = lax.axis_index("section")
    seq_count, length, feature_width = tokens.shape
    seg_count = NSEG
    seg_len = length // seg_count
    mem_rows = M
    row_count = mem_rows + seg_len
    period = max(seq_count, section_count)
    item_count = seg_count * seq_count
    tick_count = (seg_count - 1) * period + seq_count + section_count - 1
    first_matrix = first_weights[0]
    down_own = down_halves[0]
    hidden_width = first_matrix.shape[1]
    half_rows = down_own.shape[0]
    norm_scale = norm_gain[0]
    norm_shift = norm_bias[0]
    down_before = from_behind(down_own, "section", 1)
    down_matrix = jnp.concatenate([down_before, down_own], axis=0)
    section_kind = 1 + section_index % 2
    empty_rows = jnp.zeros((row_count, feature_width), jnp.bfloat16)
    empty_memory = jnp.zeros((mem_rows, feature_width), jnp.bfloat16)

    def reset_of(sequence, segment):
        return lax.dynamic_slice(reset_flags, (sequence, jnp.maximum(segment - 1, 0)), (1, 1))[0, 0]

    def segment_rows(source, sequence, segment):
        return lax.dynamic_slice(
            source, (sequence, segment * seg_len, 0), (1, seg_len, feature_width)
        )[0]

    def segment_mask(sequence, segment):
        doc_rows = lax.dynamic_slice(doc_ids, (sequence, segment * seg_len), (1, seg_len))[0]
        return allowed_mask(doc_rows, mem_rows)

    def packed(outputs):
        return (outputs,)

    def forward_spare(inputs, allowed):
        return packed(jnp.zeros_like(inputs))

    def forward_attention(inputs, allowed):
        outputs, projected, context, log_total, normed, inv_std = attention_forward(
            inputs, first_matrix, norm_scale, norm_shift, allowed, H
        )
        return packed(outputs)

    def forward_feed(inputs, allowed):
        outputs, pre_act, normed, inv_std = feed_forward(
            inputs, first_matrix, down_matrix, norm_scale, norm_shift
        )
        return packed(outputs)

    input_store = jnp.zeros((item_count, row_count, feature_width), jnp.bfloat16)
    kept_store = ()
    out_store = jnp.zeros((seq_count, length, feature_width), jnp.bfloat16)
    memory_store = jnp.zeros((seq_count, mem_rows, feature_width), jnp.bfloat16)

    def forward_tick(tick_index, loop_state):
        input_store, kept_store, out_store, arriving, memory_arriving, memory_store = loop_state
        back_sequence, back_active = locate_item(
            tick_index - section_count, period, seq_count, seg_count
        )[1:]
        memory_store = store_item(memory_store, back_sequence, memory_arriving, back_active)
        segment, sequence, active = locate_item(
            tick_index - section_index, period, seq_count, seg_count
        )
        restart = (segment == 0) | (reset_of(sequence, segment) > 0)
        memory = jnp.where(
            restart,
            empty_memory,
            lax.dynamic_index_in_dim(memory_store, sequence, 0, keepdims=False),
        )
        entering = jnp.concatenate([memory, segment_rows(tokens, sequence, segment)], axis=0)
        inputs = jnp.where(section_index == 0, entering, arriving)
        allowed = segment_mask(sequence, segment)
        results = lax.switch(
            jnp.where(active, section_kind, 0),
            [forward_spare, forward_attention, forward_feed],
            inputs,
            allowed,
        )
        outputs = results[0]
        slot_index = segment * seq_count + sequence
        input_store = store_item(input_store, slot_index, inputs, active)
        out_store = store_rows(out_store, sequence, segment * seg_len, outputs[mem_rows:], active)
        arriving = jax.tree.map(
            lambda part, own: part.astype(own.dtype),
            from_behind(shortened(outputs), "section", 1),
            outputs,
        )
        memory_arriving = from_behind(shortened(outputs[:mem_rows]), "section", 1 - section_count)
        return (input_store, kept_store, out_store, arriving, memory_arriving, memory_store)

    forward_state = (input_store, kept_store, out_store, empty_rows, empty_memory, memory_store)
    forward_state = lax.fori_loop(0, tick_count, forward_tick, forward_state)
    input_store, kept_store, out_store = forward_state[:3]

    def backward_spare(inputs, grad_in, allowed, slot_index, grad_accum):
        return (jnp.zeros_like(inputs), grad_accum)

    def backward_attention(inputs, grad_in, allowed, slot_index, grad_accum):
        projected = jnp.dot(
            inputs, first_matrix[:, : 3 * feature_width], preferred_element_type=jnp.float32
        ).astype(jnp.bfloat16)
        context, log_total = attention_core(projected, allowed, H)
        branch = jnp.dot(
            context, first_matrix[:, 3 * feature_width :], preferred_element_type=jnp.float32
        )
        normed, inv_std = norm_rows(inputs.astype(jnp.float32) + branch, norm_scale, norm_shift)[1:]
        grad_inputs, first_part, scale_part, shift_part = attention_backward(
            inputs,
            grad_in,
            first_matrix,
            norm_scale,
            allowed,
            projected,
            context,
            log_total,
            normed,
            inv_std,
            H,
        )
        return (
            grad_inputs,
            (
                grad_accum[0] + first_part,
                grad_accum[1],
                grad_accum[2] + scale_part,
                grad_accum[3] + shift_part,
            ),
        )

    def backward_feed(inputs, grad_in, allowed, slot_index, grad_accum):
        pre_act = jnp.dot(inputs, first_matrix, preferred_element_type=jnp.float32)
        hidden = jax.nn.gelu(pre_act, approximate=False).astype(jnp.bfloat16)
        branch = jnp.dot(hidden, down_matrix, preferred_element_type=jnp.float32)
        normed, inv_std = norm_rows(inputs.astype(jnp.float32) + branch, norm_scale, norm_shift)[1:]
        grad_inputs, up_part, down_part, scale_part, shift_part = feed_backward(
            inputs, grad_in, first_matrix, down_matrix, norm_scale, pre_act, normed, inv_std
        )
        return (
            grad_inputs,
            (
                grad_accum[0] + up_part,
                grad_accum[1] + down_part,
                grad_accum[2] + scale_part,
                grad_accum[3] + shift_part,
            ),
        )

    def backward_tick(tick_index, loop_state):
        grad_accum, grad_store, arriving, memory_arriving, memory_store = loop_state
        back_sequence, back_active = locate_item(
            tick_index - section_count, period, seq_count, seg_count
        )[1:]
        memory_store = store_item(memory_store, back_sequence, memory_arriving, back_active)
        reverse_index, sequence, active = locate_item(
            tick_index - (section_count - 1 - section_index), period, seq_count, seg_count
        )
        segment = seg_count - 1 - reverse_index
        memory_grad = jnp.where(
            reverse_index == 0,
            empty_memory,
            lax.dynamic_index_in_dim(memory_store, sequence, 0, keepdims=False),
        )
        leaving = jnp.concatenate([memory_grad, segment_rows(cotangent, sequence, segment)], axis=0)
        grad_in = jnp.where(section_index == section_count - 1, leaving, arriving)
        slot_index = segment * seq_count + sequence
        inputs = lax.dynamic_index_in_dim(input_store, slot_index, 0, keepdims=False)
        allowed = segment_mask(sequence, segment)
        grad_inputs, grad_accum = lax.switch(
            jnp.where(active, section_kind, 0),
            [backward_spare, backward_attention, backward_feed],
            inputs,
            grad_in,
            allowed,
            slot_index,
            grad_accum,
        )
        grad_store = store_rows(
            grad_store, sequence, segment * seg_len, grad_inputs[mem_rows:], active
        )
        passing = active & (section_index == 0) & (segment > 0) & (reset_of(sequence, segment) == 0)
        memory_out = jnp.where(passing, grad_inputs[:mem_rows], empty_memory)
        arriving = jax.tree.map(
            lambda part, own: part.astype(own.dtype),
            from_behind(shortened(grad_inputs), "section", -1),
            grad_inputs,
        )
        memory_arriving = from_behind(shortened(memory_out), "section", section_count - 1).astype(
            memory_out.dtype
        )
        return (grad_accum, grad_store, arriving, memory_arriving, memory_store)

    zero_first = jnp.zeros((feature_width, hidden_width), jnp.float32)
    zero_vector = jnp.zeros((feature_width,), jnp.float32)
    grad_accum = (
        zero_first,
        jnp.zeros((2 * half_rows, feature_width), jnp.float32),
        zero_vector,
        zero_vector,
    )
    backward_state = (
        grad_accum,
        jnp.zeros((seq_count, length, feature_width), jnp.bfloat16),
        empty_rows,
        empty_memory,
        jnp.zeros((seq_count, mem_rows, feature_width), jnp.bfloat16),
    )
    backward_state = lax.fori_loop(0, tick_count, backward_tick, backward_state)
    grad_accum, grad_store = (backward_state[0], backward_state[1])
    down_accum = grad_accum[1]
    after_grad = from_behind(down_accum[:half_rows].astype(jnp.bfloat16), "section", -1).astype(
        jnp.float32
    )
    down_local = jnp.where(section_index % 2 == 0, after_grad, down_accum[half_rows:])
    first_grad, down_grad, scale_grad, shift_grad = lax.psum(
        (grad_accum[0], down_local, grad_accum[2], grad_accum[3]), "dp"
    )
    return (
        out_store[None],
        grad_store[None],
        first_grad[None],
        down_grad[None],
        scale_grad[None],
        shift_grad[None],
    )


def solution(mesh):
    in_specs = (
        P("dp", None, None),
        P("dp", None),
        P("dp", None),
        P("section", None, None),
        P("section", None, None),
        P("section", None),
        P("section", None),
        P("dp", None, None),
    )
    out_specs = (
        P("section", "dp", None, None),
        P("section", "dp", None, None),
        P("section", None, None),
        P("section", None, None),
        P("section", None),
        P("section", None),
    )
    return jax.shard_map(shards, mesh=mesh, in_specs=in_specs, out_specs=out_specs, check_vma=False)
```

profile of v0, /device:TPU:0, one launch (start us, length us, event | category | flops | bytes accessed | tf_op | source)
XLA Modules:
  0.0 2010.7 jit_solution(12865108791364635912)
XLA Ops:
  22.0 407.0 %while.54 = (s32[]{:T(128)}, bf16[4,532,768]{2,1,0:T(8,128)(2,1)}, bf16[2,1024,768]{2,1,0:T(8,128)(2,1)}, bf16[532,768]{1,0:T(8,128)(2,1)S(1)}, bf16[20,768]{1,0...) while((s32[]{:T(128)}, bf16[4,532,768]{2,1,0:T(8,128)(2,1)}, ...), condition=%wide.region_10.11_spmd, body=%wide.region_0.10_spmd.sunk | while | flops 5134181888 | bytes 95267168 | solution.py:313
  27.2 38.9 %conditional.4 = (bf16[532,768]{1,0:T(8,128)(2,1)}) conditional(s32[]{:T(128)} %clamp.24, () %tuple.148, (bf16[532,768]{1,0:T(8,128)(2,1)S(1)}, bf16[768,3072]{1,0:T(8,128)(2,1)}, s32[532,1]{0,1:T(1,128)S(1)}, s32[1,532]{1,0:T(1,128)S(1)}, s32[2,1024]{1,0:T(2,128)S(1)}, /*index=5*/s32[]{:T(128)}, s32[]{:T(128)}, ...), branch_computations={%region_1.1_spmd, %region_2.6_spmd, %region_7.9_spmd} | conditional | flops 5131306496 | bytes 80342600 | solution.py:294
  78.6 38.9 %conditional.4 = (bf16[532,768]{1,0:T(8,128)(2,1)}) conditional(s32[]{:T(128)} %clamp.24, () %tuple.148, (bf16[532,768]{1,0:T(8,128)(2,1)S(1)}, bf16[768,3072]{1,0:T(8,128)(2,1)}, s32[532,1]{0,1:T(1,128)S(1)}, s32[1,532]{1,0:T(1,128)S(1)}, s32[2,1024]{1,0:T(2,128)S(1)}, /*index=5*/s32[]{:T(128)}, s32[]{:T(128)}, ...), branch_computations={%region_1.1_spmd, %region_2.6_spmd, %region_7.9_spmd} | conditional | flops 5131306496 | bytes 80342600 | solution.py:294
  130.9 20.7 %collective-permute-start = (bf16[532,768]{1,0:T(8,128)(2,1)}, bf16[532,768]{1,0:T(8,128)(2,1)S(1)}, u32[]{:S(2)}, u32[]{:S(2)}) collective-permute-start(bf16[532,768]{1,0:T(8,128)(2,1)} %get-tuple-element.1715), channel_id=1, source_target_pairs={{0,8},{8,16},{16,24},{1,9},{9,17},{17,25},{2,10},{10,18},{18,26},{... | collective-permute-start | bytes 2451464 | tf_op jit(solution)/shard_map/while/body/eval_jaxpr/ppermute | solution.py:20
  198.6 38.9 %conditional.4 = (bf16[532,768]{1,0:T(8,128)(2,1)}) conditional(s32[]{:T(128)} %clamp.24, () %tuple.148, (bf16[532,768]{1,0:T(8,128)(2,1)S(1)}, bf16[768,3072]{1,0:T(8,128)(2,1)}, s32[532,1]{0,1:T(1,128)S(1)}, s32[1,532]{1,0:T(1,128)S(1)}, s32[2,1024]{1,0:T(2,128)S(1)}, /*index=5*/s32[]{:T(128)}, s32[]{:T(128)}, ...), branch_computations={%region_1.1_spmd, %region_2.6_spmd, %region_7.9_spmd} | conditional | flops 5131306496 | bytes 80342600 | solution.py:294
  256.6 38.9 %conditional.4 = (bf16[532,768]{1,0:T(8,128)(2,1)}) conditional(s32[]{:T(128)} %clamp.24, () %tuple.148, (bf16[532,768]{1,0:T(8,128)(2,1)S(1)}, bf16[768,3072]{1,0:T(8,128)(2,1)}, s32[532,1]{0,1:T(1,128)S(1)}, s32[1,532]{1,0:T(1,128)S(1)}, s32[2,1024]{1,0:T(2,128)S(1)}, /*index=5*/s32[]{:T(128)}, s32[]{:T(128)}, ...), branch_computations={%region_1.1_spmd, %region_2.6_spmd, %region_7.9_spmd} | conditional | flops 5131306496 | bytes 80342600 | solution.py:294
  308.8 20.7 %collective-permute-start = (bf16[532,768]{1,0:T(8,128)(2,1)}, bf16[532,768]{1,0:T(8,128)(2,1)S(1)}, u32[]{:S(2)}, u32[]{:S(2)}) collective-permute-start(bf16[532,768]{1,0:T(8,128)(2,1)} %get-tuple-element.1715), channel_id=1, source_target_pairs={{0,8},{8,16},{16,24},{1,9},{9,17},{17,25},{2,10},{10,18},{18,26},{... | collective-permute-start | bytes 2451464 | tf_op jit(solution)/shard_map/while/body/eval_jaxpr/ppermute | solution.py:20
  357.0 13.9 collective-permute-done.1
  377.0 32.3 %collective-permute-start = (bf16[532,768]{1,0:T(8,128)(2,1)}, bf16[532,768]{1,0:T(8,128)(2,1)S(1)}, u32[]{:S(2)}, u32[]{:S(2)}) collective-permute-start(bf16[532,768]{1,0:T(8,128)(2,1)} %get-tuple-element.1715), channel_id=1, source_target_pairs={{0,8},{8,16},{16,24},{1,9},{9,17},{17,25},{2,10},{10,18},{18,26},{... | collective-permute-start | bytes 2451464 | tf_op jit(solution)/shard_map/while/body/eval_jaxpr/ppermute | solution.py:20
  414.9 12.2 collective-permute-done.1
  441.0 1073.8 %while.55 = (s32[]{:T(128)}, f32[768,3072]{0,1:T(8,128)}, f32[3072,768]{1,0:T(8,128)}, f32[768]{0:T(1024)S(1)}, f32[768]{0:T(1024)S(1)}, /*index=5*/bf16[2,1024,...) while((s32[]{:T(128)}, f32[768,3072]{0,1:T(8,128)}, ...), condition=%wide.region_30.31_spmd, body=%wide.region_11.30_spmd.sunk | while | flops 15216034816 | bytes 364196096 | solution.py:428
  453.2 70.4 %collective-permute-start.3 = (bf16[20,768]{1,0:T(8,128)(2,1)S(1)}, bf16[20,768]{1,0:T(8,128)(2,1)S(1)}, u32[]{:S(2)}, u32[]{:S(2)}) collective-permute-start(bf16[20,768]{1,0:T(8,128)(2,1)S(1)} %broadcast_select_fusion.2), channel_id=1, source_target_pairs={{0,24},{1,25},{2,26},{3,27},{4,28},{5,29},{6,30},{7,31}} | collective-permute-start | bytes 92168 | tf_op jit(solution)/shard_map/while/body/eval_jaxpr/ppermute | solution.py:20
  537.5 111.9 %collective-permute-start.3 = (bf16[20,768]{1,0:T(8,128)(2,1)S(1)}, bf16[20,768]{1,0:T(8,128)(2,1)S(1)}, u32[]{:S(2)}, u32[]{:S(2)}) collective-permute-start(bf16[20,768]{1,0:T(8,128)(2,1)S(1)} %broadcast_select_fusion.2), channel_id=1, source_target_pairs={{0,24},{1,25},{2,26},{3,27},{4,28},{5,29},{6,30},{7,31}} | collective-permute-start | bytes 92168 | tf_op jit(solution)/shard_map/while/body/eval_jaxpr/ppermute | solution.py:20
  663.2 119.8 %collective-permute-start.3 = (bf16[20,768]{1,0:T(8,128)(2,1)S(1)}, bf16[20,768]{1,0:T(8,128)(2,1)S(1)}, u32[]{:S(2)}, u32[]{:S(2)}) collective-permute-start(bf16[20,768]{1,0:T(8,128)(2,1)S(1)} %broadcast_select_fusion.2), channel_id=1, source_target_pairs={{0,24},{1,25},{2,26},{3,27},{4,28},{5,29},{6,30},{7,31}} | collective-permute-start | bytes 92168 | tf_op jit(solution)/shard_map/while/body/eval_jaxpr/ppermute | solution.py:20
  792.2 114.3 %conditional.5 = (bf16[532,768]{1,0:T(8,128)(2,1)}, f32[768,3072]{0,1:T(8,128)}, f32[3072,768]{1,0:T(8,128)}, f32[768]{0:T(1024)S(1)}, f32[768]{0:T(1024)S(1)}, ...) conditional(s32[]{:T(128)} %clamp.25, (f32[768,3072]{0,1:T(8,128)}, ...), branch_computations={%region_12.12_spmd, %region_13.22_spmd, %region_23.29_spmd} | conditional | flops 15213552640 | bytes 347656000 | solution.py:389
  921.0 114.2 %conditional.5 = (bf16[532,768]{1,0:T(8,128)(2,1)}, f32[768,3072]{0,1:T(8,128)}, f32[3072,768]{1,0:T(8,128)}, f32[768]{0:T(1024)S(1)}, f32[768]{0:T(1024)S(1)}, ...) conditional(s32[]{:T(128)} %clamp.25, (f32[768,3072]{0,1:T(8,128)}, ...), branch_computations={%region_12.12_spmd, %region_13.22_spmd, %region_23.29_spmd} | conditional | flops 15213552640 | bytes 347656000 | solution.py:389
  993.0 12.3 multiply_convert_fusion
  1055.9 68.3 %collective-permute-start.3 = (bf16[20,768]{1,0:T(8,128)(2,1)S(1)}, bf16[20,768]{1,0:T(8,128)(2,1)S(1)}, u32[]{:S(2)}, u32[]{:S(2)}) collective-permute-start(bf16[20,768]{1,0:T(8,128)(2,1)S(1)} %broadcast_select_fusion.2), channel_id=1, source_target_pairs={{0,24},{1,25},{2,26},{3,27},{4,28},{5,29},{6,30},{7,31}} | collective-permute-start | bytes 92168 | tf_op jit(solution)/shard_map/while/body/eval_jaxpr/ppermute | solution.py:20
  1138.3 113.6 %collective-permute-start.3 = (bf16[20,768]{1,0:T(8,128)(2,1)S(1)}, bf16[20,768]{1,0:T(8,128)(2,1)S(1)}, u32[]{:S(2)}, u32[]{:S(2)}) collective-permute-start(bf16[20,768]{1,0:T(8,128)(2,1)S(1)} %broadcast_select_fusion.2), channel_id=1, source_target_pairs={{0,24},{1,25},{2,26},{3,27},{4,28},{5,29},{6,30},{7,31}} | collective-permute-start | bytes 92168 | tf_op jit(solution)/shard_map/while/body/eval_jaxpr/ppermute | solution.py:20
  1261.1 114.1 %conditional.5 = (bf16[532,768]{1,0:T(8,128)(2,1)}, f32[768,3072]{0,1:T(8,128)}, f32[3072,768]{1,0:T(8,128)}, f32[768]{0:T(1024)S(1)}, f32[768]{0:T(1024)S(1)}, ...) conditional(s32[]{:T(128)} %clamp.25, (f32[768,3072]{0,1:T(8,128)}, ...), branch_computations={%region_12.12_spmd, %region_13.22_spmd, %region_23.29_spmd} | conditional | flops 15213552640 | bytes 347656000 | solution.py:389
  1332.9 12.3 multiply_convert_fusion
  1390.1 114.0 %conditional.5 = (bf16[532,768]{1,0:T(8,128)(2,1)}, f32[768,3072]{0,1:T(8,128)}, f32[3072,768]{1,0:T(8,128)}, f32[768]{0:T(1024)S(1)}, f32[768]{0:T(1024)S(1)}, ...) conditional(s32[]{:T(128)} %clamp.25, (f32[768,3072]{0,1:T(8,128)}, ...), branch_computations={%region_12.12_spmd, %region_13.22_spmd, %region_23.29_spmd} | conditional | flops 15213552640 | bytes 347656000 | solution.py:389
  1534.1 23.3 %all-reduce.2 = (f32[1,768]{1,0:T(1,128)}, f32[1,768]{1,0:T(1,128)}) all-reduce(f32[1,768]{1,0:T(1,128)S(1)} %broadcast_in_dim.195, f32[1,768]{1,0:T(1,128)S(1)} %broadcast_in_dim.196), channel_id=1, replica_groups=mesh['section'=4,'dp'=8] {'dp'}, use_global_device_ids=true, to_apply=%region_33.34 | all-reduce | flops 1536 | bytes 12288 | tf_op jit(solution)/shard_map/psum | solution.py:435
  1557.4 434.8 %all-reduce.6.cloned.1.call-done = (f32[1,768,3072]{2,1,0:T(8,128)}, f32[1,1536,768]{2,1,0:T(8,128)}) async-done(((f32[1,768,3072]{2,1,0:T(8,128)}, f32[1,1536,768]{2,1,0:T(8,128)}), (f32[1,768,3072]{2,1,0:T(8,128)}, f32[1,1536,768]{2,1,0:T(8,128)})) %all-reduce.6.cloned.1.call-update) | async-done | bytes 14155792 | tf_op jit(solution)/shard_map/psum | solution.py:435
  (767 shorter events, 878.9 us)
Async XLA Ops:
  7.2 1985.1 %all-reduce.6.cloned.1.call-start = ((), (), s32[]{:S(2)}) async-start(), calls=%async_computation | async-start | bytes 28311552 | tf_op jit(solution)/shard_map/psum | solution.py:435
  66.1 7.4 collective-permute-start
  117.5 7.4 collective-permute-start
  130.9 26.8 %collective-permute-start = (bf16[532,768]{1,0:T(8,128)(2,1)}, bf16[532,768]{1,0:T(8,128)(2,1)S(1)}, u32[]{:S(2)}, u32[]{:S(2)}) collective-permute-start(bf16[532,768]{1,0:T(8,128)(2,1)} %get-tuple-element.1715), channel_id=1, source_target_pairs={{0,8},{8,16},{16,24},{1,9},{9,17},{17,25},{2,10},{10,18},{18,26},{... | collective-permute-start | bytes 2451464 | tf_op jit(solution)/shard_map/while/body/eval_jaxpr/ppermute | solution.py:20
  163.8 29.7 %collective-permute-start = (bf16[532,768]{1,0:T(8,128)(2,1)}, bf16[532,768]{1,0:T(8,128)(2,1)S(1)}, u32[]{:S(2)}, u32[]{:S(2)}) collective-permute-start(bf16[532,768]{1,0:T(8,128)(2,1)} %get-tuple-element.1715), channel_id=1, source_target_pairs={{0,8},{8,16},{16,24},{1,9},{9,17},{17,25},{2,10},{10,18},{18,26},{... | collective-permute-start | bytes 2451464 | tf_op jit(solution)/shard_map/while/body/eval_jaxpr/ppermute | solution.py:20
  176.5 17.0 collective-permute-start.1
  237.5 14.0 collective-permute-start
  239.6 11.9 collective-permute-start.1
  308.8 26.8 %collective-permute-start = (bf16[532,768]{1,0:T(8,128)(2,1)}, bf16[532,768]{1,0:T(8,128)(2,1)S(1)}, u32[]{:S(2)}, u32[]{:S(2)}) collective-permute-start(bf16[532,768]{1,0:T(8,128)(2,1)} %get-tuple-element.1715), channel_id=1, source_target_pairs={{0,8},{8,16},{16,24},{1,9},{9,17},{17,25},{2,10},{10,18},{18,26},{... | collective-permute-start | bytes 2451464 | tf_op jit(solution)/shard_map/while/body/eval_jaxpr/ppermute | solution.py:20
  341.7 29.3 %collective-permute-start = (bf16[532,768]{1,0:T(8,128)(2,1)}, bf16[532,768]{1,0:T(8,128)(2,1)S(1)}, u32[]{:S(2)}, u32[]{:S(2)}) collective-permute-start(bf16[532,768]{1,0:T(8,128)(2,1)} %get-tuple-element.1715), channel_id=1, source_target_pairs={{0,8},{8,16},{16,24},{1,9},{9,17},{17,25},{2,10},{10,18},{18,26},{... | collective-permute-start | bytes 2451464 | tf_op jit(solution)/shard_map/while/body/eval_jaxpr/ppermute | solution.py:20
  352.2 18.7 collective-permute-start.1
  377.0 50.1 %collective-permute-start = (bf16[532,768]{1,0:T(8,128)(2,1)}, bf16[532,768]{1,0:T(8,128)(2,1)S(1)}, u32[]{:S(2)}, u32[]{:S(2)}) collective-permute-start(bf16[532,768]{1,0:T(8,128)(2,1)} %get-tuple-element.1715), channel_id=1, source_target_pairs={{0,8},{8,16},{16,24},{1,9},{9,17},{17,25},{2,10},{10,18},{18,26},{... | collective-permute-start | bytes 2451464 | tf_op jit(solution)/shard_map/while/body/eval_jaxpr/ppermute | solution.py:20
  410.1 17.0 collective-permute-start.1
  450.7 75.3 %collective-permute-start.2 = (bf16[532,768]{1,0:T(8,128)(2,1)}, bf16[532,768]{1,0:T(8,128)(2,1)S(1)}, u32[]{:S(2)}, u32[]{:S(2)}) collective-permute-start(bf16[532,768]{1,0:T(8,128)(2,1)} %get-tuple-element.1522), channel_id=1, source_target_pairs={{8,0},{16,8},{24,16},{9,1},{17,9},{25,17},{10,2},{18,10},{26,18},{... | collective-permute-start | bytes 2451464 | tf_op jit(solution)/shard_map/while/body/eval_jaxpr/ppermute | solution.py:20
  453.2 72.7 %collective-permute-start.3 = (bf16[20,768]{1,0:T(8,128)(2,1)S(1)}, bf16[20,768]{1,0:T(8,128)(2,1)S(1)}, u32[]{:S(2)}, u32[]{:S(2)}) collective-permute-start(bf16[20,768]{1,0:T(8,128)(2,1)S(1)} %broadcast_select_fusion.2), channel_id=1, source_target_pairs={{0,24},{1,25},{2,26},{3,27},{4,28},{5,29},{6,30},{7,31}} | collective-permute-start | bytes 92168 | tf_op jit(solution)/shard_map/while/body/eval_jaxpr/ppermute | solution.py:20
  534.9 116.8 %collective-permute-start.2 = (bf16[532,768]{1,0:T(8,128)(2,1)}, bf16[532,768]{1,0:T(8,128)(2,1)S(1)}, u32[]{:S(2)}, u32[]{:S(2)}) collective-permute-start(bf16[532,768]{1,0:T(8,128)(2,1)} %get-tuple-element.1522), channel_id=1, source_target_pairs={{8,0},{16,8},{24,16},{9,1},{17,9},{25,17},{10,2},{18,10},{26,18},{... | collective-permute-start | bytes 2451464 | tf_op jit(solution)/shard_map/while/body/eval_jaxpr/ppermute | solution.py:20
  537.5 114.2 %collective-permute-start.3 = (bf16[20,768]{1,0:T(8,128)(2,1)S(1)}, bf16[20,768]{1,0:T(8,128)(2,1)S(1)}, u32[]{:S(2)}, u32[]{:S(2)}) collective-permute-start(bf16[20,768]{1,0:T(8,128)(2,1)S(1)} %broadcast_select_fusion.2), channel_id=1, source_target_pairs={{0,24},{1,25},{2,26},{3,27},{4,28},{5,29},{6,30},{7,31}} | collective-permute-start | bytes 92168 | tf_op jit(solution)/shard_map/while/body/eval_jaxpr/ppermute | solution.py:20
  660.6 124.6 %collective-permute-start.2 = (bf16[532,768]{1,0:T(8,128)(2,1)}, bf16[532,768]{1,0:T(8,128)(2,1)S(1)}, u32[]{:S(2)}, u32[]{:S(2)}) collective-permute-start(bf16[532,768]{1,0:T(8,128)(2,1)} %get-tuple-element.1522), channel_id=1, source_target_pairs={{8,0},{16,8},{24,16},{9,1},{17,9},{25,17},{10,2},{18,10},{26,18},{... | collective-permute-start | bytes 2451464 | tf_op jit(solution)/shard_map/while/body/eval_jaxpr/ppermute | solution.py:20
  663.2 122.0 %collective-permute-start.3 = (bf16[20,768]{1,0:T(8,128)(2,1)S(1)}, bf16[20,768]{1,0:T(8,128)(2,1)S(1)}, u32[]{:S(2)}, u32[]{:S(2)}) collective-permute-start(bf16[20,768]{1,0:T(8,128)(2,1)S(1)} %broadcast_select_fusion.2), channel_id=1, source_target_pairs={{0,24},{1,25},{2,26},{3,27},{4,28},{5,29},{6,30},{7,31}} | collective-permute-start | bytes 92168 | tf_op jit(solution)/shard_map/while/body/eval_jaxpr/ppermute | solution.py:20
  1053.4 73.1 %collective-permute-start.2 = (bf16[532,768]{1,0:T(8,128)(2,1)}, bf16[532,768]{1,0:T(8,128)(2,1)S(1)}, u32[]{:S(2)}, u32[]{:S(2)}) collective-permute-start(bf16[532,768]{1,0:T(8,128)(2,1)} %get-tuple-element.1522), channel_id=1, source_target_pairs={{8,0},{16,8},{24,16},{9,1},{17,9},{25,17},{10,2},{18,10},{26,18},{... | collective-permute-start | bytes 2451464 | tf_op jit(solution)/shard_map/while/body/eval_jaxpr/ppermute | solution.py:20
  1055.9 70.5 %collective-permute-start.3 = (bf16[20,768]{1,0:T(8,128)(2,1)S(1)}, bf16[20,768]{1,0:T(8,128)(2,1)S(1)}, u32[]{:S(2)}, u32[]{:S(2)}) collective-permute-start(bf16[20,768]{1,0:T(8,128)(2,1)S(1)} %broadcast_select_fusion.2), channel_id=1, source_target_pairs={{0,24},{1,25},{2,26},{3,27},{4,28},{5,29},{6,30},{7,31}} | collective-permute-start | bytes 92168 | tf_op jit(solution)/shard_map/while/body/eval_jaxpr/ppermute | solution.py:20
  1135.7 118.5 %collective-permute-start.2 = (bf16[532,768]{1,0:T(8,128)(2,1)}, bf16[532,768]{1,0:T(8,128)(2,1)S(1)}, u32[]{:S(2)}, u32[]{:S(2)}) collective-permute-start(bf16[532,768]{1,0:T(8,128)(2,1)} %get-tuple-element.1522), channel_id=1, source_target_pairs={{8,0},{16,8},{24,16},{9,1},{17,9},{25,17},{10,2},{18,10},{26,18},{... | collective-permute-start | bytes 2451464 | tf_op jit(solution)/shard_map/while/body/eval_jaxpr/ppermute | solution.py:20
  1138.3 115.9 %collective-permute-start.3 = (bf16[20,768]{1,0:T(8,128)(2,1)S(1)}, bf16[20,768]{1,0:T(8,128)(2,1)S(1)}, u32[]{:S(2)}, u32[]{:S(2)}) collective-permute-start(bf16[20,768]{1,0:T(8,128)(2,1)S(1)} %broadcast_select_fusion.2), channel_id=1, source_target_pairs={{0,24},{1,25},{2,26},{3,27},{4,28},{5,29},{6,30},{7,31}} | collective-permute-start | bytes 92168 | tf_op jit(solution)/shard_map/while/body/eval_jaxpr/ppermute | solution.py:20
  1517.4 11.0 collective-permute-start.5
  (114 other events, 980.4 us)
Sparse Core Ops, SparseCore 0:
  1534.2 457.9 all-reduce.5
where the time goes:
time: 2040 us; the launch traced here: 2010 us
  starting transfers between devices  617 us (30%)
  waiting for transfers between devices  487 us (24%)
  matrix products  347 us (17%)
  other arithmetic  245 us (12%)
  local copies, waits for them, and re-layouts  210 us (10%)
  loops' own time  67.5 us (3%)
  blocking collectives  23.3 us (1%)
    ppermute x38, starting transfers between devices, from_behind(): return lax.ppermute(shard, axis, pairs)  617 us
    psum x1, waiting for transfers between devices, shards(): lax.psum((grad_accum[0], down_local, grad_accum[2], grad_accum[3]), 'dp')  435 us
    dot_general x8, matrix products, attention_core(): jnp.einsum('hrk,khd->rhd', attn_probs, values, preferred_element_type=jnp...  80.4 us
    reduce_sum x8, other arithmetic, attention_core(): jnp.sum(jnp.exp(scores - row_peak), axis=2, keepdims=True)  74.2 us
    dot_general x8, matrix products, attention_scores(): jnp.einsum('rhd,khd->hrk', queries, keys, preferred_element_type=jnp.floa...  58.8 us
    ppermute x38, waiting for transfers between devices, from_behind(): return lax.ppermute(shard, axis, pairs)  52 us
    convert_element_type x4, other arithmetic, attention_backward(): grad_scores = (attn_probs * (grad_probs - row_inner)).astype(jnp.bfloat16)  48.8 us
    dot_general x4, matrix products, attention_backward(): jnp.einsum('rhd,khd->hrk', grad_heads, values, preferred_element_type=jnp...  47.9 us
  transfers between devices with their start and end apart: 39, of which 11 were waited for; matrix products, arithmetic and copies ran while one was open for 4% of the time, Pallas kernels for 0%

commit v1 on v0

v1 whole, which is shorter than its diff:
```python
from functools import partial

import jax
import jax.numpy as jnp
from jax import lax
from jax.experimental import pallas as pl
from jax.experimental.pallas import tpu as pltpu
from jax.sharding import PartitionSpec as P

H = 12
M = 20
NSEG = 2
MEM_PAD = 16
NORM_EPSILON = 1e-05
MASKED_SCORE = -1000000000.0
ABSENT_SCORE = -3e38
MESH = pl.DeviceIdType.MESH
BF16 = jnp.bfloat16
F32 = jnp.float32

OUT_ATT, OUT_FF, GIN_ATT, GIN_FF = 0, 1, 2, 3
S_X0, S_CTX, S_DQ, S_DKV, S_DATT, S_GLO, S_DFF0 = 4, 5, 6, 7, 8, 9, 10
S_Y1, S_Y2, S_DU, S_GHI, S_DFF1 = 11, 12, 13, 14, 15
KINDS = 16


def dot(a, b, lhs_dim=1, rhs_dim=0):
    return lax.dot_general(
        a, b, (((lhs_dim,), (rhs_dim,)), ((), ())), preferred_element_type=F32
    )


def normalize(summed):
    mean = jnp.mean(summed, axis=-1, keepdims=True)
    centered = summed - mean
    var = jnp.mean(centered * centered, axis=-1, keepdims=True)
    inv = lax.rsqrt(var + NORM_EPSILON)
    return centered * inv, inv


def layers_kernel(
    n, nseg, heads,
    tokens, cotangent, first, down, bias, gain_bias, keep,
    out, gin, sx1, sx2, sr, sg, sd, norm_grad,
    wf, wd, nrm, x0, q, kv, ctx, natt, yatt, nff, yd, gy, g, gp, stats, biasb,
    memin, mgin, dkvs, dkvin, dhb, dctx, acc, accp,
    wl, ws, wr, tok_sem, cot_sem, bias_sem, kvs_sem, kvr_sem, xs_sem, xr_sem,
    ms_sem, mr_sem, gs_sem, gr_sem, hs_sem, hr_sem, ds_sem, dr_sem, as_sem, ar_sem,
    lsem, ssem, rsem,
):
    items = n * nseg
    section = lax.axis_index("section")
    c = lax.rem(section, 2)
    x = lax.div(section, 2)
    core_peer = {"section": x * 2 + (1 - c)}
    chip_peer = {"section": (1 - x) * 2 + c}
    rows, width = x0.shape[1:]
    toks = rows - MEM_PAD
    seg_len = 2 * toks
    hidden_half = wd.shape[1]
    hidden = 2 * hidden_half
    wide = 3 * width
    lanes = 128
    chunk = 512 if hidden_half % 512 == 0 else 256
    per_half = hidden_half // chunk
    ncol = 256

    def remote(src, dst, send, recv, peer):
        return pltpu.make_async_remote_copy(
            src_ref=src, dst_ref=dst, send_sem=send, recv_sem=recv,
            device_id=peer, device_id_type=MESH,
        )

    barrier = pltpu.get_barrier_semaphore()
    pl.semaphore_signal(barrier, inc=1, device_id=core_peer, device_id_type=MESH)
    pl.semaphore_signal(barrier, inc=1, device_id=chip_peer, device_id_type=MESH)
    pl.semaphore_wait(barrier, 2)

    def weight_piece(k):
        if k == 0:
            return first.at[:, width:wide], wf.at[c, :, width:wide]
        if k == 1:
            return first.at[:, 0:width], wf.at[c, :, 0:width]
        if k == 2:
            return first.at[:, wide:], wf.at[c, :, wide:]
        return down, wd.at[c]

    nrm[c] = gain_bias[...]
    nrm_copy = remote(nrm.at[c], nrm.at[c], ws.at[4], wr.at[4], core_peer)
    for k in range(4):
        src, dst = weight_piece(k)
        remote(src, dst, ws.at[k], wr.at[k], core_peer).start()
        pltpu.make_async_copy(src, dst, wl.at[k]).start()
    nrm_copy.start()

    def wait_local(k):
        src, dst = weight_piece(k)
        pltpu.make_async_copy(src, dst, wl.at[k]).wait()

    def wait_remote(k):
        if k == 4:
            nrm_copy.wait_recv()
        else:
            src, dst = weight_piece(k)
            remote(src, dst, ws.at[k], wr.at[k], core_peer).wait_recv()

    def wait_first_of(core, ks):
        @pl.when(c == core)
        def _():
            for k in ks:
                wait_local(k)

        @pl.when(c != core)
        def _():
            for k in ks:
                wait_remote(k)

    def bias_copy(i):
        return pltpu.make_async_copy(bias.at[i], biasb.at[i], bias_sem.at[i])

    def token_rows(ref, i):
        return ref.at[lax.rem(i, n), pl.ds(lax.div(i, n) * seg_len + c * toks, toks), :]

    def token_copy(i):
        return pltpu.make_async_copy(
            token_rows(tokens, i), x0.at[i, 0:toks, :], tok_sem.at[i]
        )

    def cot_copy(i):
        return pltpu.make_async_copy(
            token_rows(cotangent, i), gy.at[i, 0:toks, :], cot_sem.at[i]
        )

    for i in range(items):
        @pl.when(x == 0)
        def _():
            token_copy(i).start()

        bias_copy(i).start()

    for i in range(items):
        @pl.when(x == 1)
        def _():
            cot_copy(i).start()

    def routed(kind, i):
        block = i * 2 + c
        sec = 0
        if kind == OUT_ATT:
            src, dst = yatt.at[i, 0:toks, :], token_rows(out, i)
        elif kind == OUT_FF:
            src, dst, sec = yd.at[i, 0:toks, :], token_rows(out, i), 1
        elif kind == GIN_ATT:
            src, dst = yd.at[i, 0:toks, :], token_rows(gin, i)
        elif kind == GIN_FF:
            src, dst, sec = gy.at[i, 0:toks, :], token_rows(gin, i), 1
        elif kind == S_X0:
            src, dst = x0.at[i], sx1.at[block]
        elif kind == S_CTX:
            src, dst = ctx.at[i], sx2.at[block]
        elif kind == S_DQ:
            src, dst = q.at[i], sr.at[block, :, 0:width]
        elif kind == S_DKV:
            src, dst = kv.at[i, c], sr.at[block, :, width:wide]
        elif kind == S_DATT:
            src, dst = natt.at[i], sr.at[block, :, wide:]
        elif kind == S_GLO:
            src, dst = g.at[i, :, 0:hidden_half], sg.at[block]
        elif kind == S_DFF0:
            src, dst = nff.at[i], sd.at[block]
        elif kind == S_Y1:
            src, dst, sec = yatt.at[i], sx1.at[block], 1
        elif kind == S_Y2:
            src, dst, sec = yatt.at[i], sx2.at[block], 1
        elif kind == S_DU:
            src, dst, sec = gp.at[i], sr.at[block], 1
        elif kind == S_GHI:
            src, dst, sec = g.at[i, :, hidden_half:], sg.at[block], 1
        else:
            src, dst, sec = nff.at[i], sd.at[block], 1
        return src, dst, sec

    def route_local(kind, i):
        src, dst, _ = routed(kind, i)
        return pltpu.make_async_copy(src, dst, lsem.at[kind, i])

    def route_away(kind, i):
        src, dst, _ = routed(kind, i)
        return remote(src, dst, ssem.at[kind, i], rsem.at[kind, i], core_peer)

    def route(kind, i):
        sec = routed(kind, i)[2]

        @pl.when(c == sec)
        def _():
            route_local(kind, i).start()

        @pl.when(c != sec)
        def _():
            route_away(kind, i).start()

    def route_sent(kind, i):
        sec = routed(kind, i)[2]

        @pl.when(c == sec)
        def _():
            route_local(kind, i).wait()

        @pl.when(c != sec)
        def _():
            route_away(kind, i).wait_send()

    def route_received(kind, i):
        @pl.when(c == routed(kind, i)[2])
        def _():
            route_away(kind, i).wait_recv()

    def kv_copy(i):
        return remote(kv.at[i, c], kv.at[i, c], kvs_sem.at[i], kvr_sem.at[i], core_peer)

    def x_copy(i):
        return remote(yd.at[i], x0.at[i], xs_sem.at[i], xr_sem.at[i], chip_peer)

    def mem_copy(i):
        return remote(
            yd.at[i, toks:rows, :], memin.at[i], ms_sem.at[i], mr_sem.at[i], chip_peer
        )

    def gy_copy(i):
        return remote(yd.at[i], gy.at[i], gs_sem.at[i], gr_sem.at[i], chip_peer)

    def mg_copy(i):
        return remote(
            yd.at[i, toks:rows, :], mgin.at[i], hs_sem.at[i], hr_sem.at[i], chip_peer
        )

    def dkv_copy(i, slot):
        return remote(
            dkvs.at[1 - c], dkvin.at[slot], ds_sem.at[i], dr_sem.at[i], core_peer
        )

    lane = lax.broadcasted_iota(jnp.int32, (rows, lanes), 1)
    first_head = lane < lanes // 2
    stat_lane = lax.broadcasted_iota(jnp.int32, (rows, lanes), 1)
    key_first_head = lax.broadcasted_iota(jnp.int32, (2 * rows, lanes), 1) < lanes // 2

    def lane_block(j, base=0):
        return pl.ds(pl.multiple_of(base + j * lanes, lanes), lanes)

    def masked_scores(qm, k2, i):
        s = dot(qm, k2, 1, 1)
        b = biasb[i]
        return jnp.where(b == 0.0, s, b)

    def both_keys(i, cols):
        return jnp.concatenate([kv[i, 0, :, cols], kv[i, 1, :, cols]], axis=0)

    def forward_tick(t, carry):
        i = t - x

        @pl.when((i >= 0) & (i < items))
        def _():
            @pl.when(x == 0)
            def _():
                token_copy(i).wait()

                @pl.when(i < n)
                def _():
                    x0[i, toks:rows, :] = jnp.zeros((MEM_PAD, width), BF16)

                @pl.when(i >= n)
                def _():
                    mem_copy(i - n).wait_recv()
                    x0[i, toks:rows, :] = jnp.where(
                        keep[i][:, 0:1] > 0.0, memin[i - n], jnp.zeros((), BF16)
                    )

            @pl.when(x == 1)
            def _():
                x_copy(i).wait_recv()

            @pl.when(i == 0)
            def _():
                wait_first_of(0, (0,))

            xb = x0[i]
            for col in range(width, wide, ncol):
                kv[i, c, :, col - width : col - width + ncol] = dot(
                    xb, wf[0, :, col : col + ncol]
                ).astype(BF16)
            kv_copy(i).start()
            route(S_X0, i)

            @pl.when(i == 0)
            def _():
                wait_first_of(0, (1,))

            for col in range(0, width, ncol):
                q[i, :, col : col + ncol] = (
                    dot(xb, wf[0, :, col : col + ncol]).astype(BF16) * BF16(0.125)
                )
            bias_copy(i).wait()
            kv_copy(i).wait_recv()
            stats[i] = jnp.zeros((rows, lanes), F32)

            def head_pair(j, carry):
                cols = lane_block(j)
                q2 = q[i, :, cols]
                k2 = both_keys(i, cols)
                v2 = both_keys(i, lane_block(j, width))
                outs = []
                for e in range(2):
                    mine = first_head if e == 0 else ~first_head
                    s = masked_scores(jnp.where(mine, q2, BF16(0)), k2, i)
                    peak = jnp.max(s, axis=1, keepdims=True)
                    p = jnp.exp(s - peak)
                    total = jnp.sum(p, axis=1, keepdims=True)
                    outs.append(dot(p.astype(BF16), v2) * (1.0 / total))
                    lse = peak + jnp.log(total)
                    stats[i] = jnp.where(stat_lane == 2 * j + e, lse, stats[i])
                ctx[i, :, cols] = jnp.where(first_head, outs[0], outs[1]).astype(BF16)
                return carry

            lax.fori_loop(0, heads // 2, head_pair, 0)
            route(S_CTX, i)

            @pl.when(i == 0)
            def _():
                wait_first_of(0, (2,))

                @pl.when(c == 0)
                def _():
                    wait_remote(4)

                @pl.when(c == 1)
                def _():
                    wait_remote(4)

            for col in range(0, width, ncol):
                dhb[:, col : col + ncol] = dot(
                    ctx[i], wf[0, :, wide + col : wide + col + ncol]
                ) + x0[i, :, col : col + ncol].astype(F32)
            normed, inv = normalize(dhb[...])
            natt[i] = normed.astype(BF16)
            stats[i] = jnp.where(stat_lane == heads, inv, stats[i])
            yatt[i] = (normed * nrm[0, 0:1, :] + nrm[0, 1:2, :]).astype(BF16)
            route(OUT_ATT, i)
            route(S_Y1, i)
            route(S_Y2, i)

            @pl.when(i == 0)
            def _():
                wait_first_of(1, (0, 1, 2))

            def up(k, carry):
                cols = pl.ds(pl.multiple_of(k * chunk, chunk), chunk)
                u = dot(yatt[i], wf[1, :, cols])
                cdf = 0.5 + 0.5 * lax.erf(u * 0.7071067811865476)
                pdf = 0.3989422804014327 * jnp.exp(-0.5 * u * u)
                g[i, :, cols] = (u * cdf).astype(BF16)
                gp[i, :, cols] = (cdf + u * pdf).astype(BF16)
                return carry

            lax.fori_loop(0, hidden // chunk, up, 0)
            route(S_GLO, i)
            route(S_GHI, i)

            @pl.when(i == 0)
            def _():
                wait_first_of(0, (3,))
                wait_first_of(1, (3,))

            for col in range(0, width, ncol):
                dhb[:, col : col + ncol] = (
                    dot(g[i, :, 0:hidden_half], wd[0, :, col : col + ncol])
                    + dot(g[i, :, hidden_half:], wd[1, :, col : col + ncol])
                    + yatt[i, :, col : col + ncol].astype(F32)
                )
            normed, inv = normalize(dhb[...])
            nff[i] = normed.astype(BF16)
            stats[i] = jnp.where(stat_lane == heads + 1, inv, stats[i])
            yd[i] = (normed * nrm[1, 0:1, :] + nrm[1, 1:2, :]).astype(BF16)

            @pl.when(x == 0)
            def _():
                x_copy(i).start()

            @pl.when((x == 1) & (i < items - n))
            def _():
                mem_copy(i).start()

            route(OUT_FF, i)

        return carry

    lax.fori_loop(0, items + 1, forward_tick, 0)

    def forward_drain(i, carry):
        kv_copy(i).wait_send()
        route_sent(OUT_FF, i)

        @pl.when(x == 0)
        def _():
            x_copy(i).wait_send()

        @pl.when((x == 1) & (i < items - n))
        def _():
            mem_copy(i).wait_send()

        return carry

    lax.fori_loop(0, items, forward_drain, 0)
    acc[...] = jnp.zeros_like(acc)

    def norm_back(s, i, normed_ref):
        grad = gy[i].astype(F32)
        normed = normed_ref[i].astype(F32)
        inv = jnp.sum(jnp.where(stat_lane == heads + s, stats[i], 0.0), axis=1, keepdims=True)
        acc[s, 0:1, :] += jnp.sum(grad * normed, axis=0, keepdims=True)
        acc[s, 1:2, :] += jnp.sum(grad, axis=0, keepdims=True)
        scaled = grad * nrm[s, 0:1, :]
        row_term = jnp.mean(scaled, axis=1, keepdims=True)
        row_cross = jnp.mean(scaled * normed, axis=1, keepdims=True)
        dh = inv * (scaled - row_term - normed * row_cross)
        dhb[...] = dh
        normed_ref[i] = dh.astype(BF16)

    def backward_tick(t, carry):
        r = t - (1 - x)

        @pl.when((r >= 0) & (r < items))
        def _():
            i = (nseg - 1 - lax.div(r, n)) * n + lax.rem(r, n)
            slot = lax.rem(r, 2)

            @pl.when(x == 1)
            def _():
                cot_copy(i).wait()

                @pl.when(i >= items - n)
                def _():
                    gy[i, toks:rows, :] = jnp.zeros((MEM_PAD, width), BF16)

                @pl.when(i < items - n)
                def _():
                    mg_copy(i + n).wait_recv()
                    gy[i, toks:rows, :] = jnp.where(
                        keep[i + n][:, 0:1] > 0.0, mgin[i + n], jnp.zeros((), BF16)
                    )

            @pl.when(x == 0)
            def _():
                gy_copy(i).wait_recv()

            norm_back(1, i, nff)
            route(S_DFF0, i)
            route(S_DFF1, i)

            def down_back(k, carry):
                cols = pl.ds(pl.multiple_of(k * chunk, chunk), chunk)
                part = pl.ds(pl.multiple_of(lax.rem(k, per_half) * chunk, chunk), chunk)
                dg = dot(nff[i], wd[lax.div(k, per_half), part, :], 1, 1)
                gp[i, :, cols] = (dg * gp[i, :, cols].astype(F32)).astype(BF16)
                return carry

            lax.fori_loop(0, hidden // chunk, down_back, 0)
            route(S_DU, i)
            for col in range(0, width, ncol):
                gy[i, :, col : col + ncol] = (
                    dot(gp[i], wf[1, col : col + ncol, :], 1, 1) + dhb[:, col : col + ncol]
                ).astype(BF16)
            route(GIN_FF, i)

            norm_back(0, i, natt)
            route(S_DATT, i)
            for col in range(0, width, ncol):
                dctx[:, col : col + ncol] = dot(
                    natt[i], wf[0, col : col + ncol, wide:], 1, 1
                ).astype(BF16)

            def head_pair(j, carry):
                cols = lane_block(j)
                q2 = q[i, :, cols]
                k2 = both_keys(i, cols)
                v2 = both_keys(i, lane_block(j, width))
                c2 = dctx[:, cols]
                t2 = c2.astype(F32) * ctx[i, :, cols].astype(F32)
                dq2, dk2, dv2 = 0.0, 0.0, 0.0
                for e in range(2):
                    mine = first_head if e == 0 else ~first_head
                    key_mine = key_first_head if e == 0 else ~key_first_head
                    qm = jnp.where(mine, q2, BF16(0))
                    cm = jnp.where(mine, c2, BF16(0))
                    km = jnp.where(key_mine, k2, BF16(0))
                    lse = jnp.sum(
                        jnp.where(stat_lane == 2 * j + e, stats[i], 0.0), axis=1, keepdims=True
                    )
                    inner = jnp.sum(jnp.where(mine, t2, 0.0), axis=1, keepdims=True)
                    p = jnp.exp(masked_scores(qm, k2, i) - lse)
                    dp = dot(cm, v2, 1, 1)
                    ds = (p * (dp - inner)).astype(BF16)
                    dv2 = dv2 + dot(p.astype(BF16), cm, 0, 0)
                    dk2 = dk2 + dot(ds, qm, 0, 0)
                    dq2 = dq2 + dot(ds, km)
                q[i, :, cols] = (dq2 * 0.125).astype(BF16)
                vcols = lane_block(j, width)
                dkvs[0, :, cols] = dk2[0:rows].astype(BF16)
                dkvs[1, :, cols] = dk2[rows:].astype(BF16)
                dkvs[0, :, vcols] = dv2[0:rows].astype(BF16)
                dkvs[1, :, vcols] = dv2[rows:].astype(BF16)
                return carry

            lax.fori_loop(0, heads // 2, head_pair, 0)
            dkv_copy(i, slot).start()
            route(S_DQ, i)
            for col in range(0, width, ncol):
                dhb[:, col : col + ncol] += dot(q[i], wf[0, col : col + ncol, 0:width], 1, 1)
            dkv_copy(i, slot).wait_recv()
            kv[i, c] = (dkvs[c].astype(F32) + dkvin[slot].astype(F32)).astype(BF16)
            route(S_DKV, i)
            for col in range(0, width, ncol):
                yd[i, :, col : col + ncol] = (
                    dot(kv[i, c], wf[0, col : col + ncol, width:wide], 1, 1)
                    + dhb[:, col : col + ncol]
                ).astype(BF16)

            @pl.when(x == 1)
            def _():
                gy_copy(i).start()

            @pl.when((x == 0) & (i >= n))
            def _():
                mg_copy(i).start()

            route(GIN_ATT, i)
            dkv_copy(i, slot).wait_send()

        return carry

    lax.fori_loop(0, items + 1, backward_tick, 0)

    acc_copy = remote(acc.at[1 - c], accp, as_sem, ar_sem, core_peer)
    acc_copy.start()

    def backward_drain(i, carry):
        @pl.when(x == 1)
        def _():
            gy_copy(i).wait_send()

        @pl.when((x == 0) & (i >= n))
        def _():
            mg_copy(i).wait_send()

        for kind in range(KINDS):
            if kind != OUT_FF:
                route_sent(kind, i)
            route_received(kind, i)
        return carry

    lax.fori_loop(0, items, backward_drain, 0)
    for k in range(4):
        src, dst = weight_piece(k)
        remote(src, dst, ws.at[k], wr.at[k], core_peer).wait_send()
    nrm_copy.wait_send()
    acc_copy.wait()
    norm_grad[...] = acc[c] + accp[...]


def run_layers(n, nseg, heads, tokens, cotangent, first, down, bias, gain_bias, keep):
    length, width = tokens.shape[1:]
    toks = length // nseg // 2
    rows = toks + MEM_PAD
    items = n * nseg
    hidden_half = down.shape[0]
    any_spec = pl.BlockSpec(memory_space=pl.ANY)
    vmem_spec = pl.BlockSpec(memory_space=pltpu.VMEM)
    dma = pltpu.SemaphoreType.DMA
    item_rows = pltpu.VMEM((items, rows, width), BF16)
    return pl.pallas_call(
        partial(layers_kernel, n, nseg, heads),
        out_shape=(
            jax.ShapeDtypeStruct((n, length, width), BF16),
            jax.ShapeDtypeStruct((n, length, width), BF16),
            jax.ShapeDtypeStruct((2 * items, rows, width), BF16),
            jax.ShapeDtypeStruct((2 * items, rows, width), BF16),
            jax.ShapeDtypeStruct((2 * items, rows, 4 * width), BF16),
            jax.ShapeDtypeStruct((2 * items, rows, hidden_half), BF16),
            jax.ShapeDtypeStruct((2 * items, rows, width), BF16),
            jax.ShapeDtypeStruct((2, width), F32),
        ),
        in_specs=[any_spec] * 5 + [vmem_spec] * 2,
        out_specs=[any_spec] * 7 + [vmem_spec],
        scratch_shapes=[
            pltpu.VMEM((2, width, 4 * width), BF16),
            pltpu.VMEM((2, hidden_half, width), BF16),
            pltpu.VMEM((2, 2, width), F32),
            item_rows,
            item_rows,
            pltpu.VMEM((items, 2, rows, 2 * width), BF16),
            item_rows,
            item_rows,
            item_rows,
            item_rows,
            item_rows,
            item_rows,
            pltpu.VMEM((items, rows, 2 * hidden_half), BF16),
            pltpu.VMEM((items, rows, 2 * hidden_half), BF16),
            pltpu.VMEM((items, rows, 128), F32),
            pltpu.VMEM((items, rows, 2 * rows), F32),
            pltpu.VMEM((items, MEM_PAD, width), BF16),
            pltpu.VMEM((items, MEM_PAD, width), BF16),
            pltpu.VMEM((2, rows, 2 * width), BF16),
            pltpu.VMEM((2, rows, 2 * width), BF16),
            pltpu.VMEM((rows, width), F32),
            pltpu.VMEM((rows, width), BF16),
            pltpu.VMEM((2, 2, width), F32),
            pltpu.VMEM((2, width), F32),
            dma((4,)), dma((5,)), dma((5,)),
        ]
        + [dma((items,))] * 15
        + [dma(()), dma(())]
        + [dma((KINDS, items))] * 3,
        compiler_params=pltpu.CompilerParams(
            collective_id=0, has_side_effects=True, vmem_limit_bytes=60 * 1024 * 1024
        ),
    )(tokens, cotangent, first, down, bias, gain_bias, keep)


def shards(
    tokens, doc_ids, reset_flags, first_weights, down_halves, norm_gain, norm_bias, cotangent
):
    c = lax.rem(lax.axis_index("section"), 2)
    n, length, width = tokens.shape
    nseg = NSEG
    seg_len = length // nseg
    toks = seg_len // 2
    items = n * nseg
    mem_half = M // 2
    rows = toks + MEM_PAD

    docs = doc_ids.reshape(n, nseg, 2, toks).transpose(1, 0, 2, 3).reshape(items, 2, toks)
    tail = jnp.where(lax.iota(jnp.int32, MEM_PAD) < mem_half, -1, -2)
    tail = jnp.broadcast_to(tail, (items, 2, MEM_PAD))
    marks = jnp.concatenate([docs, tail], axis=2)
    own = lax.dynamic_index_in_dim(marks, c, 1, keepdims=False)
    keys = marks.reshape(items, 1, 2 * rows)
    own = own[:, :, None]
    allowed = (own == keys) | (keys == -1) | (own < 0)
    bias = jnp.where(keys == -2, ABSENT_SCORE, jnp.where(allowed, 0.0, MASKED_SCORE))
    bias = bias.astype(F32)
    resets = jnp.concatenate([jnp.ones((n, 1), jnp.int32), reset_flags], axis=1)
    keep = (1 - resets).astype(F32).T.reshape(items, 1, 1)
    keep = jnp.broadcast_to(keep, (items, MEM_PAD, 128))
    gain_bias = jnp.concatenate([norm_gain, norm_bias], axis=0)

    out, gin, sx1, sx2, sr, sg, sd, norm_grad = run_layers(
        n, nseg, H, tokens, cotangent, first_weights[0], down_halves[0], bias, gain_bias, keep
    )
    total = 2 * items * rows
    sx1, sx2, sd = (a.reshape(total, width) for a in (sx1, sx2, sd))
    sr = sr.reshape(total, 4 * width)
    sg = sg.reshape(total, -1)

    def weight_grad(left, right):
        return jnp.einsum("rd,re->de", left, right, preferred_element_type=F32).astype(BF16)

    first_grad = jnp.concatenate(
        [weight_grad(sx1, sr[:, : 3 * width]), weight_grad(sx2, sr[:, 3 * width :])], axis=1
    )
    down_grad = weight_grad(sg, sd)
    first_grad, down_grad = lax.psum((first_grad, down_grad), "dp")
    norm_grad = lax.psum(norm_grad, "dp")
    return (
        out[None],
        gin[None],
        first_grad.astype(F32)[None],
        down_grad.astype(F32)[None],
        norm_grad[0:1],
        norm_grad[1:2],
    )


def solution(mesh):
    in_specs = (
        P("dp", None, None),
        P("dp", None),
        P("dp", None),
        P("section", None, None),
        P("section", None, None),
        P("section", None),
        P("section", None),
        P("dp", None, None),
    )
    out_specs = (
        P("section", "dp", None, None),
        P("section", "dp", None, None),
        P("section", None, None),
        P("section", None, None),
        P("section", None),
        P("section", None),
    )
    return jax.shard_map(shards, mesh=mesh, in_specs=in_specs, out_specs=out_specs, check_vma=False)
```

time: 2040 us -> 537 us (0.26); the launches traced: 2010 us -> 537 us
  starting transfers between devices: 617 us -> 0.04 us
  matrix products: 347 us -> 25.6 us
  waiting for transfers between devices: 487 us -> 211 us
  Pallas kernels: 0 us -> 239 us
  other arithmetic: 245 us -> 16.9 us
  local copies, waits for them, and re-layouts: 210 us -> 7.12 us
  loops' own time: 67.5 us -> 0 us
    ppermute x38 -> x0, starting transfers between devices: 617 us -> none  [from_behind(): return lax.ppermute(shard, axis, pairs)]
    dot_general x64 -> x3, matrix products: 347 us -> 25.6 us  [weight_grad(): jnp.einsum('rd,re->de', left, right, preferred_element_type=F32)]
    pallas_call x0 -> x1, Pallas kernels: none -> 239 us  [run_layers(): pl.pallas_call(partial(layers_kernel, n, nseg, heads), out_shape=(jax.Sha...]
    psum x1, waiting for transfers between devices: 435 us -> 211 us  [shards(): first_grad, down_grad = lax.psum((first_grad, down_grad), 'dp')]
    reduce_sum x20 -> x0, other arithmetic: 85.7 us -> none  [the longest x8 74.2 us: attention_core(): jnp.sum(jnp.exp(scores - row_peak), axis=2, keepdims=True)]
    another operation x20 -> x0, loops' own time: 67.5 us -> none  [the longest x9 47.3 us: backward_tick(): lax.switch(jnp.where(active, section_kind, 0), [backward_spare, backward_...]
    slice x60 -> x1, local copies, waits for them, and re-layouts: 60.3 us -> 0.59 us  [shards(): norm_grad[1:2]]
    convert_element_type x8 -> x0, other arithmetic: 53.7 us -> none  [the longest x4 48.8 us: attention_backward(): grad_scores = (attn_probs * (grad_probs - row_inner)).astype(jnp.bfloat16)]
  transfers between devices with their start and end apart: 39 -> 1, of which waited for: 11 -> 1; matrix products, arithmetic and copies ran while one was open for 4% -> 0% of each run, Pallas kernels for 0% -> 0%
where the time goes in v1:
time: 537 us
  Pallas kernels  239 us (45%)
  waiting for transfers between devices  211 us (39%)
  matrix products  25.6 us (5%)
  blocking collectives  22.8 us (4%)
  other arithmetic  16.9 us (3%)
  between operations  14.2 us (3%)
  local copies, waits for them, and re-layouts  7.12 us (1%)
    pallas_call x1, Pallas kernels, run_layers(): pl.pallas_call(partial(layers_kernel, n, nseg, heads), out_shape=(jax.Sha...  239 us
    psum x1, waiting for transfers between devices, shards(): first_grad, down_grad = lax.psum((first_grad, down_grad), 'dp')  211 us
    dot_general x3, matrix products, weight_grad(): jnp.einsum('rd,re->de', left, right, preferred_element_type=F32)  25.6 us
    psum x1, blocking collectives, shards(): norm_grad = lax.psum(norm_grad, 'dp')  22.8 us
  transfers between devices with their start and end apart: 1, of which 1 were waited for; matrix products, arithmetic and copies ran while one was open for 0% of the time, Pallas kernels for 0%

profile of v1, /device:TPU:0, one launch (start us, length us, event | category | flops | bytes accessed | tf_op | source)
XLA Modules:
  0.0 536.7 jit_solution(3221909988281906726)
XLA Ops:
  7.2 0.0 all-reduce.4.cloned.1.call-start
  7.2 0.7 reshape.58
  8.0 0.1 reshape.60
  8.1 0.7 convert_bitcast_fusion
  8.8 0.1 broadcast_in_dim.64
  8.9 1.3 pad_maximum_fusion.gain_bias
  10.2 1.9 select_select_fusion.bias
  12.1 0.7 broadcast_in_dim.65.keep
  12.8 239.2 %shard_map.127 = (bf16[2,1024,768]{2,1,0:T(8,128)(2,1)}, bf16[2,1024,768]{2,1,0:T(8,128)(2,1)}, bf16[8,272,768]{2,1,0:T(8,128)(2,1)}, bf16[8,272,768]{2,1,0:T(8,...) custom-call(bf16[2,1024,768]{2,1,0:T(8,128)(2,1)} %tokens.1, ...), custom_call_target="tpu_custom_call" | custom-call | tf_op jit(solution)/shard_map/pallas_call | solution.py:579
  252.1 13.4 %fusion.2 = bf16[768,2304]{1,0:T(8,128)(2,1)S(1)} fusion(bf16[2176,768]{1,0:T(8,128)(2,1)} %bitcast.38, bf16[2176,3072]{1,0:T(8,128)(2,1)} %bitcast.35), kind=kOutput, calls=%fused_computation.2 | convolution fusion | flops 7702511616 | bytes 16908288 | tf_op jit(solution)/shard_map/rd,re->de/dot_general | solution.py:665
  265.5 5.1 fusion.8
  270.7 7.1 %fusion.7 = bf16[1,1536,768]{2,1,0:T(8,128)(2,1)} fusion(bf16[8,272,1536]{2,1,0:T(8,128)(2,1)S(1)} %copy-done.4, bf16[8,272,768]{2,1,0:T(8,128)(2,1)S(1)} %copy-done.5), kind=kOutput, calls=%fused_computation.7 | convolution fusion | flops 5135007744 | bytes 12386304 | tf_op jit(solution)/shard_map/rd,re->de/dot_general | solution.py:665
  277.7 2.8 maximum_bitcast_fusion
  280.5 0.0 all-reduce.4.cloned.1.call-update
  280.6 0.7 copy-done.3
  281.2 22.8 %psum.23 = f32[2,768]{1,0:T(2,128)S(1)} all-reduce(f32[2,768]{1,0:T(2,128)S(1)} %copy-done.3), channel_id=1, replica_groups=mesh['section'=4,'dp'=8] {'dp'}, use_global_device_ids=true, to_apply=%region_2.3 | all-reduce | flops 1536 | bytes 12288 | tf_op jit(solution)/shard_map/psum | solution.py:672
  304.0 0.6 fusion.11
  304.6 210.9 %all-reduce.4.cloned.1.call-done = (bf16[1,768,3072]{2,1,0:T(8,128)(2,1)}, bf16[1,1536,768]{2,1,0:T(8,128)(2,1)}) async-done(((bf16[1,768,3072]{2,1,0:T(8,128)(2,1)}, bf16[1,1536,768]{2,1,0:T(8,128)(2,1)}), (bf16[1,768,3072]{2,1,0:T(8,128)(2,1)}, bf16[1,1536,768]{2,1,0:T(8,128)(2,1)})) %all-reduce.4.cloned.1.call-update) | async-done | bytes 7077904 | tf_op jit(solution)/shard_map/psum | solution.py:671
  515.5 7.5 %broadcast_in_dim.69 = f32[1,768,3072]{2,1,0:T(8,128)} convert(bf16[1,768,3072]{2,1,0:T(8,128)(2,1)} %get-tuple-element.22) | non-fusion elementwise | flops 2359296 | bytes 14155776 | tf_op jit(solution)/shard_map/broadcast_in_dim | solution.py:676
  523.0 2.6 broadcast_in_dim.71
  525.6 0.7 copy-done.1
  526.3 1.7 copy.28
  528.0 0.2 copy-done
  528.2 1.7 copy.29
  (19 shorter events, 0.1 us)
Async XLA Ops:
  7.2 508.3 %all-reduce.4.cloned.1.call-start = ((), (), s32[]{:S(2)}) async-start(), calls=%async_computation | async-start | bytes 14155776 | tf_op jit(solution)/shard_map/psum | solution.py:671
  252.0 13.5 %copy-start.6 = (bf16[8,272,768]{2,1,0:T(8,128)(2,1)S(1)}, bf16[8,272,768]{2,1,0:T(8,128)(2,1)}, u32[]{:S(2)}) copy-start(bf16[8,272,768]{2,1,0:T(8,128)(2,1)} %get-tuple-element.18) | copy-start | bytes 10027012
  252.0 18.6 %copy-start.5 = (bf16[8,272,768]{2,1,0:T(8,128)(2,1)S(1)}, bf16[8,272,768]{2,1,0:T(8,128)(2,1)}, u32[]{:S(2)}) copy-start(bf16[8,272,768]{2,1,0:T(8,128)(2,1)} %get-tuple-element.20) | copy-start | bytes 10027012
  265.5 5.2 copy-start.4
  280.5 0.7 copy-start.3
  515.5 7.5 %copy-start.2 = (bf16[1,1536,768]{2,1,0:T(8,128)(2,1)S(1)}, bf16[1,1536,768]{2,1,0:T(8,128)(2,1)}, u32[]{:S(2)}) copy-start(bf16[1,1536,768]{2,1,0:T(8,128)(2,1)} %get-tuple-element.23) | copy-start | bytes 7077892
  523.0 3.3 copy-start.1
  525.6 2.6 copy-start
Sparse Core Ops, SparseCore 0:
  280.7 234.7 all-reduce.3

commit v2 on v1

--- a/solution.py
+++ b/solution.py
@@ -626,6 +626,404 @@
     )(tokens, cotangent, first, down, bias, gain_bias, keep)
 
 
+def reduce_kernel(
+    chunks,
+    sx1, sx2, sr, sg, sd, norm_part,
+    first_out, down_out, norm_out,
+    x1, x2, rr, gg, dd, work, done, got_u, got_uz, got_vz, got_vy, stage, norms,
+    in_sem, out_sem, u_s, u_r, uz_s, uz_r, vz_s, vz_r, vy_s, vy_r, vg_s, vg_r,
+    uzg_s, uzg_r, vzg_s, vzg_r, ug_s, ug_r, n_s, n_r,
+):
+    lines = 4
+    d = lax.axis_index("dp")
+    y = lax.rem(d, 2)
+    z = lax.div(d, 2)
+    dp = lax.axis_size("dp")
+    width = sd.shape[1]
+    half = width // 2
+    part = width // chunks
+    hr = part // 2
+    lane_group = 128
+    per_group = lane_group // part
+    y_peer = {"dp": z * 2 + (1 - y)}
+
+    def remote(src, dst, send, recv, peer):
+        return pltpu.make_async_remote_copy(
+            src_ref=src, dst_ref=dst, send_sem=send, recv_sem=recv,
+            device_id=peer, device_id_type=MESH,
+        )
+
+    def other(step):
+        return {"dp": lax.rem(d + step, dp)}
+
+    barrier = pltpu.get_barrier_semaphore()
+    for step in range(1, dp):
+        pl.semaphore_signal(barrier, inc=1, device_id=other(step), device_id_type=MESH)
+
+    loads = [
+        (sd, dd),
+        (sg.at[:, 0:width], gg.at[:, 0:width]),
+        (sg.at[:, width:], gg.at[:, width:]),
+        (sx2, x2),
+        (sr.at[:, 3 * width :], rr.at[:, 3 * width :]),
+        (sx1, x1),
+        (sr.at[:, 0 : 3 * width], rr.at[:, 0 : 3 * width]),
+    ]
+    for k, (src, dst) in enumerate(loads):
+        pltpu.make_async_copy(src, dst, in_sem.at[k]).start()
+
+    norms[d] = norm_part[...]
+    pl.semaphore_wait(barrier, dp - 1)
+
+    def norm_copy(step):
+        return remote(norms.at[d], norms.at[d], n_s.at[step - 1], n_r.at[step - 1], other(step))
+
+    def norm_arrival(step):
+        source = lax.rem(d + dp - step, dp)
+        return remote(
+            norms.at[source], norms.at[source], n_s.at[step - 1], n_r.at[step - 1], other(step)
+        )
+
+    for step in range(1, dp):
+        norm_copy(step).start()
+
+    def column_half(h):
+        return pl.ds(pl.multiple_of(h * half, 128), half)
+
+    mine, theirs = column_half(y), column_half(1 - y)
+
+    def place(flow):
+        return z if flow == 0 else lines - 1 - z
+
+    def onward(flow):
+        step = -1 if flow == 0 else 1
+        return {"dp": (z + step) * 2 + y}
+
+    def back(flow):
+        step = 1 if flow == 0 else -1
+        return {"dp": (z + step) * 2 + y}
+
+    def rows_of(flow):
+        return slice(flow * hr, (flow + 1) * hr)
+
+    def u_copy(k):
+        return remote(
+            work.at[k, 0:3, :, theirs], got_u.at[k], u_s.at[k], u_r.at[k], y_peer
+        )
+
+    def uz_copy(flow, k):
+        return remote(
+            work.at[k, 0:3, rows_of(flow), mine], got_uz.at[flow, k],
+            uz_s.at[flow, k], uz_r.at[flow, k], onward(flow),
+        )
+
+    def vz_copy(flow, k):
+        return remote(
+            work.at[k, 3:6, rows_of(flow), :], got_vz.at[flow, k],
+            vz_s.at[flow, k], vz_r.at[flow, k], onward(flow),
+        )
+
+    def vy_copy(flow, k):
+        return remote(
+            work.at[k, 3:6, rows_of(flow), theirs], got_vy.at[k], vy_s.at[k], vy_r.at[k], y_peer
+        )
+
+    def vg_copy(flow, k, cols):
+        spot = done.at[k, 3:6, rows_of(flow), cols]
+        return remote(spot, spot, vg_s.at[k], vg_r.at[k], y_peer)
+
+    def uzg_copy(flow, k):
+        spot = done.at[k, 0:3, rows_of(flow), mine]
+        return remote(spot, spot, uzg_s.at[flow, k], uzg_r.at[flow, k], back(flow))
+
+    def vzg_copy(flow, k):
+        spot = done.at[k, 3:6, rows_of(flow), :]
+        return remote(spot, spot, vzg_s.at[flow, k], vzg_r.at[flow, k], back(flow))
+
+    def ug_copy(flow, k, cols):
+        spot = done.at[k, 0:3, rows_of(flow), cols]
+        return remote(spot, spot, ug_s.at[flow, k], ug_r.at[flow, k], y_peer)
+
+    def out_copies(k, slot):
+        rows = pl.ds(pl.multiple_of(k * part, part), part)
+        copies = []
+        for b in range(6):
+            if b < 4:
+                dst = first_out.at[rows, b * width : (b + 1) * width]
+            else:
+                low = pl.ds(pl.multiple_of((b - 4) * width + k * part, part), part)
+                dst = down_out.at[low, :]
+            copies.append(
+                pltpu.make_async_copy(stage.at[slot, b], dst, out_sem.at[slot, b])
+            )
+        return copies
+
+    def plus(a, b):
+        return (a.astype(F32) + b.astype(F32)).astype(BF16)
+
+    def wait_load(k):
+        src, dst = loads[k]
+        pltpu.make_async_copy(src, dst, in_sem.at[k]).wait()
+
+    def ready(k, low=0):
+        return (k >= low) & (k < chunks)
+
+    def store_chunks(group, block, value):
+        for e in range(per_group):
+            work[group * per_group + e, block] = value[e * part : (e + 1) * part]
+
+    def round_step(r, carry):
+        group = lax.div(r, per_group)
+
+        @pl.when((lax.rem(r, per_group) == 0) & (r < chunks))
+        def _():
+            cols = pl.ds(pl.multiple_of(group * lane_group, lane_group), lane_group)
+            gcols = pl.ds(pl.multiple_of(width + group * lane_group, lane_group), lane_group)
+
+            @pl.when(r == 0)
+            def _():
+                wait_load(0)
+                wait_load(1)
+
+            store_chunks(group, 4, dot(gg[:, cols], dd[...], 0, 0).astype(BF16))
+
+            @pl.when(r == 0)
+            def _():
+                wait_load(2)
+
+            store_chunks(group, 5, dot(gg[:, gcols], dd[...], 0, 0).astype(BF16))
+
+            @pl.when(r == 0)
+            def _():
+                wait_load(3)
+                wait_load(4)
+
+            store_chunks(group, 3, dot(x2[:, cols], rr[:, 3 * width :], 0, 0).astype(BF16))
+
+            @pl.when(r == 0)
+            def _():
+                wait_load(5)
+                wait_load(6)
+
+            for b in range(3):
+                store_chunks(
+                    group, b,
+                    dot(x1[:, cols], rr[:, b * width : (b + 1) * width], 0, 0).astype(BF16),
+                )
+
+        @pl.when(ready(r))
+        def _():
+            u_copy(r).start()
+
+        for flow in range(2):
+            p = place(flow)
+            k = r - (lines - 1 - p)
+            rows = rows_of(flow)
+
+            @pl.when(ready(k))
+            def _():
+                @pl.when(p < lines - 1)
+                def _():
+                    vz_copy(flow, k).wait_recv()
+                    work[k, 3:6, rows, :] = plus(work[k, 3:6, rows, :], got_vz[flow, k])
+
+                @pl.when(p > 0)
+                def _():
+                    vz_copy(flow, k).start()
+
+                @pl.when(p == 0)
+                def _():
+                    vy_copy(flow, k).start()
+
+        @pl.when(ready(r - 1))
+        def _():
+            k = r - 1
+            u_copy(k).wait_recv()
+            work[k, 0:3, :, mine] = plus(work[k, 0:3, :, mine], got_u[k])
+
+        for flow in range(2):
+            p = place(flow)
+            k = r - 1 - (lines - 1 - p)
+            rows = rows_of(flow)
+
+            @pl.when(ready(k))
+            def _():
+                @pl.when(p < lines - 1)
+                def _():
+                    uz_copy(flow, k).wait_recv()
+                    total = plus(work[k, 0:3, rows, mine], got_uz[flow, k])
+
+                    @pl.when(p > 0)
+                    def _():
+                        work[k, 0:3, rows, mine] = total
+
+                    @pl.when(p == 0)
+                    def _():
+                        done[k, 0:3, rows, mine] = total
+
+                @pl.when(p > 0)
+                def _():
+                    uz_copy(flow, k).start()
+
+                @pl.when(p == 0)
+                def _():
+                    uzg_copy(flow, k).start()
+                    ug_copy(flow, k, mine).start()
+
+        for flow in range(2):
+            p = place(flow)
+            rows = rows_of(flow)
+
+            @pl.when((p == 0) & ready(r - lines))
+            def _():
+                k = r - lines
+                vy_copy(flow, k).wait_recv()
+                done[k, 3:6, rows, mine] = plus(work[k, 3:6, rows, mine], got_vy[k])
+                vg_copy(flow, k, mine).start()
+
+            @pl.when((p == 0) & ready(r - lines - 1))
+            def _():
+                k = r - lines - 1
+                vg_copy(flow, k, theirs).wait_recv()
+                vzg_copy(flow, k).start()
+
+        for flow in range(2):
+            p = place(flow)
+            k = r - lines - p
+
+            @pl.when((p > 0) & ready(k))
+            def _():
+                uzg_copy(flow, k).wait_recv()
+
+                @pl.when(p < lines - 1)
+                def _():
+                    uzg_copy(flow, k).start()
+
+                ug_copy(flow, k, mine).start()
+
+        for flow in range(2):
+            p = place(flow)
+            k = r - lines - 1 - p
+
+            @pl.when((p > 0) & ready(k))
+            def _():
+                vzg_copy(flow, k).wait_recv()
+
+                @pl.when(p < lines - 1)
+                def _():
+                    vzg_copy(flow, k).start()
+
+            @pl.when(ready(k))
+            def _():
+                ug_copy(flow, k, theirs).wait_recv()
+
+        k = r - 2 * lines
+
+        @pl.when(ready(k))
+        def _():
+            slot = lax.rem(k, 2)
+
+            @pl.when(k >= 2)
+            def _():
+                for copy in out_copies(k - 2, slot):
+                    copy.wait()
+
+            stage[slot] = done[k].astype(F32)
+            for copy in out_copies(k, slot):
+                copy.start()
+
+        return carry
+
+    lax.fori_loop(0, chunks + 2 * lines, round_step, 0)
+
+    for step in range(1, dp):
+        norm_arrival(step).wait_recv()
+    total = norms[0]
+    for e in range(1, dp):
+        total = total + norms[e]
+    norm_out[...] = total
+
+    def drain(k, carry):
+        u_copy(k).wait_send()
+        for flow in range(2):
+            p = place(flow)
+            ug_copy(flow, k, mine).wait_send()
+
+            @pl.when(p > 0)
+            def _():
+                vz_copy(flow, k).wait_send()
+                uz_copy(flow, k).wait_send()
+
+            @pl.when(p < lines - 1)
+            def _():
+                uzg_copy(flow, k).wait_send()
+                vzg_copy(flow, k).wait_send()
+
+            @pl.when(p == 0)
+            def _():
+                vy_copy(flow, k).wait_send()
+                vg_copy(flow, k, mine).wait_send()
+
+        return carry
+
+    lax.fori_loop(0, chunks, drain, 0)
+    for k in (chunks - 2, chunks - 1):
+        for copy in out_copies(k, k % 2):
+            copy.wait()
+    for step in range(1, dp):
+        norm_copy(step).wait_send()
+
+
+def sum_weights(dp, sx1, sx2, sr, sg, sd, norm_part):
+    total, width = sx1.shape
+    chunks = 12
+    part = width // chunks
+    half = width // 2
+    any_spec = pl.BlockSpec(memory_space=pl.ANY)
+    vmem_spec = pl.BlockSpec(memory_space=pltpu.VMEM)
+    dma = pltpu.SemaphoreType.DMA
+    one, two = dma((chunks,)), dma((2, chunks))
+    return pl.pallas_call(
+        partial(reduce_kernel, chunks),
+        out_shape=(
+            jax.ShapeDtypeStruct((width, 4 * width), F32),
+            jax.ShapeDtypeStruct((2 * width, width), F32),
+            jax.ShapeDtypeStruct((2, width), F32),
+        ),
+        in_specs=[any_spec] * 5 + [vmem_spec],
+        out_specs=[any_spec] * 2 + [vmem_spec],
+        scratch_shapes=[
+            pltpu.VMEM((total, width), BF16),
+            pltpu.VMEM((total, width), BF16),
+            pltpu.VMEM((total, 4 * width), BF16),
+            pltpu.VMEM((total, 2 * width), BF16),
+            pltpu.VMEM((total, width), BF16),
+            pltpu.VMEM((chunks, 6, part, width), BF16),
+            pltpu.VMEM((chunks, 6, part, width), BF16),
+            pltpu.VMEM((chunks, 3, part, half), BF16),
+            pltpu.VMEM((2, chunks, 3, part // 2, half), BF16),
+            pltpu.VMEM((2, chunks, 3, part // 2, width), BF16),
+            pltpu.VMEM((chunks, 3, part // 2, half), BF16),
+            pltpu.VMEM((2, 6, part, width), F32),
+            pltpu.VMEM((dp, 2, width), F32),
+            dma((7,)),
+            dma((2, 6)),
+            one, one,
+            two, two,
+            two, two,
+            one, one,
+            one, one,
+            two, two,
+            two, two,
+            two, two,
+            dma((dp - 1,)), dma((dp - 1,)),
+        ],
+        compiler_params=pltpu.CompilerParams(
+            collective_id=1, has_side_effects=True, vmem_limit_bytes=60 * 1024 * 1024
+        ),
+    )(sx1, sx2, sr, sg, sd, norm_part)
+
+
 def shards(
     tokens, doc_ids, reset_flags, first_weights, down_halves, norm_gain, norm_bias, cotangent
 ):
@@ -661,15 +1059,20 @@
     sr = sr.reshape(total, 4 * width)
     sg = sg.reshape(total, -1)
 
-    def weight_grad(left, right):
-        return jnp.einsum("rd,re->de", left, right, preferred_element_type=F32).astype(BF16)
-
-    first_grad = jnp.concatenate(
-        [weight_grad(sx1, sr[:, : 3 * width]), weight_grad(sx2, sr[:, 3 * width :])], axis=1
-    )
-    down_grad = weight_grad(sg, sd)
-    first_grad, down_grad = lax.psum((first_grad, down_grad), "dp")
-    norm_grad = lax.psum(norm_grad, "dp")
+    dp = lax.axis_size("dp")
+    if dp == 8:
+        first_grad, down_grad, norm_grad = sum_weights(dp, sx1, sx2, sr, sg, sd, norm_grad)
+    else:
+
+        def weight_grad(left, right):
+            return jnp.einsum("rd,re->de", left, right, preferred_element_type=F32).astype(BF16)
+
+        first_grad = jnp.concatenate(
+            [weight_grad(sx1, sr[:, : 3 * width]), weight_grad(sx2, sr[:, 3 * width :])], axis=1
+        )
+        down_grad = weight_grad(sg, sd)
+        first_grad, down_grad = lax.psum((first_grad, down_grad), "dp")
+        norm_grad = lax.psum(norm_grad, "dp")
     return (
         out[None],
         gin[None],

time: 537 us -> 410 us (0.76)
  waiting for transfers between devices: 211 us -> 0 us
  Pallas kernels: 239 us -> 389 us
  matrix products: 25.6 us -> 0 us
  blocking collectives: 22.8 us -> 0 us
  between operations: 14.2 us -> 0.72 us
  other arithmetic: 16.9 us -> 3.94 us
  local copies, waits for them, and re-layouts: 7.12 us -> 15.8 us
    psum x1 -> x0, waiting for transfers between devices: 211 us -> none  [shards(): first_grad, down_grad = lax.psum((first_grad, down_grad), 'dp')]
    pallas_call x0 -> x1, Pallas kernels: none -> 150 us  [sum_weights(): pl.pallas_call(partial(reduce_kernel, chunks), out_shape=(jax.ShapeDtypeS...]
    dot_general x3 -> x0, matrix products: 25.6 us -> none  [weight_grad(): jnp.einsum('rd,re->de', left, right, preferred_element_type=F32)]
    psum x1 -> x0, blocking collectives: 22.8 us -> none  [shards(): norm_grad = lax.psum(norm_grad, 'dp')]
    broadcast_in_dim x3 -> x0, other arithmetic: 13 us -> none  [the longest x2 10.4 us: shards(): first_grad.astype(F32)[None]]
    unnamed x17 -> x13, local copies, waits for them, and re-layouts: 4.93 us -> 12.8 us
  transfers between devices with their start and end apart: 1 -> 0, of which waited for: 1 -> 0; matrix products, arithmetic and copies ran while one was open for 0% -> 0% of each run, Pallas kernels for 0% -> 0%
where the time goes in v2:
time: 410 us
  Pallas kernels  389 us (95%)
  local copies, waits for them, and re-layouts  15.8 us (4%)
    pallas_call x1, Pallas kernels, run_layers(): pl.pallas_call(partial(layers_kernel, n, nseg, heads), out_shape=(jax.Sha...  239 us
    pallas_call x1, Pallas kernels, sum_weights(): pl.pallas_call(partial(reduce_kernel, chunks), out_shape=(jax.ShapeDtypeS...  150 us
    unnamed x13, local copies, waits for them, and re-layouts  12.8 us

profile of v2, /device:TPU:0, one launch (start us, length us, event | category | flops | bytes accessed | tf_op | source)
XLA Modules:
  0.0 409.9 jit_solution(2375836677564310461)
XLA Ops:
  0.7 0.7 convert_bitcast_fusion
  1.3 0.1 broadcast_in_dim.58
  1.4 1.3 pad_maximum_fusion.gain_bias
  2.7 0.7 reshape.62
  3.5 0.1 reshape.64
  3.6 0.7 broadcast_in_dim.59.keep
  4.3 1.9 select_select_fusion.bias
  6.2 239.2 %shard_map.127 = (bf16[2,1024,768]{2,1,0:T(8,128)(2,1)}, bf16[2,1024,768]{2,1,0:T(8,128)(2,1)}, bf16[8,272,768]{2,1,0:T(8,128)(2,1)}, bf16[8,272,768]{2,1,0:T(8,...) custom-call(bf16[2,1024,768]{2,1,0:T(8,128)(2,1)} %tokens.1, ...), custom_call_target="tpu_custom_call" | custom-call | tf_op jit(solution)/shard_map/pallas_call | solution.py:579
  245.4 0.0 copy-start.1
  245.4 150.2 %shard_map.128 = (f32[768,3072]{1,0:T(8,128)}, f32[1536,768]{1,0:T(8,128)}, f32[2,768]{1,0:T(2,128)}) custom-call(bf16[2176,768]{1,0:T(8,128)(2,1)} %bitcast.28, bf16[2176,768]{1,0:T(8,128)(2,1)} %bitcast.29, bf16[2176,3072]{1,0:T(8,128)(2,1)} %bitcast.21, bf16[2176,1536]{1,0:T(8,128)(2,1)} %bitcast.23, bf16[2176,768]{1,0:T(8,128)(2,1)} %bitcast.30, ...), custom_call_target="tpu_custom_call" | custom-call | tf_op jit(solution)/shard_map/pallas_call | solution.py:986
  395.7 1.4 fusion
  397.0 0.0 copy-start
  397.0 3.9 copy.25
  401.0 0.0 copy-done.1
  401.0 0.0 slice-start
  401.0 1.7 copy.26
  402.6 1.3 copy-done
  403.9 0.0 slice-start.1
  403.9 3.7 copy.27
  407.7 0.0 slice-done
  407.7 0.0 slice-done.1
  407.7 2.2 copy.28
  (9 shorter events, 0.1 us)
Async XLA Ops:
  245.4 155.5 %copy-start.1 = (bf16[2,1024,768]{2,1,0:T(8,128)(2,1)S(1)}, bf16[2,1024,768]{2,1,0:T(8,128)(2,1)}, u32[]{:S(2)}) copy-start(bf16[2,1024,768]{2,1,0:T(8,128)(2,1)} %get-tuple-element.18) | copy-start | bytes 9437188
  397.0 6.9 %copy-start = (f32[768,3072]{1,0:T(8,128)S(1)}, f32[768,3072]{1,0:T(8,128)}, u32[]{:S(2)}) copy-start(f32[768,3072]{1,0:T(8,128)} %get-tuple-element.25) | copy-start | bytes 28311556
  401.0 6.7 %slice-start = ((s8[4718592]{0:T(1024)(128)(4,1)}), s8[4194304]{0:T(1024)(128)(4,1)S(1)}, s32[]{:S(2)}) async-start(s8[4718592]{0:T(1024)(128)(4,1)} %bitcast.25), calls=%async_computation | async-start | bytes 8388608
  403.9 3.7 slice-start.1

commit v3 on v2

--- a/solution.py
+++ b/solution.py
@@ -38,13 +38,25 @@
     return centered * inv, inv
 
 
+def group_of(shape, dim, size):
+    index = lax.broadcasted_iota(jnp.int32, shape, dim)
+    return lax.shift_right_logical(index, size.bit_length() - 1)
+
+
+def spread(values, groups):
+    result = values[-1]
+    for h in range(len(values) - 1):
+        result = jnp.where(groups == h, values[h], result)
+    return result
+
+
 def layers_kernel(
     n, nseg, heads,
-    tokens, cotangent, first, down, bias, gain_bias, keep,
+    tokens, cotangent, first, down, docs, resets, gain, shift,
     out, gin, sx1, sx2, sr, sg, sd, norm_grad,
-    wf, wd, nrm, x0, q, kv, ctx, natt, yatt, nff, yd, gy, g, gp, stats, biasb,
+    wf, wd, nrm, x0, q, kv, ctx, natt, yatt, nff, yd, gy, g, gp, stats, qdoc, kdoc, keep,
     memin, mgin, dkvs, dkvin, dhb, dctx, acc, accp,
-    wl, ws, wr, tok_sem, cot_sem, bias_sem, kvs_sem, kvr_sem, xs_sem, xr_sem,
+    wl, ws, wr, tok_sem, cot_sem, kvs_sem, kvr_sem, xs_sem, xr_sem,
     ms_sem, mr_sem, gs_sem, gr_sem, hs_sem, hr_sem, ds_sem, dr_sem, as_sem, ar_sem,
     lsem, ssem, rsem,
 ):
@@ -58,12 +70,12 @@
     toks = rows - MEM_PAD
     seg_len = 2 * toks
     hidden_half = wd.shape[1]
-    hidden = 2 * hidden_half
     wide = 3 * width
-    lanes = 128
-    chunk = 512 if hidden_half % 512 == 0 else 256
-    per_half = hidden_half // chunk
-    ncol = 256
+    head_dim = width // heads
+    quad = 4 * head_dim
+    quads = heads // 4
+    mem_keys = 2 * MEM_PAD
+    scale = head_dim ** (-0.5)
 
     def remote(src, dst, send, recv, peer):
         return pltpu.make_async_remote_copy(
@@ -74,49 +86,6 @@
     barrier = pltpu.get_barrier_semaphore()
     pl.semaphore_signal(barrier, inc=1, device_id=core_peer, device_id_type=MESH)
     pl.semaphore_signal(barrier, inc=1, device_id=chip_peer, device_id_type=MESH)
-    pl.semaphore_wait(barrier, 2)
-
-    def weight_piece(k):
-        if k == 0:
-            return first.at[:, width:wide], wf.at[c, :, width:wide]
-        if k == 1:
-            return first.at[:, 0:width], wf.at[c, :, 0:width]
-        if k == 2:
-            return first.at[:, wide:], wf.at[c, :, wide:]
-        return down, wd.at[c]
-
-    nrm[c] = gain_bias[...]
-    nrm_copy = remote(nrm.at[c], nrm.at[c], ws.at[4], wr.at[4], core_peer)
-    for k in range(4):
-        src, dst = weight_piece(k)
-        remote(src, dst, ws.at[k], wr.at[k], core_peer).start()
-        pltpu.make_async_copy(src, dst, wl.at[k]).start()
-    nrm_copy.start()
-
-    def wait_local(k):
-        src, dst = weight_piece(k)
-        pltpu.make_async_copy(src, dst, wl.at[k]).wait()
-
-    def wait_remote(k):
-        if k == 4:
-            nrm_copy.wait_recv()
-        else:
-            src, dst = weight_piece(k)
-            remote(src, dst, ws.at[k], wr.at[k], core_peer).wait_recv()
-
-    def wait_first_of(core, ks):
-        @pl.when(c == core)
-        def _():
-            for k in ks:
-                wait_local(k)
-
-        @pl.when(c != core)
-        def _():
-            for k in ks:
-                wait_remote(k)
-
-    def bias_copy(i):
-        return pltpu.make_async_copy(bias.at[i], biasb.at[i], bias_sem.at[i])
 
     def token_rows(ref, i):
         return ref.at[lax.rem(i, n), pl.ds(lax.div(i, n) * seg_len + c * toks, toks), :]
@@ -131,17 +100,69 @@
             token_rows(cotangent, i), gy.at[i, 0:toks, :], cot_sem.at[i]
         )
 
+    def weight_piece(k):
+        if k == 0:
+            return first.at[0, :, width:wide], wf.at[c, :, width:wide]
+        if k == 1:
+            return first.at[0, :, 0:width], wf.at[c, :, 0:width]
+        if k == 2:
+            return first.at[0, :, wide:], wf.at[c, :, wide:]
+        return down.at[0], wd.at[c]
+
+    def weight_local(k):
+        src, dst = weight_piece(k)
+        return pltpu.make_async_copy(src, dst, wl.at[k])
+
+    def weight_remote(k):
+        if k == 4:
+            return remote(nrm.at[c], nrm.at[c], ws.at[4], wr.at[4], core_peer)
+        src, dst = weight_piece(k)
+        return remote(src, dst, ws.at[k], wr.at[k], core_peer)
+
+    nrm[c, 0:1, :] = gain[...]
+    nrm[c, 1:2, :] = shift[...]
+    weight_local(0).start()
+
+    @pl.when(x == 0)
+    def _():
+        token_copy(0).start()
+
+    pl.semaphore_wait(barrier, 2)
+    for k in range(5):
+        weight_remote(k).start()
+    for k in range(1, 4):
+        weight_local(k).start()
     for i in range(items):
-        @pl.when(x == 0)
-        def _():
-            token_copy(i).start()
-
-        bias_copy(i).start()
+        if i > 0:
+
+            @pl.when(x == 0)
+            def _():
+                token_copy(i).start()
+
+        @pl.when(x == 1)
+        def _():
+            cot_copy(i).start()
+
+    def wait_first_of(core, ks):
+        @pl.when(c == core)
+        def _():
+            for k in ks:
+                weight_local(k).wait()
+
+        @pl.when(c != core)
+        def _():
+            for k in ks:
+                weight_remote(k).wait_recv()
 
     for i in range(items):
-        @pl.when(x == 1)
-        def _():
-            cot_copy(i).start()
+        seq, seg = i % n, i // n
+        kdoc[i] = docs[seq : seq + 1, seg * seg_len : (seg + 1) * seg_len].astype(F32)
+        own = pl.ds(pl.multiple_of(seg * seg_len + c * toks, toks), toks)
+        own_row = docs[seq : seq + 1, own].astype(F32)
+        qdoc[i] = jnp.transpose(jnp.broadcast_to(own_row, (128, toks)))
+        if seg > 0:
+            flag = resets[seq : seq + 1, seg - 1 : seg].astype(F32)
+            keep[i] = jnp.broadcast_to(1.0 - flag, (MEM_PAD, 128))
 
     def routed(kind, i):
         block = i * 2 + c
@@ -215,8 +236,9 @@
         def _():
             route_away(kind, i).wait_recv()
 
-    def kv_copy(i):
-        return remote(kv.at[i, c], kv.at[i, c], kvs_sem.at[i], kvr_sem.at[i], core_peer)
+    def kv_copy(part, i):
+        piece = kv.at[i, c, :, part * width : (part + 1) * width]
+        return remote(piece, piece, kvs_sem.at[part, i], kvr_sem.at[part, i], core_peer)
 
     def x_copy(i):
         return remote(yd.at[i], x0.at[i], xs_sem.at[i], xr_sem.at[i], chip_peer)
@@ -234,26 +256,76 @@
             yd.at[i, toks:rows, :], mgin.at[i], hs_sem.at[i], hr_sem.at[i], chip_peer
         )
 
-    def dkv_copy(i, slot):
+    def dkv_copy(j, i, slot):
         return remote(
-            dkvs.at[1 - c], dkvin.at[slot], ds_sem.at[i], dr_sem.at[i], core_peer
-        )
-
-    lane = lax.broadcasted_iota(jnp.int32, (rows, lanes), 1)
-    first_head = lane < lanes // 2
-    stat_lane = lax.broadcasted_iota(jnp.int32, (rows, lanes), 1)
-    key_first_head = lax.broadcasted_iota(jnp.int32, (2 * rows, lanes), 1) < lanes // 2
-
-    def lane_block(j, base=0):
-        return pl.ds(pl.multiple_of(base + j * lanes, lanes), lanes)
-
-    def masked_scores(qm, k2, i):
-        s = dot(qm, k2, 1, 1)
-        b = biasb[i]
-        return jnp.where(b == 0.0, s, b)
-
-    def both_keys(i, cols):
-        return jnp.concatenate([kv[i, 0, :, cols], kv[i, 1, :, cols]], axis=0)
+            dkvs.at[1 - c, j], dkvin.at[slot, j], ds_sem.at[j, i], dr_sem.at[j, i], core_peer
+        )
+
+    head_lanes = group_of((rows, quad), 1, head_dim)
+    mem_lanes = group_of((rows, 4 * mem_keys), 1, mem_keys)
+    key_lane = lax.broadcasted_iota(jnp.int32, (rows, 4 * mem_keys), 1)
+    mem_valid = lax.rem(key_lane, MEM_PAD) < M // 2
+    diagonal = group_of((4 * mem_keys, quad), 0, mem_keys) == group_of(
+        (4 * mem_keys, quad), 1, head_dim
+    )
+    stat_lane = lax.broadcasted_iota(jnp.int32, (rows, 128), 1)
+
+    def stacked(block):
+        return jnp.concatenate(
+            [jnp.where(head_lanes == h, block, BF16(0)) for h in range(4)], axis=0
+        )
+
+    def head_rows(block):
+        return [block[h * rows : (h + 1) * rows] for h in range(4)]
+
+    def token_and_memory(i, low):
+        cols = slice(low, low + quad)
+        tok = jnp.concatenate([kv[i, 0, 0:toks, cols], kv[i, 1, 0:toks, cols]], axis=0)
+        mem = jnp.concatenate([kv[i, 0, toks:, cols], kv[i, 1, toks:, cols]], axis=0)
+        return tok, jnp.where(diagonal, jnp.concatenate([mem] * 4, axis=0), BF16(0))
+
+    def only_same_document(s, i):
+        mine = jnp.concatenate([qdoc[i]] * (seg_len // 128), axis=1)
+        same = jnp.where(mine == kdoc[i], s[0:toks], MASKED_SCORE)
+        return jnp.concatenate([same, s[toks:]], axis=0)
+
+    def memory_scores(q4, mem_k):
+        return jnp.where(mem_valid, dot(q4, mem_k, 1, 1), ABSENT_SCORE)
+
+    def attend(i):
+        st = jnp.zeros((rows, 128), F32)
+        for j in range(quads):
+            cols = slice(j * quad, (j + 1) * quad)
+            q4 = q[i, :, cols]
+            if j == 0:
+                kv_copy(0, i).wait_recv()
+            tok_k, mem_k = token_and_memory(i, j * quad)
+            s = head_rows(dot(stacked(q4), tok_k, 1, 1))
+            sm = memory_scores(q4, mem_k)
+            peaks, totals, probs = [], [], []
+            for h in range(4):
+                sh = only_same_document(s[h], i)
+                own_mem = jnp.where(mem_lanes == h, sm, ABSENT_SCORE)
+                peak = jnp.maximum(
+                    jnp.max(sh, axis=1, keepdims=True), jnp.max(own_mem, axis=1, keepdims=True)
+                )
+                p = jnp.exp(sh - peak)
+                peaks.append(peak)
+                totals.append(jnp.sum(p, axis=1, keepdims=True))
+                probs.append(p.astype(BF16))
+            pm = jnp.exp(sm - spread(peaks, mem_lanes))
+            for h in range(4):
+                totals[h] += jnp.sum(jnp.where(mem_lanes == h, pm, 0.0), axis=1, keepdims=True)
+                lse = peaks[h] + jnp.log(totals[h])
+                st = jnp.where(stat_lane == 4 * j + h, lse, st)
+            if j == 0:
+                kv_copy(1, i).wait_recv()
+            tok_v, mem_v = token_and_memory(i, width + j * quad)
+            o = spread(head_rows(dot(jnp.concatenate(probs, axis=0), tok_v)), head_lanes)
+            o = o + dot(pm.astype(BF16), mem_v)
+            inverse = spread([1.0 / total for total in totals], head_lanes)
+            ctx[i, :, cols] = (o * inverse).astype(BF16)
+        stats[i] = st
 
     def forward_tick(t, carry):
         i = t - x
@@ -283,85 +355,45 @@
             def _():
                 wait_first_of(0, (0,))
 
-            xb = x0[i]
-            for col in range(width, wide, ncol):
-                kv[i, c, :, col - width : col - width + ncol] = dot(
-                    xb, wf[0, :, col : col + ncol]
+            for part in range(2):
+                kv[i, c, :, part * width : (part + 1) * width] = dot(
+                    x0[i], wf[0, :, (part + 1) * width : (part + 2) * width]
                 ).astype(BF16)
-            kv_copy(i).start()
+                kv_copy(part, i).start()
+
+            @pl.when(i == 0)
+            def _():
+                wait_first_of(0, (1,))
+
+            q[i] = dot(x0[i], wf[0, :, 0:width]).astype(BF16) * BF16(scale)
+            attend(i)
             route(S_X0, i)
+            route(S_CTX, i)
 
             @pl.when(i == 0)
             def _():
-                wait_first_of(0, (1,))
-
-            for col in range(0, width, ncol):
-                q[i, :, col : col + ncol] = (
-                    dot(xb, wf[0, :, col : col + ncol]).astype(BF16) * BF16(0.125)
-                )
-            bias_copy(i).wait()
-            kv_copy(i).wait_recv()
-            stats[i] = jnp.zeros((rows, lanes), F32)
-
-            def head_pair(j, carry):
-                cols = lane_block(j)
-                q2 = q[i, :, cols]
-                k2 = both_keys(i, cols)
-                v2 = both_keys(i, lane_block(j, width))
-                outs = []
-                for e in range(2):
-                    mine = first_head if e == 0 else ~first_head
-                    s = masked_scores(jnp.where(mine, q2, BF16(0)), k2, i)
-                    peak = jnp.max(s, axis=1, keepdims=True)
-                    p = jnp.exp(s - peak)
-                    total = jnp.sum(p, axis=1, keepdims=True)
-                    outs.append(dot(p.astype(BF16), v2) * (1.0 / total))
-                    lse = peak + jnp.log(total)
-                    stats[i] = jnp.where(stat_lane == 2 * j + e, lse, stats[i])
-                ctx[i, :, cols] = jnp.where(first_head, outs[0], outs[1]).astype(BF16)
-                return carry
-
-            lax.fori_loop(0, heads // 2, head_pair, 0)
-            route(S_CTX, i)
-
-            @pl.when(i == 0)
-            def _():
                 wait_first_of(0, (2,))
-
-                @pl.when(c == 0)
-                def _():
-                    wait_remote(4)
-
-                @pl.when(c == 1)
-                def _():
-                    wait_remote(4)
-
-            for col in range(0, width, ncol):
-                dhb[:, col : col + ncol] = dot(
-                    ctx[i], wf[0, :, wide + col : wide + col + ncol]
-                ) + x0[i, :, col : col + ncol].astype(F32)
-            normed, inv = normalize(dhb[...])
+                weight_remote(4).wait_recv()
+
+            normed, inv = normalize(dot(ctx[i], wf[0, :, wide:]) + x0[i].astype(F32))
             natt[i] = normed.astype(BF16)
             stats[i] = jnp.where(stat_lane == heads, inv, stats[i])
             yatt[i] = (normed * nrm[0, 0:1, :] + nrm[0, 1:2, :]).astype(BF16)
-            route(OUT_ATT, i)
-            route(S_Y1, i)
-            route(S_Y2, i)
 
             @pl.when(i == 0)
             def _():
                 wait_first_of(1, (0, 1, 2))
 
-            def up(k, carry):
-                cols = pl.ds(pl.multiple_of(k * chunk, chunk), chunk)
+            for part in range(2):
+                cols = slice(part * hidden_half, (part + 1) * hidden_half)
                 u = dot(yatt[i], wf[1, :, cols])
                 cdf = 0.5 + 0.5 * lax.erf(u * 0.7071067811865476)
                 pdf = 0.3989422804014327 * jnp.exp(-0.5 * u * u)
                 g[i, :, cols] = (u * cdf).astype(BF16)
                 gp[i, :, cols] = (cdf + u * pdf).astype(BF16)
-                return carry
-
-            lax.fori_loop(0, hidden // chunk, up, 0)
+            route(OUT_ATT, i)
+            route(S_Y1, i)
+            route(S_Y2, i)
             route(S_GLO, i)
             route(S_GHI, i)
 
@@ -370,25 +402,23 @@
                 wait_first_of(0, (3,))
                 wait_first_of(1, (3,))
 
-            for col in range(0, width, ncol):
-                dhb[:, col : col + ncol] = (
-                    dot(g[i, :, 0:hidden_half], wd[0, :, col : col + ncol])
-                    + dot(g[i, :, hidden_half:], wd[1, :, col : col + ncol])
-                    + yatt[i, :, col : col + ncol].astype(F32)
-                )
-            normed, inv = normalize(dhb[...])
+            normed, inv = normalize(
+                dot(g[i, :, 0:hidden_half], wd[0])
+                + dot(g[i, :, hidden_half:], wd[1])
+                + yatt[i].astype(F32)
+            )
+            yd[i] = (normed * nrm[1, 0:1, :] + nrm[1, 1:2, :]).astype(BF16)
+
+            @pl.when(x == 0)
+            def _():
+                x_copy(i).start()
+
+            @pl.when((x == 1) & (i < items - n))
+            def _():
+                mem_copy(i).start()
+
             nff[i] = normed.astype(BF16)
             stats[i] = jnp.where(stat_lane == heads + 1, inv, stats[i])
-            yd[i] = (normed * nrm[1, 0:1, :] + nrm[1, 1:2, :]).astype(BF16)
-
-            @pl.when(x == 0)
-            def _():
-                x_copy(i).start()
-
-            @pl.when((x == 1) & (i < items - n))
-            def _():
-                mem_copy(i).start()
-
             route(OUT_FF, i)
 
         return carry
@@ -396,7 +426,8 @@
     lax.fori_loop(0, items + 1, forward_tick, 0)
 
     def forward_drain(i, carry):
-        kv_copy(i).wait_send()
+        kv_copy(0, i).wait_send()
+        kv_copy(1, i).wait_send()
         route_sent(OUT_FF, i)
 
         @pl.when(x == 0)
@@ -415,7 +446,7 @@
     def norm_back(s, i, normed_ref):
         grad = gy[i].astype(F32)
         normed = normed_ref[i].astype(F32)
-        inv = jnp.sum(jnp.where(stat_lane == heads + s, stats[i], 0.0), axis=1, keepdims=True)
+        inv = stats[i][:, heads + s : heads + s + 1]
         acc[s, 0:1, :] += jnp.sum(grad * normed, axis=0, keepdims=True)
         acc[s, 1:2, :] += jnp.sum(grad, axis=0, keepdims=True)
         scaled = grad * nrm[s, 0:1, :]
@@ -425,6 +456,64 @@
         dhb[...] = dh
         normed_ref[i] = dh.astype(BF16)
 
+    def attend_back(i, slot):
+        for j in range(quads):
+            cols = slice(j * quad, (j + 1) * quad)
+            q4 = q[i, :, cols]
+            c4 = dctx[:, cols]
+            tok_k, mem_k = token_and_memory(i, j * quad)
+            tok_v, mem_v = token_and_memory(i, width + j * quad)
+            products = c4.astype(F32) * ctx[i, :, cols].astype(F32)
+            qs, cs = stacked(q4), stacked(c4)
+            s = head_rows(dot(qs, tok_k, 1, 1))
+            dp = head_rows(dot(cs, tok_v, 1, 1))
+            sm = memory_scores(q4, mem_k)
+            dpm = dot(c4, mem_v, 1, 1)
+            lse = [stats[i][:, 4 * j + h : 4 * j + h + 1] for h in range(4)]
+            inner = [
+                jnp.sum(jnp.where(head_lanes == h, products, 0.0), axis=1, keepdims=True)
+                for h in range(4)
+            ]
+            probs, dscores = [], []
+            for h in range(4):
+                p = jnp.exp(only_same_document(s[h], i) - lse[h])
+                probs.append(p.astype(BF16))
+                dscores.append((p * (dp[h] - inner[h])).astype(BF16))
+            pm = jnp.exp(sm - spread(lse, mem_lanes))
+            dsm = (pm * (dpm - spread(inner, mem_lanes))).astype(BF16)
+            probs = jnp.concatenate(probs, axis=0)
+            dscores = jnp.concatenate(dscores, axis=0)
+            dv = dot(probs, cs, 0, 0)
+            dk = dot(dscores, qs, 0, 0)
+            dq = spread(head_rows(dot(dscores, tok_k)), head_lanes) + dot(dsm, mem_k)
+            q[i, :, cols] = (dq * scale).astype(BF16)
+            dvm = jnp.where(diagonal, dot(pm.astype(BF16), c4, 0, 0), 0.0)
+            dkm = jnp.where(diagonal, dot(dsm, q4, 0, 0), 0.0)
+            dvm = sum(dvm[h * mem_keys : (h + 1) * mem_keys] for h in range(4))
+            dkm = sum(dkm[h * mem_keys : (h + 1) * mem_keys] for h in range(4))
+            for half, (tok_part, mem_part) in enumerate(((dk, dkm), (dv, dvm))):
+                cols = slice(half * quad, (half + 1) * quad)
+                for core in range(2):
+                    dkvs[core, j, 0:toks, cols] = tok_part[
+                        core * toks : (core + 1) * toks
+                    ].astype(BF16)
+                    dkvs[core, j, toks:rows, cols] = mem_part[
+                        core * MEM_PAD : (core + 1) * MEM_PAD
+                    ].astype(BF16)
+            dkv_copy(j, i, slot).start()
+
+    def gather_dkv(j, i, slot):
+        dkv_copy(j, i, slot).wait_recv()
+        both = (dkvs[c, j].astype(F32) + dkvin[slot, j].astype(F32)).astype(BF16)
+        kv[i, c, :, j * quad : (j + 1) * quad] = both[:, 0:quad]
+        kv[i, c, :, width + j * quad : width + (j + 1) * quad] = both[:, quad:]
+
+    def dkv_back(i, low, high):
+        return dot(kv[i, c, :, low:high], wf[0, :, width + low : width + high], 1, 1) + dot(
+            kv[i, c, :, width + low : width + high],
+            wf[0, :, 2 * width + low : 2 * width + high], 1, 1,
+        )
+
     def backward_tick(t, carry):
         r = t - (1 - x)
 
@@ -453,87 +542,42 @@
                 gy_copy(i).wait_recv()
 
             norm_back(1, i, nff)
+            for part in range(2):
+                cols = slice(part * hidden_half, (part + 1) * hidden_half)
+                dg = dot(nff[i], wd[part], 1, 1)
+                gp[i, :, cols] = (dg * gp[i, :, cols].astype(F32)).astype(BF16)
+            gy[i] = (dot(gp[i], wf[1], 1, 1) + dhb[...]).astype(BF16)
+            norm_back(0, i, natt)
+            dctx[...] = dot(natt[i], wf[0, :, wide:], 1, 1).astype(BF16)
             route(S_DFF0, i)
             route(S_DFF1, i)
-
-            def down_back(k, carry):
-                cols = pl.ds(pl.multiple_of(k * chunk, chunk), chunk)
-                part = pl.ds(pl.multiple_of(lax.rem(k, per_half) * chunk, chunk), chunk)
-                dg = dot(nff[i], wd[lax.div(k, per_half), part, :], 1, 1)
-                gp[i, :, cols] = (dg * gp[i, :, cols].astype(F32)).astype(BF16)
-                return carry
-
-            lax.fori_loop(0, hidden // chunk, down_back, 0)
             route(S_DU, i)
-            for col in range(0, width, ncol):
-                gy[i, :, col : col + ncol] = (
-                    dot(gp[i], wf[1, col : col + ncol, :], 1, 1) + dhb[:, col : col + ncol]
-                ).astype(BF16)
             route(GIN_FF, i)
-
-            norm_back(0, i, natt)
             route(S_DATT, i)
-            for col in range(0, width, ncol):
-                dctx[:, col : col + ncol] = dot(
-                    natt[i], wf[0, col : col + ncol, wide:], 1, 1
-                ).astype(BF16)
-
-            def head_pair(j, carry):
-                cols = lane_block(j)
-                q2 = q[i, :, cols]
-                k2 = both_keys(i, cols)
-                v2 = both_keys(i, lane_block(j, width))
-                c2 = dctx[:, cols]
-                t2 = c2.astype(F32) * ctx[i, :, cols].astype(F32)
-                dq2, dk2, dv2 = 0.0, 0.0, 0.0
-                for e in range(2):
-                    mine = first_head if e == 0 else ~first_head
-                    key_mine = key_first_head if e == 0 else ~key_first_head
-                    qm = jnp.where(mine, q2, BF16(0))
-                    cm = jnp.where(mine, c2, BF16(0))
-                    km = jnp.where(key_mine, k2, BF16(0))
-                    lse = jnp.sum(
-                        jnp.where(stat_lane == 2 * j + e, stats[i], 0.0), axis=1, keepdims=True
-                    )
-                    inner = jnp.sum(jnp.where(mine, t2, 0.0), axis=1, keepdims=True)
-                    p = jnp.exp(masked_scores(qm, k2, i) - lse)
-                    dp = dot(cm, v2, 1, 1)
-                    ds = (p * (dp - inner)).astype(BF16)
-                    dv2 = dv2 + dot(p.astype(BF16), cm, 0, 0)
-                    dk2 = dk2 + dot(ds, qm, 0, 0)
-                    dq2 = dq2 + dot(ds, km)
-                q[i, :, cols] = (dq2 * 0.125).astype(BF16)
-                vcols = lane_block(j, width)
-                dkvs[0, :, cols] = dk2[0:rows].astype(BF16)
-                dkvs[1, :, cols] = dk2[rows:].astype(BF16)
-                dkvs[0, :, vcols] = dv2[0:rows].astype(BF16)
-                dkvs[1, :, vcols] = dv2[rows:].astype(BF16)
-                return carry
-
-            lax.fori_loop(0, heads // 2, head_pair, 0)
-            dkv_copy(i, slot).start()
+            attend_back(i, slot)
+            for j in range(quads - 1):
+                gather_dkv(j, i, slot)
+            early = (quads - 1) * quad
+            partial_sum = dot(q[i], wf[0, :, 0:width], 1, 1) + dhb[...]
+            if early:
+                partial_sum = partial_sum + dkv_back(i, 0, early)
+            dhb[...] = partial_sum
+            gather_dkv(quads - 1, i, slot)
+            yd[i] = (dkv_back(i, early, width) + dhb[...]).astype(BF16)
+
+            @pl.when(x == 1)
+            def _():
+                gy_copy(i).start()
+
+            @pl.when((x == 0) & (i >= n))
+            def _():
+                mg_copy(i).start()
+
             route(S_DQ, i)
-            for col in range(0, width, ncol):
-                dhb[:, col : col + ncol] += dot(q[i], wf[0, col : col + ncol, 0:width], 1, 1)
-            dkv_copy(i, slot).wait_recv()
-            kv[i, c] = (dkvs[c].astype(F32) + dkvin[slot].astype(F32)).astype(BF16)
             route(S_DKV, i)
-            for col in range(0, width, ncol):
-                yd[i, :, col : col + ncol] = (
-                    dot(kv[i, c], wf[0, col : col + ncol, width:wide], 1, 1)
-                    + dhb[:, col : col + ncol]
-                ).astype(BF16)
-
-            @pl.when(x == 1)
-            def _():
-                gy_copy(i).start()
-
-            @pl.when((x == 0) & (i >= n))
-            def _():
-                mg_copy(i).start()
-
             route(GIN_ATT, i)
-            dkv_copy(i, slot).wait_send()
+            for j in range(quads):
+                dkv_copy(j, i, slot).wait_send()
 
         return carry
 
@@ -558,24 +602,25 @@
         return carry
 
     lax.fori_loop(0, items, backward_drain, 0)
-    for k in range(4):
-        src, dst = weight_piece(k)
-        remote(src, dst, ws.at[k], wr.at[k], core_peer).wait_send()
-    nrm_copy.wait_send()
+    for k in range(5):
+        weight_remote(k).wait_send()
     acc_copy.wait()
     norm_grad[...] = acc[c] + accp[...]
 
 
-def run_layers(n, nseg, heads, tokens, cotangent, first, down, bias, gain_bias, keep):
+def run_layers(n, nseg, heads, tokens, cotangent, first, down, docs, resets, gain, shift):
     length, width = tokens.shape[1:]
     toks = length // nseg // 2
     rows = toks + MEM_PAD
     items = n * nseg
-    hidden_half = down.shape[0]
+    hidden_half = down.shape[1]
+    quads = heads // 4
+    quad = width // quads
     any_spec = pl.BlockSpec(memory_space=pl.ANY)
     vmem_spec = pl.BlockSpec(memory_space=pltpu.VMEM)
     dma = pltpu.SemaphoreType.DMA
     item_rows = pltpu.VMEM((items, rows, width), BF16)
+    one = dma((items,))
     return pl.pallas_call(
         partial(layers_kernel, n, nseg, heads),
         out_shape=(
@@ -588,7 +633,7 @@
             jax.ShapeDtypeStruct((2 * items, rows, width), BF16),
             jax.ShapeDtypeStruct((2, width), F32),
         ),
-        in_specs=[any_spec] * 5 + [vmem_spec] * 2,
+        in_specs=[any_spec] * 4 + [vmem_spec] * 4,
         out_specs=[any_spec] * 7 + [vmem_spec],
         scratch_shapes=[
             pltpu.VMEM((2, width, 4 * width), BF16),
@@ -606,24 +651,29 @@
             pltpu.VMEM((items, rows, 2 * hidden_half), BF16),
             pltpu.VMEM((items, rows, 2 * hidden_half), BF16),
             pltpu.VMEM((items, rows, 128), F32),
-            pltpu.VMEM((items, rows, 2 * rows), F32),
+            pltpu.VMEM((items, toks, 128), F32),
+            pltpu.VMEM((items, 1, 2 * toks), F32),
+            pltpu.VMEM((items, MEM_PAD, 128), F32),
             pltpu.VMEM((items, MEM_PAD, width), BF16),
             pltpu.VMEM((items, MEM_PAD, width), BF16),
-            pltpu.VMEM((2, rows, 2 * width), BF16),
-            pltpu.VMEM((2, rows, 2 * width), BF16),
+            pltpu.VMEM((2, quads, rows, 2 * quad), BF16),
+            pltpu.VMEM((2, quads, rows, 2 * quad), BF16),
             pltpu.VMEM((rows, width), F32),
             pltpu.VMEM((rows, width), BF16),
             pltpu.VMEM((2, 2, width), F32),
             pltpu.VMEM((2, width), F32),
             dma((4,)), dma((5,)), dma((5,)),
+            one, one,
+            dma((2, items)), dma((2, items)),
+            one, one, one, one, one, one, one, one,
+            dma((quads, items)), dma((quads, items)),
+            dma(()), dma(()),
         ]
-        + [dma((items,))] * 15
-        + [dma(()), dma(())]
         + [dma((KINDS, items))] * 3,
         compiler_params=pltpu.CompilerParams(
-            collective_id=0, has_side_effects=True, vmem_limit_bytes=60 * 1024 * 1024
+            collective_id=0, has_side_effects=True, vmem_limit_bytes=61 * 1024 * 1024
         ),
-    )(tokens, cotangent, first, down, bias, gain_bias, keep)
+    )(tokens, cotangent, first, down, docs, resets, gain, shift)
 
 
 def reduce_kernel(
@@ -800,6 +850,30 @@
 
             store_chunks(group, 3, dot(x2[:, cols], rr[:, 3 * width :], 0, 0).astype(BF16))
 
+        for flow in range(2):
+            p = place(flow)
+            k = r - (lines - 1 - p)
+            rows = rows_of(flow)
+
+            @pl.when(ready(k))
+            def _():
+                @pl.when(p < lines - 1)
+                def _():
+                    vz_copy(flow, k).wait_recv()
+                    work[k, 3:6, rows, :] = plus(work[k, 3:6, rows, :], got_vz[flow, k])
+
+                @pl.when(p > 0)
+                def _():
+                    vz_copy(flow, k).start()
+
+                @pl.when(p == 0)
+                def _():
+                    vy_copy(flow, k).start()
+
+        @pl.when((lax.rem(r, per_group) == 0) & (r < chunks))
+        def _():
+            cols = pl.ds(pl.multiple_of(group * lane_group, lane_group), lane_group)
+
             @pl.when(r == 0)
             def _():
                 wait_load(5)
@@ -814,26 +888,6 @@
         @pl.when(ready(r))
         def _():
             u_copy(r).start()
-
-        for flow in range(2):
-            p = place(flow)
-            k = r - (lines - 1 - p)
-            rows = rows_of(flow)
-
-            @pl.when(ready(k))
-            def _():
-                @pl.when(p < lines - 1)
-                def _():
-                    vz_copy(flow, k).wait_recv()
-                    work[k, 3:6, rows, :] = plus(work[k, 3:6, rows, :], got_vz[flow, k])
-
-                @pl.when(p > 0)
-                def _():
-                    vz_copy(flow, k).start()
-
-                @pl.when(p == 0)
-                def _():
-                    vy_copy(flow, k).start()
 
         @pl.when(ready(r - 1))
         def _():
@@ -1027,32 +1081,12 @@
 def shards(
     tokens, doc_ids, reset_flags, first_weights, down_halves, norm_gain, norm_bias, cotangent
 ):
-    c = lax.rem(lax.axis_index("section"), 2)
     n, length, width = tokens.shape
-    nseg = NSEG
-    seg_len = length // nseg
-    toks = seg_len // 2
-    items = n * nseg
-    mem_half = M // 2
-    rows = toks + MEM_PAD
-
-    docs = doc_ids.reshape(n, nseg, 2, toks).transpose(1, 0, 2, 3).reshape(items, 2, toks)
-    tail = jnp.where(lax.iota(jnp.int32, MEM_PAD) < mem_half, -1, -2)
-    tail = jnp.broadcast_to(tail, (items, 2, MEM_PAD))
-    marks = jnp.concatenate([docs, tail], axis=2)
-    own = lax.dynamic_index_in_dim(marks, c, 1, keepdims=False)
-    keys = marks.reshape(items, 1, 2 * rows)
-    own = own[:, :, None]
-    allowed = (own == keys) | (keys == -1) | (own < 0)
-    bias = jnp.where(keys == -2, ABSENT_SCORE, jnp.where(allowed, 0.0, MASKED_SCORE))
-    bias = bias.astype(F32)
-    resets = jnp.concatenate([jnp.ones((n, 1), jnp.int32), reset_flags], axis=1)
-    keep = (1 - resets).astype(F32).T.reshape(items, 1, 1)
-    keep = jnp.broadcast_to(keep, (items, MEM_PAD, 128))
-    gain_bias = jnp.concatenate([norm_gain, norm_bias], axis=0)
-
+    items = n * NSEG
+    rows = length // NSEG // 2 + MEM_PAD
     out, gin, sx1, sx2, sr, sg, sd, norm_grad = run_layers(
-        n, nseg, H, tokens, cotangent, first_weights[0], down_halves[0], bias, gain_bias, keep
+        n, NSEG, H, tokens, cotangent, first_weights, down_halves,
+        doc_ids, reset_flags, norm_gain, norm_bias,
     )
     total = 2 * items * rows
     sx1, sx2, sd = (a.reshape(total, width) for a in (sx1, sx2, sd))

time: 410 us -> 362 us (0.88)
  Pallas kernels: 389 us -> 347 us
    pallas_call x1, Pallas kernels: 239 us -> 200 us  [run_layers(): pl.pallas_call(partial(layers_kernel, n, nseg, heads), out_shape=(jax.Sha...]
    unnamed x13 -> x15, local copies, waits for them, and re-layouts: 12.8 us -> 13.3 us
where the time goes in v3:
time: 362 us
  Pallas kernels  347 us (96%)
  local copies, waits for them, and re-layouts  14.7 us (4%)
    pallas_call x1, Pallas kernels, run_layers(): pl.pallas_call(partial(layers_kernel, n, nseg, heads), out_shape=(jax.Sha...  200 us
    pallas_call x1, Pallas kernels, sum_weights(): pl.pallas_call(partial(reduce_kernel, chunks), out_shape=(jax.ShapeDtypeS...  147 us
    unnamed x15, local copies, waits for them, and re-layouts  13.3 us

profile of v3, /device:TPU:0, one launch (start us, length us, event | category | flops | bytes accessed | tf_op | source)
XLA Modules:
  0.0 362.1 jit_solution(966600154994723055)
XLA Ops:
  0.6 1.3 copy.14.resets
  1.9 200.1 %shard_map.127 = (bf16[2,1024,768]{2,1,0:T(8,128)(2,1)}, bf16[2,1024,768]{2,1,0:T(8,128)(2,1)}, bf16[8,272,768]{2,1,0:T(8,128)(2,1)}, bf16[8,272,768]{2,1,0:T(8,...) custom-call(bf16[2,1024,768]{2,1,0:T(8,128)(2,1)} %tokens.1, ...), custom_call_target="tpu_custom_call" | custom-call | tf_op jit(solution)/shard_map/pallas_call | solution.py:624
  202.0 0.0 copy-start.2
  202.0 146.7 %shard_map.128 = (f32[768,3072]{1,0:T(8,128)}, f32[1536,768]{1,0:T(8,128)}, f32[2,768]{1,0:T(2,128)}) custom-call(bf16[2176,768]{1,0:T(8,128)(2,1)} %bitcast.15, bf16[2176,768]{1,0:T(8,128)(2,1)} %bitcast.16, bf16[2176,3072]{1,0:T(8,128)(2,1)} %bitcast.9, bf16[2176,1536]{1,0:T(8,128)(2,1)} %bitcast.11, bf16[2176,768]{1,0:T(8,128)(2,1)} %bitcast.17, ...), custom_call_target="tpu_custom_call" | custom-call | tf_op jit(solution)/shard_map/pallas_call | solution.py:1040
  348.7 0.0 copy-start.1
  348.7 1.4 fusion
  350.1 0.0 copy-done.2
  350.1 0.0 copy-start
  350.1 1.7 copy.19
  351.8 0.0 copy-done.1
  351.8 0.0 slice-start
  351.8 1.7 copy.20
  353.5 2.7 copy-done
  356.2 0.0 slice-start.1
  356.2 3.7 %copy.21 = f32[1,768,3072]{2,1,0:T(8,128)} copy(f32[1,768,3072]{2,1,0:T(8,128)S(1)} %bitcast.10) | data formatting | bytes 18874368
  360.0 0.0 slice-done
  360.0 0.0 slice-done.1
  360.0 2.2 copy.22
  (1 shorter events, 0.0 us)
Async XLA Ops:
  202.0 148.1 %copy-start.2 = (bf16[2,1024,768]{2,1,0:T(8,128)(2,1)S(1)}, bf16[2,1024,768]{2,1,0:T(8,128)(2,1)}, u32[]{:S(2)}) copy-start(bf16[2,1024,768]{2,1,0:T(8,128)(2,1)} %get-tuple-element.17) | copy-start | bytes 9437188
  348.7 3.1 copy-start.1
  350.1 6.1 %copy-start = (f32[768,3072]{1,0:T(8,128)S(1)}, f32[768,3072]{1,0:T(8,128)}, u32[]{:S(2)}) copy-start(f32[768,3072]{1,0:T(8,128)} %get-tuple-element.25) | copy-start | bytes 28311556
  351.8 8.1 %slice-start = ((s8[4718592]{0:T(1024)(128)(4,1)}), s8[4194304]{0:T(1024)(128)(4,1)S(1)}, s32[]{:S(2)}) async-start(s8[4718592]{0:T(1024)(128)(4,1)} %bitcast.12), calls=%async_computation | async-start | bytes 8388608
  356.2 3.7 %slice-start.1 = ((s8[4718592]{0:T(1024)(128)(4,1)}), s8[524288]{0:T(1024)(128)(4,1)S(1)}, s32[]{:S(2)}) async-start(s8[4718592]{0:T(1024)(128)(4,1)} %bitcast.12), calls=%async_computation.1 | async-start | bytes 1048576

commit v4 on v3

--- a/solution.py
+++ b/solution.py
@@ -54,9 +54,9 @@
     n, nseg, heads,
     tokens, cotangent, first, down, docs, resets, gain, shift,
     out, gin, sx1, sx2, sr, sg, sd, norm_grad,
-    wf, wd, nrm, x0, q, kv, ctx, natt, yatt, nff, yd, gy, g, gp, stats, qdoc, kdoc, keep,
+    wf, wd, nrm, x0, xo, q, kv, ctx, natt, yatt, nff, yd, gy, g, gpb, gp, stats, qdoc, kdoc, keep,
     memin, mgin, dkvs, dkvin, dhb, dctx, acc, accp,
-    wl, ws, wr, tok_sem, cot_sem, kvs_sem, kvr_sem, xs_sem, xr_sem,
+    wl, ws, wr, tok_sem, cot_sem, gp_sem, fs_sem, fr_sem, xs_sem, xr_sem,
     ms_sem, mr_sem, gs_sem, gr_sem, hs_sem, hr_sem, ds_sem, dr_sem, as_sem, ar_sem,
     lsem, ssem, rsem,
 ):
@@ -66,6 +66,7 @@
     x = lax.div(section, 2)
     core_peer = {"section": x * 2 + (1 - c)}
     chip_peer = {"section": (1 - x) * 2 + c}
+    cross_peer = {"section": (1 - x) * 2 + (1 - c)}
     rows, width = x0.shape[1:]
     toks = rows - MEM_PAD
     seg_len = 2 * toks
@@ -86,14 +87,18 @@
     barrier = pltpu.get_barrier_semaphore()
     pl.semaphore_signal(barrier, inc=1, device_id=core_peer, device_id_type=MESH)
     pl.semaphore_signal(barrier, inc=1, device_id=chip_peer, device_id_type=MESH)
-
-    def token_rows(ref, i):
-        return ref.at[lax.rem(i, n), pl.ds(lax.div(i, n) * seg_len + c * toks, toks), :]
-
-    def token_copy(i):
-        return pltpu.make_async_copy(
-            token_rows(tokens, i), x0.at[i, 0:toks, :], tok_sem.at[i]
-        )
+    pl.semaphore_signal(barrier, inc=1, device_id=cross_peer, device_id_type=MESH)
+
+    def token_rows(ref, i, core=None):
+        core = c if core is None else core
+        return ref.at[lax.rem(i, n), pl.ds(lax.div(i, n) * seg_len + core * toks, toks), :]
+
+    def token_copy(which, i):
+        if which == 0:
+            src, dst = token_rows(tokens, i), x0.at[i, 0:toks, :]
+        else:
+            src, dst = token_rows(tokens, i, 1 - c), xo.at[i, 0:toks, :]
+        return pltpu.make_async_copy(src, dst, tok_sem.at[which, i])
 
     def cot_copy(i):
         return pltpu.make_async_copy(
@@ -125,9 +130,10 @@
 
     @pl.when(x == 0)
     def _():
-        token_copy(0).start()
-
-    pl.semaphore_wait(barrier, 2)
+        token_copy(0, 0).start()
+        token_copy(1, 0).start()
+
+    pl.semaphore_wait(barrier, 3)
     for k in range(5):
         weight_remote(k).start()
     for k in range(1, 4):
@@ -137,7 +143,8 @@
 
             @pl.when(x == 0)
             def _():
-                token_copy(i).start()
+                token_copy(0, i).start()
+                token_copy(1, i).start()
 
         @pl.when(x == 1)
         def _():
@@ -186,7 +193,7 @@
         elif kind == S_DATT:
             src, dst = natt.at[i], sr.at[block, :, wide:]
         elif kind == S_GLO:
-            src, dst = g.at[i, :, 0:hidden_half], sg.at[block]
+            src, dst = g.at[:, 0:hidden_half], sg.at[block]
         elif kind == S_DFF0:
             src, dst = nff.at[i], sd.at[block]
         elif kind == S_Y1:
@@ -196,7 +203,7 @@
         elif kind == S_DU:
             src, dst, sec = gp.at[i], sr.at[block], 1
         elif kind == S_GHI:
-            src, dst, sec = g.at[i, :, hidden_half:], sg.at[block], 1
+            src, dst, sec = g.at[:, hidden_half:], sg.at[block], 1
         else:
             src, dst, sec = nff.at[i], sd.at[block], 1
         return src, dst, sec
@@ -236,16 +243,28 @@
         def _():
             route_away(kind, i).wait_recv()
 
-    def kv_copy(part, i):
-        piece = kv.at[i, c, :, part * width : (part + 1) * width]
-        return remote(piece, piece, kvs_sem.at[part, i], kvr_sem.at[part, i], core_peer)
-
-    def x_copy(i):
-        return remote(yd.at[i], x0.at[i], xs_sem.at[i], xr_sem.at[i], chip_peer)
-
-    def mem_copy(i):
+    def gp_copy(i):
+        return pltpu.make_async_copy(gpb, gp.at[i], gp_sem.at[i])
+
+    cut = rows // 32 * 16
+
+    def piece(p):
+        return slice(0, cut) if p == 0 else slice(cut, rows)
+
+    def x_copy(p, i):
         return remote(
-            yd.at[i, toks:rows, :], memin.at[i], ms_sem.at[i], mr_sem.at[i], chip_peer
+            yd.at[i, piece(p)], x0.at[i, piece(p)], xs_sem.at[p, i], xr_sem.at[p, i], chip_peer
+        )
+
+    def pass_copy(p, i):
+        return remote(
+            x0.at[i, piece(p)], xo.at[i, piece(p)], fs_sem.at[p, i], fr_sem.at[p, i], core_peer
+        )
+
+    def mem_copy(which, i):
+        return remote(
+            yd.at[i, toks:rows, :], memin.at[which, i], ms_sem.at[which, i],
+            mr_sem.at[which, i], cross_peer if which else chip_peer,
         )
 
     def gy_copy(i):
@@ -297,8 +316,6 @@
         for j in range(quads):
             cols = slice(j * quad, (j + 1) * quad)
             q4 = q[i, :, cols]
-            if j == 0:
-                kv_copy(0, i).wait_recv()
             tok_k, mem_k = token_and_memory(i, j * quad)
             s = head_rows(dot(stacked(q4), tok_k, 1, 1))
             sm = memory_scores(q4, mem_k)
@@ -318,8 +335,6 @@
                 totals[h] += jnp.sum(jnp.where(mem_lanes == h, pm, 0.0), axis=1, keepdims=True)
                 lse = peaks[h] + jnp.log(totals[h])
                 st = jnp.where(stat_lane == 4 * j + h, lse, st)
-            if j == 0:
-                kv_copy(1, i).wait_recv()
             tok_v, mem_v = token_and_memory(i, width + j * quad)
             o = spread(head_rows(dot(jnp.concatenate(probs, axis=0), tok_v)), head_lanes)
             o = o + dot(pm.astype(BF16), mem_v)
@@ -334,38 +349,44 @@
         def _():
             @pl.when(x == 0)
             def _():
-                token_copy(i).wait()
-
-                @pl.when(i < n)
-                def _():
-                    x0[i, toks:rows, :] = jnp.zeros((MEM_PAD, width), BF16)
-
-                @pl.when(i >= n)
-                def _():
-                    mem_copy(i - n).wait_recv()
-                    x0[i, toks:rows, :] = jnp.where(
-                        keep[i][:, 0:1] > 0.0, memin[i - n], jnp.zeros((), BF16)
-                    )
+                for which, rows_ref in enumerate((x0, xo)):
+                    token_copy(which, i).wait()
+
+                    @pl.when(i < n)
+                    def _():
+                        rows_ref[i, toks:rows, :] = jnp.zeros((MEM_PAD, width), BF16)
+
+                    @pl.when(i >= n)
+                    def _():
+                        mem_copy(which, i - n).wait_recv()
+                        rows_ref[i, toks:rows, :] = jnp.where(
+                            keep[i][:, 0:1] > 0.0, memin[which, i - n], jnp.zeros((), BF16)
+                        )
 
             @pl.when(x == 1)
             def _():
-                x_copy(i).wait_recv()
+                for p in range(2):
+                    x_copy(p, i).wait_recv()
+                    pass_copy(p, i).start()
 
             @pl.when(i == 0)
             def _():
                 wait_first_of(0, (0,))
 
-            for part in range(2):
-                kv[i, c, :, part * width : (part + 1) * width] = dot(
-                    x0[i], wf[0, :, (part + 1) * width : (part + 2) * width]
-                ).astype(BF16)
-                kv_copy(part, i).start()
+            kv[i, c] = dot(x0[i], wf[0, :, width:wide]).astype(BF16)
 
             @pl.when(i == 0)
             def _():
                 wait_first_of(0, (1,))
 
             q[i] = dot(x0[i], wf[0, :, 0:width]).astype(BF16) * BF16(scale)
+
+            @pl.when(x == 1)
+            def _():
+                for p in range(2):
+                    pass_copy(p, i).wait_recv()
+
+            kv[i, 1 - c] = dot(xo[i], wf[0, :, width:wide]).astype(BF16)
             attend(i)
             route(S_X0, i)
             route(S_CTX, i)
@@ -383,14 +404,21 @@
             @pl.when(i == 0)
             def _():
                 wait_first_of(1, (0, 1, 2))
+
+            @pl.when(i > 0)
+            def _():
+                route_sent(S_GLO, i - 1)
+                route_sent(S_GHI, i - 1)
+                gp_copy(i - 1).wait()
 
             for part in range(2):
                 cols = slice(part * hidden_half, (part + 1) * hidden_half)
                 u = dot(yatt[i], wf[1, :, cols])
                 cdf = 0.5 + 0.5 * lax.erf(u * 0.7071067811865476)
                 pdf = 0.3989422804014327 * jnp.exp(-0.5 * u * u)
-                g[i, :, cols] = (u * cdf).astype(BF16)
-                gp[i, :, cols] = (cdf + u * pdf).astype(BF16)
+                g[:, cols] = (u * cdf).astype(BF16)
+                gpb[:, cols] = (cdf + u * pdf).astype(BF16)
+            gp_copy(i).start()
             route(OUT_ATT, i)
             route(S_Y1, i)
             route(S_Y2, i)
@@ -403,19 +431,21 @@
                 wait_first_of(1, (3,))
 
             normed, inv = normalize(
-                dot(g[i, :, 0:hidden_half], wd[0])
-                + dot(g[i, :, hidden_half:], wd[1])
+                dot(g[:, 0:hidden_half], wd[0])
+                + dot(g[:, hidden_half:], wd[1])
                 + yatt[i].astype(F32)
             )
             yd[i] = (normed * nrm[1, 0:1, :] + nrm[1, 1:2, :]).astype(BF16)
 
             @pl.when(x == 0)
             def _():
-                x_copy(i).start()
+                for p in range(2):
+                    x_copy(p, i).start()
 
             @pl.when((x == 1) & (i < items - n))
             def _():
-                mem_copy(i).start()
+                for which in range(2):
+                    mem_copy(which, i).start()
 
             nff[i] = normed.astype(BF16)
             stats[i] = jnp.where(stat_lane == heads + 1, inv, stats[i])
@@ -426,21 +456,29 @@
     lax.fori_loop(0, items + 1, forward_tick, 0)
 
     def forward_drain(i, carry):
-        kv_copy(0, i).wait_send()
-        kv_copy(1, i).wait_send()
         route_sent(OUT_FF, i)
 
         @pl.when(x == 0)
         def _():
-            x_copy(i).wait_send()
+            for p in range(2):
+                x_copy(p, i).wait_send()
+
+        @pl.when(x == 1)
+        def _():
+            for p in range(2):
+                pass_copy(p, i).wait_send()
 
         @pl.when((x == 1) & (i < items - n))
         def _():
-            mem_copy(i).wait_send()
+            for which in range(2):
+                mem_copy(which, i).wait_send()
 
         return carry
 
     lax.fori_loop(0, items, forward_drain, 0)
+    route_sent(S_GLO, items - 1)
+    route_sent(S_GHI, items - 1)
+    gp_copy(items - 1).wait()
     acc[...] = jnp.zeros_like(acc)
 
     def norm_back(s, i, normed_ref):
@@ -596,7 +634,7 @@
             mg_copy(i).wait_send()
 
         for kind in range(KINDS):
-            if kind != OUT_FF:
+            if kind not in (OUT_FF, S_GLO, S_GHI):
                 route_sent(kind, i)
             route_received(kind, i)
         return carry
@@ -620,7 +658,7 @@
     vmem_spec = pl.BlockSpec(memory_space=pltpu.VMEM)
     dma = pltpu.SemaphoreType.DMA
     item_rows = pltpu.VMEM((items, rows, width), BF16)
-    one = dma((items,))
+    one, two = dma((items,)), dma((2, items))
     return pl.pallas_call(
         partial(layers_kernel, n, nseg, heads),
         out_shape=(
@@ -641,6 +679,7 @@
             pltpu.VMEM((2, 2, width), F32),
             item_rows,
             item_rows,
+            item_rows,
             pltpu.VMEM((items, 2, rows, 2 * width), BF16),
             item_rows,
             item_rows,
@@ -648,13 +687,14 @@
             item_rows,
             item_rows,
             item_rows,
-            pltpu.VMEM((items, rows, 2 * hidden_half), BF16),
+            pltpu.VMEM((rows, 2 * hidden_half), BF16),
+            pltpu.VMEM((rows, 2 * hidden_half), BF16),
             pltpu.VMEM((items, rows, 2 * hidden_half), BF16),
             pltpu.VMEM((items, rows, 128), F32),
             pltpu.VMEM((items, toks, 128), F32),
             pltpu.VMEM((items, 1, 2 * toks), F32),
             pltpu.VMEM((items, MEM_PAD, 128), F32),
-            pltpu.VMEM((items, MEM_PAD, width), BF16),
+            pltpu.VMEM((2, items, MEM_PAD, width), BF16),
             pltpu.VMEM((items, MEM_PAD, width), BF16),
             pltpu.VMEM((2, quads, rows, 2 * quad), BF16),
             pltpu.VMEM((2, quads, rows, 2 * quad), BF16),
@@ -663,9 +703,11 @@
             pltpu.VMEM((2, 2, width), F32),
             pltpu.VMEM((2, width), F32),
             dma((4,)), dma((5,)), dma((5,)),
-            one, one,
-            dma((2, items)), dma((2, items)),
-            one, one, one, one, one, one, one, one,
+            two, one, one,
+            two, two,
+            two, two,
+            two, two,
+            one, one, one, one,
             dma((quads, items)), dma((quads, items)),
             dma(()), dma(()),
         ]
@@ -681,7 +723,7 @@
     sx1, sx2, sr, sg, sd, norm_part,
     first_out, down_out, norm_out,
     x1, x2, rr, gg, dd, work, done, got_u, got_uz, got_vz, got_vy, stage, norms,
-    in_sem, out_sem, u_s, u_r, uz_s, uz_r, vz_s, vz_r, vy_s, vy_r, vg_s, vg_r,
+    right_sem, left_sem, out_sem, u_s, u_r, uz_s, uz_r, vz_s, vz_r, vy_s, vy_r, vg_s, vg_r,
     uzg_s, uzg_r, vzg_s, vzg_r, ug_s, ug_r, n_s, n_r,
 ):
     lines = 4
@@ -710,17 +752,32 @@
     for step in range(1, dp):
         pl.semaphore_signal(barrier, inc=1, device_id=other(step), device_id_type=MESH)
 
-    loads = [
-        (sd, dd),
-        (sg.at[:, 0:width], gg.at[:, 0:width]),
-        (sg.at[:, width:], gg.at[:, width:]),
-        (sx2, x2),
-        (sr.at[:, 3 * width :], rr.at[:, 3 * width :]),
-        (sx1, x1),
-        (sr.at[:, 0 : 3 * width], rr.at[:, 0 : 3 * width]),
+    lane_groups = width // lane_group
+    right_loads = [(sd, dd)] + [
+        (sr.at[:, b * width : (b + 1) * width], rr.at[:, b * width : (b + 1) * width])
+        for b in range(4)
     ]
-    for k, (src, dst) in enumerate(loads):
-        pltpu.make_async_copy(src, dst, in_sem.at[k]).start()
+
+    def right_load(k):
+        src, dst = right_loads[k]
+        return pltpu.make_async_copy(src, dst, right_sem.at[k])
+
+    def left_load(which, group):
+        src, dst, low = ((sg, gg, 0), (sg, gg, width), (sx2, x2, 0), (sx1, x1, 0))[which]
+        cols = pl.ds(pl.multiple_of(low + group * lane_group, lane_group), lane_group)
+        return pltpu.make_async_copy(src.at[:, cols], dst.at[:, cols], left_sem.at[which, group])
+
+    right_load(0).start()
+    left_load(0, 0).start()
+    left_load(1, 0).start()
+    left_load(2, 0).start()
+    right_load(4).start()
+    left_load(3, 0).start()
+    for k in range(1, 4):
+        right_load(k).start()
+    for group in range(1, lane_groups):
+        for which in range(4):
+            left_load(which, group).start()
 
     norms[d] = norm_part[...]
     pl.semaphore_wait(barrier, dp - 1)
@@ -811,10 +868,6 @@
     def plus(a, b):
         return (a.astype(F32) + b.astype(F32)).astype(BF16)
 
-    def wait_load(k):
-        src, dst = loads[k]
-        pltpu.make_async_copy(src, dst, in_sem.at[k]).wait()
-
     def ready(k, low=0):
         return (k >= low) & (k < chunks)
 
@@ -832,21 +885,17 @@
 
             @pl.when(r == 0)
             def _():
-                wait_load(0)
-                wait_load(1)
-
+                right_load(0).wait()
+
+            left_load(0, group).wait()
             store_chunks(group, 4, dot(gg[:, cols], dd[...], 0, 0).astype(BF16))
+            left_load(1, group).wait()
+            store_chunks(group, 5, dot(gg[:, gcols], dd[...], 0, 0).astype(BF16))
+            left_load(2, group).wait()
 
             @pl.when(r == 0)
             def _():
-                wait_load(2)
-
-            store_chunks(group, 5, dot(gg[:, gcols], dd[...], 0, 0).astype(BF16))
-
-            @pl.when(r == 0)
-            def _():
-                wait_load(3)
-                wait_load(4)
+                right_load(4).wait()
 
             store_chunks(group, 3, dot(x2[:, cols], rr[:, 3 * width :], 0, 0).astype(BF16))
 
@@ -874,12 +923,13 @@
         def _():
             cols = pl.ds(pl.multiple_of(group * lane_group, lane_group), lane_group)
 
-            @pl.when(r == 0)
-            def _():
-                wait_load(5)
-                wait_load(6)
-
+            left_load(3, group).wait()
             for b in range(3):
+
+                @pl.when(r == 0)
+                def _():
+                    right_load(1 + b).wait()
+
                 store_chunks(
                     group, b,
                     dot(x1[:, cols], rr[:, b * width : (b + 1) * width], 0, 0).astype(BF16),
@@ -1060,7 +1110,8 @@
             pltpu.VMEM((chunks, 3, part // 2, half), BF16),
             pltpu.VMEM((2, 6, part, width), F32),
             pltpu.VMEM((dp, 2, width), F32),
-            dma((7,)),
+            dma((5,)),
+            dma((4, width // 128)),
             dma((2, 6)),
             one, one,
             two, two,

time: 362 us -> 359 us (level)
  no operation moved by 1% of the time
where the time goes in v4:
time: 359 us
  Pallas kernels  344 us (96%)
  local copies, waits for them, and re-layouts  14.7 us (4%)
    pallas_call x1, Pallas kernels, run_layers(): pl.pallas_call(partial(layers_kernel, n, nseg, heads), out_shape=(jax.Sha...  197 us
    pallas_call x1, Pallas kernels, sum_weights(): pl.pallas_call(partial(reduce_kernel, chunks), out_shape=(jax.ShapeDtypeS...  147 us
    unnamed x15, local copies, waits for them, and re-layouts  13.3 us

profile of v4, /device:TPU:0, one launch (start us, length us, event | category | flops | bytes accessed | tf_op | source)
XLA Modules:
  0.0 359.0 jit_solution(13399125722632569525)
XLA Ops:
  0.6 1.3 copy.14.resets
  1.9 196.9 %shard_map.127 = (bf16[2,1024,768]{2,1,0:T(8,128)(2,1)}, bf16[2,1024,768]{2,1,0:T(8,128)(2,1)}, bf16[8,272,768]{2,1,0:T(8,128)(2,1)}, bf16[8,272,768]{2,1,0:T(8,...) custom-call(bf16[2,1024,768]{2,1,0:T(8,128)(2,1)} %tokens.1, ...), custom_call_target="tpu_custom_call" | custom-call | tf_op jit(solution)/shard_map/pallas_call | solution.py:662
  198.8 0.0 copy-start.2
  198.8 146.7 %shard_map.128 = (f32[768,3072]{1,0:T(8,128)}, f32[1536,768]{1,0:T(8,128)}, f32[2,768]{1,0:T(2,128)}) custom-call(bf16[2176,768]{1,0:T(8,128)(2,1)} %bitcast.15, bf16[2176,768]{1,0:T(8,128)(2,1)} %bitcast.16, bf16[2176,3072]{1,0:T(8,128)(2,1)} %bitcast.9, bf16[2176,1536]{1,0:T(8,128)(2,1)} %bitcast.11, bf16[2176,768]{1,0:T(8,128)(2,1)} %bitcast.17, ...), custom_call_target="tpu_custom_call" | custom-call | tf_op jit(solution)/shard_map/pallas_call | solution.py:1090
  345.6 0.0 copy-start.1
  345.6 1.4 fusion
  347.0 0.0 copy-done.2
  347.0 0.0 copy-start
  347.0 1.7 copy.19
  348.7 0.0 copy-done.1
  348.7 0.0 slice-start
  348.7 1.7 copy.20
  350.3 2.7 copy-done
  353.1 0.0 slice-start.1
  353.1 3.7 %copy.21 = f32[1,768,3072]{2,1,0:T(8,128)} copy(f32[1,768,3072]{2,1,0:T(8,128)S(1)} %bitcast.10) | data formatting | bytes 18874368
  356.8 0.0 slice-done
  356.8 0.0 slice-done.1
  356.8 2.2 copy.22
  (1 shorter events, 0.0 us)
Async XLA Ops:
  198.8 148.2 %copy-start.2 = (bf16[2,1024,768]{2,1,0:T(8,128)(2,1)S(1)}, bf16[2,1024,768]{2,1,0:T(8,128)(2,1)}, u32[]{:S(2)}) copy-start(bf16[2,1024,768]{2,1,0:T(8,128)(2,1)} %get-tuple-element.17) | copy-start | bytes 9437188
  345.6 3.1 copy-start.1
  347.0 6.1 %copy-start = (f32[768,3072]{1,0:T(8,128)S(1)}, f32[768,3072]{1,0:T(8,128)}, u32[]{:S(2)}) copy-start(f32[768,3072]{1,0:T(8,128)} %get-tuple-element.25) | copy-start | bytes 28311556
  348.7 8.1 %slice-start = ((s8[4718592]{0:T(1024)(128)(4,1)}), s8[4194304]{0:T(1024)(128)(4,1)S(1)}, s32[]{:S(2)}) async-start(s8[4718592]{0:T(1024)(128)(4,1)} %bitcast.12), calls=%async_computation | async-start | bytes 8388608
  353.1 3.7 %slice-start.1 = ((s8[4718592]{0:T(1024)(128)(4,1)}), s8[524288]{0:T(1024)(128)(4,1)S(1)}, s32[]{:S(2)}) async-start(s8[4718592]{0:T(1024)(128)(4,1)} %bitcast.12), calls=%async_computation.1 | async-start | bytes 1048576

commit v5 on v4

--- a/solution.py
+++ b/solution.py
@@ -53,10 +53,10 @@
 def layers_kernel(
     n, nseg, heads,
     tokens, cotangent, first, down, docs, resets, gain, shift,
-    out, gin, sx1, sx2, sr, sg, sd, norm_grad,
+    out, gin, sx1, sx2, sr, sg, sd, norm_grad, ptok, pmem,
     wf, wd, nrm, x0, xo, q, kv, ctx, natt, yatt, nff, yd, gy, g, gpb, gp, stats, qdoc, kdoc, keep,
-    memin, mgin, dkvs, dkvin, dhb, dctx, acc, accp,
-    wl, ws, wr, tok_sem, cot_sem, gp_sem, fs_sem, fr_sem, xs_sem, xr_sem,
+    memin, mgin, dkvs, dkvin, dhb, dctx, ctxb, dqb, gab, acc, accp, tprob, mprob,
+    wl, ws, wr, tok_sem, cot_sem, gp_sem, pw_sem, pr_sem, fs_sem, fr_sem, xs_sem, xr_sem,
     ms_sem, mr_sem, gs_sem, gr_sem, hs_sem, hr_sem, ds_sem, dr_sem, as_sem, ar_sem,
     lsem, ssem, rsem,
 ):
@@ -181,13 +181,13 @@
         elif kind == GIN_ATT:
             src, dst = yd.at[i, 0:toks, :], token_rows(gin, i)
         elif kind == GIN_FF:
-            src, dst, sec = gy.at[i, 0:toks, :], token_rows(gin, i), 1
+            src, dst, sec = gab.at[0:toks, :], token_rows(gin, i), 1
         elif kind == S_X0:
             src, dst = x0.at[i], sx1.at[block]
         elif kind == S_CTX:
             src, dst = ctx.at[i], sx2.at[block]
         elif kind == S_DQ:
-            src, dst = q.at[i], sr.at[block, :, 0:width]
+            src, dst = dqb, sr.at[block, :, 0:width]
         elif kind == S_DKV:
             src, dst = kv.at[i, c], sr.at[block, :, width:wide]
         elif kind == S_DATT:
@@ -246,6 +246,17 @@
     def gp_copy(i):
         return pltpu.make_async_copy(gpb, gp.at[i], gp_sem.at[i])
 
+    def prob_copies(i, back):
+        pairs = ((tprob, ptok.at[i]), (mprob, pmem.at[i]))
+        if back:
+            return [
+                pltpu.make_async_copy(dst, src, pr_sem.at[e, i])
+                for e, (src, dst) in enumerate(pairs)
+            ]
+        return [
+            pltpu.make_async_copy(src, dst, pw_sem.at[e, i]) for e, (src, dst) in enumerate(pairs)
+        ]
+
     cut = rows // 32 * 16
 
     def piece(p):
@@ -319,28 +330,31 @@
             tok_k, mem_k = token_and_memory(i, j * quad)
             s = head_rows(dot(stacked(q4), tok_k, 1, 1))
             sm = memory_scores(q4, mem_k)
-            peaks, totals, probs = [], [], []
+            own = [mem_lanes == h for h in range(4)]
+            s = [only_same_document(s[h], i) for h in range(4)]
+            peaks = [
+                jnp.max(
+                    jnp.concatenate([s[h], jnp.where(own[h], sm, ABSENT_SCORE)], axis=1),
+                    axis=1, keepdims=True,
+                )
+                for h in range(4)
+            ]
+            pm = jnp.exp(sm - spread(peaks, mem_lanes))
+            mprob[j] = pm.astype(BF16)
+            totals, probs = [], []
             for h in range(4):
-                sh = only_same_document(s[h], i)
-                own_mem = jnp.where(mem_lanes == h, sm, ABSENT_SCORE)
-                peak = jnp.maximum(
-                    jnp.max(sh, axis=1, keepdims=True), jnp.max(own_mem, axis=1, keepdims=True)
-                )
-                p = jnp.exp(sh - peak)
-                peaks.append(peak)
-                totals.append(jnp.sum(p, axis=1, keepdims=True))
+                p = jnp.exp(s[h] - peaks[h])
                 probs.append(p.astype(BF16))
-            pm = jnp.exp(sm - spread(peaks, mem_lanes))
-            for h in range(4):
-                totals[h] += jnp.sum(jnp.where(mem_lanes == h, pm, 0.0), axis=1, keepdims=True)
-                lse = peaks[h] + jnp.log(totals[h])
-                st = jnp.where(stat_lane == 4 * j + h, lse, st)
+                tprob[j, h * rows : (h + 1) * rows, :] = probs[h]
+                both = jnp.concatenate([p, jnp.where(own[h], pm, 0.0)], axis=1)
+                totals.append(1.0 / jnp.sum(both, axis=1, keepdims=True))
+                st = jnp.where(stat_lane == 4 * j + h, totals[h], st)
             tok_v, mem_v = token_and_memory(i, width + j * quad)
             o = spread(head_rows(dot(jnp.concatenate(probs, axis=0), tok_v)), head_lanes)
             o = o + dot(pm.astype(BF16), mem_v)
-            inverse = spread([1.0 / total for total in totals], head_lanes)
-            ctx[i, :, cols] = (o * inverse).astype(BF16)
+            ctxb[:, cols] = (o * spread(totals, head_lanes)).astype(BF16)
         stats[i] = st
+        ctx[i] = ctxb[...]
 
     def forward_tick(t, carry):
         i = t - x
@@ -387,7 +401,14 @@
                     pass_copy(p, i).wait_recv()
 
             kv[i, 1 - c] = dot(xo[i], wf[0, :, width:wide]).astype(BF16)
+            @pl.when(i > 0)
+            def _():
+                for copy in prob_copies(i - 1, False):
+                    copy.wait()
+
             attend(i)
+            for copy in prob_copies(i, False):
+                copy.start()
             route(S_X0, i)
             route(S_CTX, i)
 
@@ -396,7 +417,7 @@
                 wait_first_of(0, (2,))
                 weight_remote(4).wait_recv()
 
-            normed, inv = normalize(dot(ctx[i], wf[0, :, wide:]) + x0[i].astype(F32))
+            normed, inv = normalize(dot(ctxb[...], wf[0, :, wide:]) + x0[i].astype(F32))
             natt[i] = normed.astype(BF16)
             stats[i] = jnp.where(stat_lane == heads, inv, stats[i])
             yatt[i] = (normed * nrm[0, 0:1, :] + nrm[0, 1:2, :]).astype(BF16)
@@ -455,7 +476,7 @@
 
     lax.fori_loop(0, items + 1, forward_tick, 0)
 
-    def forward_drain(i, carry):
+    def forward_sent(i):
         route_sent(OUT_FF, i)
 
         @pl.when(x == 0)
@@ -473,16 +494,15 @@
             for which in range(2):
                 mem_copy(which, i).wait_send()
 
-        return carry
-
-    lax.fori_loop(0, items, forward_drain, 0)
-    route_sent(S_GLO, items - 1)
-    route_sent(S_GHI, items - 1)
+    for copy in prob_copies(items - 1, False):
+        copy.wait()
+    for copy in prob_copies(items - n, True):
+        copy.start()
     gp_copy(items - 1).wait()
     acc[...] = jnp.zeros_like(acc)
 
     def norm_back(s, i, normed_ref):
-        grad = gy[i].astype(F32)
+        grad = (gy[i] if s else gab[...]).astype(F32)
         normed = normed_ref[i].astype(F32)
         inv = stats[i][:, heads + s : heads + s + 1]
         acc[s, 0:1, :] += jnp.sum(grad * normed, axis=0, keepdims=True)
@@ -501,31 +521,33 @@
             c4 = dctx[:, cols]
             tok_k, mem_k = token_and_memory(i, j * quad)
             tok_v, mem_v = token_and_memory(i, width + j * quad)
+            inverse = [stats[i][:, 4 * j + h : 4 * j + h + 1] for h in range(4)]
+            c4 = (c4.astype(F32) * spread(inverse, head_lanes)).astype(BF16)
             products = c4.astype(F32) * ctx[i, :, cols].astype(F32)
-            qs, cs = stacked(q4), stacked(c4)
-            s = head_rows(dot(qs, tok_k, 1, 1))
-            dp = head_rows(dot(cs, tok_v, 1, 1))
-            sm = memory_scores(q4, mem_k)
+            dp = head_rows(dot(stacked(c4), tok_v, 1, 1))
             dpm = dot(c4, mem_v, 1, 1)
-            lse = [stats[i][:, 4 * j + h : 4 * j + h + 1] for h in range(4)]
             inner = [
                 jnp.sum(jnp.where(head_lanes == h, products, 0.0), axis=1, keepdims=True)
                 for h in range(4)
             ]
-            probs, dscores = [], []
-            for h in range(4):
-                p = jnp.exp(only_same_document(s[h], i) - lse[h])
-                probs.append(p.astype(BF16))
-                dscores.append((p * (dp[h] - inner[h])).astype(BF16))
-            pm = jnp.exp(sm - spread(lse, mem_lanes))
-            dsm = (pm * (dpm - spread(inner, mem_lanes))).astype(BF16)
-            probs = jnp.concatenate(probs, axis=0)
+            dscores = [
+                (tprob[j, h * rows : (h + 1) * rows, :].astype(F32) * (dp[h] - inner[h])).astype(BF16)
+                for h in range(4)
+            ]
+            dsm = (mprob[j].astype(F32) * (dpm - spread(inner, mem_lanes))).astype(BF16)
+            ct, qt = jnp.transpose(c4), jnp.transpose(q4)
+            mine = [slice(h * head_dim, (h + 1) * head_dim) for h in range(4)]
+            dv = [
+                dot(ct[mine[h]], tprob[j, h * rows : (h + 1) * rows, :]).astype(BF16)
+                for h in range(4)
+            ]
+            dk = [dot(qt[mine[h]], dscores[h]).astype(BF16) for h in range(4)]
+            dv = jnp.transpose(jnp.concatenate(dv, axis=0))
+            dk = jnp.transpose(jnp.concatenate(dk, axis=0))
             dscores = jnp.concatenate(dscores, axis=0)
-            dv = dot(probs, cs, 0, 0)
-            dk = dot(dscores, qs, 0, 0)
             dq = spread(head_rows(dot(dscores, tok_k)), head_lanes) + dot(dsm, mem_k)
-            q[i, :, cols] = (dq * scale).astype(BF16)
-            dvm = jnp.where(diagonal, dot(pm.astype(BF16), c4, 0, 0), 0.0)
+            dqb[:, cols] = (dq * scale).astype(BF16)
+            dvm = jnp.where(diagonal, dot(mprob[j], c4, 0, 0), 0.0)
             dkm = jnp.where(diagonal, dot(dsm, q4, 0, 0), 0.0)
             dvm = sum(dvm[h * mem_keys : (h + 1) * mem_keys] for h in range(4))
             dkm = sum(dkm[h * mem_keys : (h + 1) * mem_keys] for h in range(4))
@@ -552,12 +574,15 @@
             wf[0, :, 2 * width + low : 2 * width + high], 1, 1,
         )
 
+    def item_of(r):
+        return (nseg - 1 - lax.div(r, n)) * n + lax.rem(r, n)
+
     def backward_tick(t, carry):
         r = t - (1 - x)
 
         @pl.when((r >= 0) & (r < items))
         def _():
-            i = (nseg - 1 - lax.div(r, n)) * n + lax.rem(r, n)
+            i = item_of(r)
             slot = lax.rem(r, 2)
 
             @pl.when(x == 1)
@@ -579,12 +604,17 @@
             def _():
                 gy_copy(i).wait_recv()
 
+            @pl.when(r > 0)
+            def _():
+                route_sent(S_DQ, item_of(r - 1))
+                route_sent(GIN_FF, item_of(r - 1))
+
             norm_back(1, i, nff)
             for part in range(2):
                 cols = slice(part * hidden_half, (part + 1) * hidden_half)
                 dg = dot(nff[i], wd[part], 1, 1)
                 gp[i, :, cols] = (dg * gp[i, :, cols].astype(F32)).astype(BF16)
-            gy[i] = (dot(gp[i], wf[1], 1, 1) + dhb[...]).astype(BF16)
+            gab[...] = (dot(gp[i], wf[1], 1, 1) + dhb[...]).astype(BF16)
             norm_back(0, i, natt)
             dctx[...] = dot(natt[i], wf[0, :, wide:], 1, 1).astype(BF16)
             route(S_DFF0, i)
@@ -592,15 +622,26 @@
             route(S_DU, i)
             route(GIN_FF, i)
             route(S_DATT, i)
+            for copy in prob_copies(i, True):
+                copy.wait()
             attend_back(i, slot)
+            route(S_DQ, i)
+
+            @pl.when(r + 1 < items)
+            def _():
+                for copy in prob_copies(item_of(r + 1), True):
+                    copy.start()
+
             for j in range(quads - 1):
                 gather_dkv(j, i, slot)
             early = (quads - 1) * quad
-            partial_sum = dot(q[i], wf[0, :, 0:width], 1, 1) + dhb[...]
+            partial_sum = dot(dqb[...], wf[0, :, 0:width], 1, 1) + dhb[...]
             if early:
                 partial_sum = partial_sum + dkv_back(i, 0, early)
             dhb[...] = partial_sum
             gather_dkv(quads - 1, i, slot)
+            route(S_DKV, i)
+            forward_sent(i)
             yd[i] = (dkv_back(i, early, width) + dhb[...]).astype(BF16)
 
             @pl.when(x == 1)
@@ -611,8 +652,6 @@
             def _():
                 mg_copy(i).start()
 
-            route(S_DQ, i)
-            route(S_DKV, i)
             route(GIN_ATT, i)
             for j in range(quads):
                 dkv_copy(j, i, slot).wait_send()
@@ -634,12 +673,16 @@
             mg_copy(i).wait_send()
 
         for kind in range(KINDS):
-            if kind not in (OUT_FF, S_GLO, S_GHI):
+            if kind not in (OUT_FF, S_GLO, S_GHI, S_DQ, GIN_FF):
                 route_sent(kind, i)
             route_received(kind, i)
         return carry
 
     lax.fori_loop(0, items, backward_drain, 0)
+    route_sent(S_GLO, items - 1)
+    route_sent(S_GHI, items - 1)
+    route_sent(S_DQ, item_of(items - 1))
+    route_sent(GIN_FF, item_of(items - 1))
     for k in range(5):
         weight_remote(k).wait_send()
     acc_copy.wait()
@@ -670,9 +713,11 @@
             jax.ShapeDtypeStruct((2 * items, rows, hidden_half), BF16),
             jax.ShapeDtypeStruct((2 * items, rows, width), BF16),
             jax.ShapeDtypeStruct((2, width), F32),
+            jax.ShapeDtypeStruct((items, quads, 4 * rows, 2 * toks), BF16),
+            jax.ShapeDtypeStruct((items, quads, rows, 8 * MEM_PAD), BF16),
         ),
         in_specs=[any_spec] * 4 + [vmem_spec] * 4,
-        out_specs=[any_spec] * 7 + [vmem_spec],
+        out_specs=[any_spec] * 7 + [vmem_spec] + [any_spec] * 2,
         scratch_shapes=[
             pltpu.VMEM((2, width, 4 * width), BF16),
             pltpu.VMEM((2, hidden_half, width), BF16),
@@ -700,10 +745,15 @@
             pltpu.VMEM((2, quads, rows, 2 * quad), BF16),
             pltpu.VMEM((rows, width), F32),
             pltpu.VMEM((rows, width), BF16),
+            pltpu.VMEM((rows, width), BF16),
+            pltpu.VMEM((rows, width), BF16),
+            pltpu.VMEM((rows, width), BF16),
             pltpu.VMEM((2, 2, width), F32),
             pltpu.VMEM((2, width), F32),
+            pltpu.VMEM((quads, 4 * rows, 2 * toks), BF16),
+            pltpu.VMEM((quads, rows, 8 * MEM_PAD), BF16),
             dma((4,)), dma((5,)), dma((5,)),
-            two, one, one,
+            two, one, one, two, two,
             two, two,
             two, two,
             two, two,
@@ -1135,7 +1185,7 @@
     n, length, width = tokens.shape
     items = n * NSEG
     rows = length // NSEG // 2 + MEM_PAD
-    out, gin, sx1, sx2, sr, sg, sd, norm_grad = run_layers(
+    out, gin, sx1, sx2, sr, sg, sd, norm_grad, _, _ = run_layers(
         n, NSEG, H, tokens, cotangent, first_weights, down_halves,
         doc_ids, reset_flags, norm_gain, norm_bias,
     )

time: 359 us -> 350 us (0.975)
  Pallas kernels: 344 us -> 335 us
    pallas_call x1, Pallas kernels: 197 us -> 188 us  [run_layers(): pl.pallas_call(partial(layers_kernel, n, nseg, heads), out_shape=(jax.Sha...]
where the time goes in v5:
time: 350 us
  Pallas kernels  335 us (96%)
  local copies, waits for them, and re-layouts  14.7 us (4%)
    pallas_call x1, Pallas kernels, run_layers(): pl.pallas_call(partial(layers_kernel, n, nseg, heads), out_shape=(jax.Sha...  188 us
    pallas_call x1, Pallas kernels, sum_weights(): pl.pallas_call(partial(reduce_kernel, chunks), out_shape=(jax.ShapeDtypeS...  147 us
    unnamed x15, local copies, waits for them, and re-layouts  13.3 us

profile of v5, /device:TPU:0, one launch (start us, length us, event | category | flops | bytes accessed | tf_op | source)
XLA Modules:
  0.0 350.2 jit_solution(9156752787028064586)
XLA Ops:
  0.6 1.3 copy.14.resets
  1.9 188.0 %shard_map.127 = (bf16[2,1024,768]{2,1,0:T(8,128)(2,1)}, bf16[2,1024,768]{2,1,0:T(8,128)(2,1)}, bf16[8,272,768]{2,1,0:T(8,128)(2,1)}, bf16[8,272,768]{2,1,0:T(8,...) custom-call(bf16[2,1024,768]{2,1,0:T(8,128)(2,1)} %tokens.1, ...), custom_call_target="tpu_custom_call" | custom-call | tf_op jit(solution)/shard_map/pallas_call | solution.py:705
  190.0 0.0 copy-start.2
  190.0 146.7 %shard_map.128 = (f32[768,3072]{1,0:T(8,128)}, f32[1536,768]{1,0:T(8,128)}, f32[2,768]{1,0:T(2,128)}) custom-call(bf16[2176,768]{1,0:T(8,128)(2,1)} %bitcast.15, bf16[2176,768]{1,0:T(8,128)(2,1)} %bitcast.16, bf16[2176,3072]{1,0:T(8,128)(2,1)} %bitcast.9, bf16[2176,1536]{1,0:T(8,128)(2,1)} %bitcast.11, bf16[2176,768]{1,0:T(8,128)(2,1)} %bitcast.17, ...), custom_call_target="tpu_custom_call" | custom-call | tf_op jit(solution)/shard_map/pallas_call | solution.py:1140
  336.7 0.0 copy-start.1
  336.7 1.4 fusion
  338.2 0.0 copy-done.2
  338.2 0.0 copy-start
  338.2 1.7 copy.19
  339.8 0.0 copy-done.1
  339.8 0.0 slice-start
  339.8 1.7 copy.20
  341.5 2.7 copy-done
  344.2 0.0 slice-start.1
  344.2 3.7 %copy.21 = f32[1,768,3072]{2,1,0:T(8,128)} copy(f32[1,768,3072]{2,1,0:T(8,128)S(1)} %bitcast.10) | data formatting | bytes 18874368
  348.0 0.0 slice-done
  348.0 0.0 slice-done.1
  348.0 2.2 copy.22
  (1 shorter events, 0.0 us)
Async XLA Ops:
  190.0 148.2 %copy-start.2 = (bf16[2,1024,768]{2,1,0:T(8,128)(2,1)S(1)}, bf16[2,1024,768]{2,1,0:T(8,128)(2,1)}, u32[]{:S(2)}) copy-start(bf16[2,1024,768]{2,1,0:T(8,128)(2,1)} %get-tuple-element.17) | copy-start | bytes 9437188
  336.7 3.1 copy-start.1
  338.2 6.1 %copy-start = (f32[768,3072]{1,0:T(8,128)S(1)}, f32[768,3072]{1,0:T(8,128)}, u32[]{:S(2)}) copy-start(f32[768,3072]{1,0:T(8,128)} %get-tuple-element.25) | copy-start | bytes 28311556
  339.8 8.1 %slice-start = ((s8[4718592]{0:T(1024)(128)(4,1)}), s8[4194304]{0:T(1024)(128)(4,1)S(1)}, s32[]{:S(2)}) async-start(s8[4718592]{0:T(1024)(128)(4,1)} %bitcast.12), calls=%async_computation | async-start | bytes 8388608
  344.2 3.7 %slice-start.1 = ((s8[4718592]{0:T(1024)(128)(4,1)}), s8[524288]{0:T(1024)(128)(4,1)S(1)}, s32[]{:S(2)}) async-start(s8[4718592]{0:T(1024)(128)(4,1)} %bitcast.12), calls=%async_computation.1 | async-start | bytes 1048576

commit v6 on v5

--- a/solution.py
+++ b/solution.py
@@ -55,7 +55,7 @@
     tokens, cotangent, first, down, docs, resets, gain, shift,
     out, gin, sx1, sx2, sr, sg, sd, norm_grad, ptok, pmem,
     wf, wd, nrm, x0, xo, q, kv, ctx, natt, yatt, nff, yd, gy, g, gpb, gp, stats, qdoc, kdoc, keep,
-    memin, mgin, dkvs, dkvin, dhb, dctx, ctxb, dqb, gab, acc, accp, tprob, mprob,
+    memin, mgin, dkvs, dkvin, dhb, ctxb, acc, accp, tprob, mprob,
     wl, ws, wr, tok_sem, cot_sem, gp_sem, pw_sem, pr_sem, fs_sem, fr_sem, xs_sem, xr_sem,
     ms_sem, mr_sem, gs_sem, gr_sem, hs_sem, hr_sem, ds_sem, dr_sem, as_sem, ar_sem,
     lsem, ssem, rsem,
@@ -77,6 +77,9 @@
     quads = heads // 4
     mem_keys = 2 * MEM_PAD
     scale = head_dim ** (-0.5)
+    dqb = gpb.at[:, 0:width]
+    gab = gpb.at[:, width : 2 * width]
+    dctx = gpb.at[:, 2 * width : wide]
 
     def remote(src, dst, send, recv, peer):
         return pltpu.make_async_remote_copy(
@@ -323,15 +326,20 @@
         return jnp.where(mem_valid, dot(q4, mem_k, 1, 1), ABSENT_SCORE)
 
     def attend(i):
+        own = [mem_lanes == h for h in range(4)]
+
+        def scores(j):
+            q4 = q[i, :, j * quad : (j + 1) * quad]
+            tok_k, mem_k = token_and_memory(i, j * quad)
+            return dot(stacked(q4), tok_k, 1, 1), memory_scores(q4, mem_k)
+
         st = jnp.zeros((rows, 128), F32)
+        following = scores(0)
         for j in range(quads):
-            cols = slice(j * quad, (j + 1) * quad)
-            q4 = q[i, :, cols]
-            tok_k, mem_k = token_and_memory(i, j * quad)
-            s = head_rows(dot(stacked(q4), tok_k, 1, 1))
-            sm = memory_scores(q4, mem_k)
-            own = [mem_lanes == h for h in range(4)]
-            s = [only_same_document(s[h], i) for h in range(4)]
+            s, sm = following
+            if j + 1 < quads:
+                following = scores(j + 1)
+            s = [only_same_document(part, i) for part in head_rows(s)]
             peaks = [
                 jnp.max(
                     jnp.concatenate([s[h], jnp.where(own[h], sm, ABSENT_SCORE)], axis=1),
@@ -352,7 +360,7 @@
             tok_v, mem_v = token_and_memory(i, width + j * quad)
             o = spread(head_rows(dot(jnp.concatenate(probs, axis=0), tok_v)), head_lanes)
             o = o + dot(pm.astype(BF16), mem_v)
-            ctxb[:, cols] = (o * spread(totals, head_lanes)).astype(BF16)
+            ctxb[:, j * quad : (j + 1) * quad] = (o * spread(totals, head_lanes)).astype(BF16)
         stats[i] = st
         ctx[i] = ctxb[...]
 
@@ -515,17 +523,23 @@
         normed_ref[i] = dh.astype(BF16)
 
     def attend_back(i, slot):
+        def prob_grads(j):
+            inverse = [stats[i][:, 4 * j + h : 4 * j + h + 1] for h in range(4)]
+            c4 = dctx[:, j * quad : (j + 1) * quad].astype(F32) * spread(inverse, head_lanes)
+            c4 = c4.astype(BF16)
+            tok_v, mem_v = token_and_memory(i, width + j * quad)
+            return c4, dot(stacked(c4), tok_v, 1, 1), dot(c4, mem_v, 1, 1)
+
+        following = prob_grads(0)
         for j in range(quads):
+            c4, dp, dpm = following
+            if j + 1 < quads:
+                following = prob_grads(j + 1)
             cols = slice(j * quad, (j + 1) * quad)
             q4 = q[i, :, cols]
-            c4 = dctx[:, cols]
             tok_k, mem_k = token_and_memory(i, j * quad)
-            tok_v, mem_v = token_and_memory(i, width + j * quad)
-            inverse = [stats[i][:, 4 * j + h : 4 * j + h + 1] for h in range(4)]
-            c4 = (c4.astype(F32) * spread(inverse, head_lanes)).astype(BF16)
             products = c4.astype(F32) * ctx[i, :, cols].astype(F32)
-            dp = head_rows(dot(stacked(c4), tok_v, 1, 1))
-            dpm = dot(c4, mem_v, 1, 1)
+            dp = head_rows(dp)
             inner = [
                 jnp.sum(jnp.where(head_lanes == h, products, 0.0), axis=1, keepdims=True)
                 for h in range(4)
@@ -745,9 +759,6 @@
             pltpu.VMEM((2, quads, rows, 2 * quad), BF16),
             pltpu.VMEM((rows, width), F32),
             pltpu.VMEM((rows, width), BF16),
-            pltpu.VMEM((rows, width), BF16),
-            pltpu.VMEM((rows, width), BF16),
-            pltpu.VMEM((rows, width), BF16),
             pltpu.VMEM((2, 2, width), F32),
             pltpu.VMEM((2, width), F32),
             pltpu.VMEM((quads, 4 * rows, 2 * toks), BF16),
@@ -771,8 +782,8 @@
 def reduce_kernel(
     chunks,
     sx1, sx2, sr, sg, sd, norm_part,
-    first_out, down_out, norm_out,
-    x1, x2, rr, gg, dd, work, done, got_u, got_uz, got_vz, got_vy, stage, norms,
+    sums, norm_out,
+    x1, x2, rr, gg, dd, work, done, got_u, got_uz, got_vz, got_vy, norms,
     right_sem, left_sem, out_sem, u_s, u_r, uz_s, uz_r, vz_s, vz_r, vy_s, vy_r, vg_s, vg_r,
     uzg_s, uzg_r, vzg_s, vzg_r, ug_s, ug_r, n_s, n_r,
 ):
@@ -901,19 +912,8 @@
         spot = done.at[k, 0:3, rows_of(flow), cols]
         return remote(spot, spot, ug_s.at[flow, k], ug_r.at[flow, k], y_peer)
 
-    def out_copies(k, slot):
-        rows = pl.ds(pl.multiple_of(k * part, part), part)
-        copies = []
-        for b in range(6):
-            if b < 4:
-                dst = first_out.at[rows, b * width : (b + 1) * width]
-            else:
-                low = pl.ds(pl.multiple_of((b - 4) * width + k * part, part), part)
-                dst = down_out.at[low, :]
-            copies.append(
-                pltpu.make_async_copy(stage.at[slot, b], dst, out_sem.at[slot, b])
-            )
-        return copies
+    def out_copy(k):
+        return pltpu.make_async_copy(done.at[k], sums.at[k], out_sem.at[k])
 
     def plus(a, b):
         return (a.astype(F32) + b.astype(F32)).astype(BF16)
@@ -925,29 +925,31 @@
         for e in range(per_group):
             work[group * per_group + e, block] = value[e * part : (e + 1) * part]
 
+    def second_half(r):
+        group = lax.div(r + per_group - 1, per_group)
+        cols = pl.ds(pl.multiple_of(group * lane_group, lane_group), lane_group)
+        gcols = pl.ds(pl.multiple_of(width + group * lane_group, lane_group), lane_group)
+
+        @pl.when(r == 0)
+        def _():
+            right_load(0).wait()
+
+        left_load(0, group).wait()
+        store_chunks(group, 4, dot(gg[:, cols], dd[...], 0, 0).astype(BF16))
+        left_load(1, group).wait()
+        store_chunks(group, 5, dot(gg[:, gcols], dd[...], 0, 0).astype(BF16))
+        left_load(2, group).wait()
+
+        @pl.when(r == 0)
+        def _():
+            right_load(4).wait()
+
+        store_chunks(group, 3, dot(x2[:, cols], rr[:, 3 * width :], 0, 0).astype(BF16))
+
     def round_step(r, carry):
-        group = lax.div(r, per_group)
-
-        @pl.when((lax.rem(r, per_group) == 0) & (r < chunks))
-        def _():
-            cols = pl.ds(pl.multiple_of(group * lane_group, lane_group), lane_group)
-            gcols = pl.ds(pl.multiple_of(width + group * lane_group, lane_group), lane_group)
-
-            @pl.when(r == 0)
-            def _():
-                right_load(0).wait()
-
-            left_load(0, group).wait()
-            store_chunks(group, 4, dot(gg[:, cols], dd[...], 0, 0).astype(BF16))
-            left_load(1, group).wait()
-            store_chunks(group, 5, dot(gg[:, gcols], dd[...], 0, 0).astype(BF16))
-            left_load(2, group).wait()
-
-            @pl.when(r == 0)
-            def _():
-                right_load(4).wait()
-
-            store_chunks(group, 3, dot(x2[:, cols], rr[:, 3 * width :], 0, 0).astype(BF16))
+        @pl.when(r == 0)
+        def _():
+            second_half(r)
 
         for flow in range(2):
             p = place(flow)
@@ -971,8 +973,8 @@
 
         @pl.when((lax.rem(r, per_group) == 0) & (r < chunks))
         def _():
+            group = lax.div(r, per_group)
             cols = pl.ds(pl.multiple_of(group * lane_group, lane_group), lane_group)
-
             left_load(3, group).wait()
             for b in range(3):
 
@@ -989,6 +991,10 @@
         def _():
             u_copy(r).start()
 
+        @pl.when((lax.rem(r, per_group) == per_group - 1) & (r + 1 < chunks))
+        def _():
+            second_half(r)
+
         @pl.when(ready(r - 1))
         def _():
             k = r - 1
@@ -1071,20 +1077,9 @@
             def _():
                 ug_copy(flow, k, theirs).wait_recv()
 
-        k = r - 2 * lines
-
-        @pl.when(ready(k))
-        def _():
-            slot = lax.rem(k, 2)
-
-            @pl.when(k >= 2)
-            def _():
-                for copy in out_copies(k - 2, slot):
-                    copy.wait()
-
-            stage[slot] = done[k].astype(F32)
-            for copy in out_copies(k, slot):
-                copy.start()
+        @pl.when(ready(r - 2 * lines))
+        def _():
+            out_copy(r - 2 * lines).start()
 
         return carry
 
@@ -1098,6 +1093,7 @@
     norm_out[...] = total
 
     def drain(k, carry):
+        out_copy(k).wait()
         u_copy(k).wait_send()
         for flow in range(2):
             p = place(flow)
@@ -1121,9 +1117,6 @@
         return carry
 
     lax.fori_loop(0, chunks, drain, 0)
-    for k in (chunks - 2, chunks - 1):
-        for copy in out_copies(k, k % 2):
-            copy.wait()
     for step in range(1, dp):
         norm_copy(step).wait_send()
 
@@ -1140,12 +1133,11 @@
     return pl.pallas_call(
         partial(reduce_kernel, chunks),
         out_shape=(
-            jax.ShapeDtypeStruct((width, 4 * width), F32),
-            jax.ShapeDtypeStruct((2 * width, width), F32),
+            jax.ShapeDtypeStruct((chunks, 6, part, width), BF16),
             jax.ShapeDtypeStruct((2, width), F32),
         ),
         in_specs=[any_spec] * 5 + [vmem_spec],
-        out_specs=[any_spec] * 2 + [vmem_spec],
+        out_specs=[any_spec, vmem_spec],
         scratch_shapes=[
             pltpu.VMEM((total, width), BF16),
             pltpu.VMEM((total, width), BF16),
@@ -1158,11 +1150,10 @@
             pltpu.VMEM((2, chunks, 3, part // 2, half), BF16),
             pltpu.VMEM((2, chunks, 3, part // 2, width), BF16),
             pltpu.VMEM((chunks, 3, part // 2, half), BF16),
-            pltpu.VMEM((2, 6, part, width), F32),
             pltpu.VMEM((dp, 2, width), F32),
             dma((5,)),
             dma((4, width // 128)),
-            dma((2, 6)),
+            one,
             one, one,
             two, two,
             two, two,
@@ -1179,6 +1170,52 @@
     )(sx1, sx2, sr, sg, sd, norm_part)
 
 
+def finish_kernel(sums, out, gin, norms, first_grad, down_grad, out_copy, gin_copy, gain, shift):
+    width = sums.shape[3]
+    for b in range(4):
+        first_grad[:, b * width : (b + 1) * width] = sums[0, b].astype(F32)
+    for b in range(2):
+        down_grad[b] = sums[0, 4 + b].astype(F32)
+    out_copy[...] = out[...]
+    gin_copy[...] = gin[...]
+    gain[...] = norms[0:1]
+    shift[...] = norms[1:2]
+
+
+def finish(sums, out, gin, norms):
+    chunks, _, part, width = sums.shape
+    total = out.shape[0]
+    blocks = 8
+    tokens = pl.BlockSpec((total // blocks, width), lambda k: (jnp.minimum(k, blocks - 1), 0))
+    whole = pl.BlockSpec((1, width), lambda k: (0, 0))
+    return pl.pallas_call(
+        finish_kernel,
+        grid=(chunks,),
+        out_shape=(
+            jax.ShapeDtypeStruct((width, 4 * width), F32),
+            jax.ShapeDtypeStruct((2, width, width), F32),
+            jax.ShapeDtypeStruct(out.shape, BF16),
+            jax.ShapeDtypeStruct(gin.shape, BF16),
+            jax.ShapeDtypeStruct((1, width), F32),
+            jax.ShapeDtypeStruct((1, width), F32),
+        ),
+        in_specs=[
+            pl.BlockSpec((1, 6, part, width), lambda k: (k, 0, 0, 0)),
+            tokens,
+            tokens,
+            pl.BlockSpec((2, width), lambda k: (0, 0)),
+        ],
+        out_specs=[
+            pl.BlockSpec((part, 4 * width), lambda k: (k, 0)),
+            pl.BlockSpec((2, part, width), lambda k: (0, k, 0)),
+            tokens,
+            tokens,
+            whole,
+            whole,
+        ],
+    )(sums, out, gin, norms)
+
+
 def shards(
     tokens, doc_ids, reset_flags, first_weights, down_halves, norm_gain, norm_bias, cotangent
 ):
@@ -1196,7 +1233,12 @@
 
     dp = lax.axis_size("dp")
     if dp == 8:
-        first_grad, down_grad, norm_grad = sum_weights(dp, sx1, sx2, sr, sg, sd, norm_grad)
+        sums, norm_grad = sum_weights(dp, sx1, sx2, sr, sg, sd, norm_grad)
+        first_grad, down_grad, out, gin, gain_grad, shift_grad = finish(
+            sums, out.reshape(-1, width), gin.reshape(-1, width), norm_grad
+        )
+        down_grad = down_grad.reshape(-1, width)
+        out, gin = (a.reshape(n, length, width) for a in (out, gin))
     else:
 
         def weight_grad(left, right):
@@ -1208,13 +1250,14 @@
         down_grad = weight_grad(sg, sd)
         first_grad, down_grad = lax.psum((first_grad, down_grad), "dp")
         norm_grad = lax.psum(norm_grad, "dp")
+        gain_grad, shift_grad = norm_grad[0:1], norm_grad[1:2]
     return (
         out[None],
         gin[None],
         first_grad.astype(F32)[None],
         down_grad.astype(F32)[None],
-        norm_grad[0:1],
-        norm_grad[1:2],
+        gain_grad,
+        shift_grad,
     )
 
 

time: 350 us -> 346 us (0.989)
  local copies, waits for them, and re-layouts: 14.7 us -> 1.3 us
  Pallas kernels: 335 us -> 343 us
    pallas_call x0 -> x1, Pallas kernels: none -> 14.6 us  [finish(): pl.pallas_call(finish_kernel, grid=(chunks,), out_shape=(jax.ShapeDtypeSt...]
    unnamed x15 -> x1, local copies, waits for them, and re-layouts: 13.3 us -> 1.3 us
    pallas_call x1, Pallas kernels: 188 us -> 183 us  [run_layers(): pl.pallas_call(partial(layers_kernel, n, nseg, heads), out_shape=(jax.Sha...]
where the time goes in v6:
time: 346 us; the launch traced here: 345 us
  Pallas kernels  343 us (99%)
    pallas_call x1, Pallas kernels, run_layers(): pl.pallas_call(partial(layers_kernel, n, nseg, heads), out_shape=(jax.Sha...  183 us
    pallas_call x1, Pallas kernels, sum_weights(): pl.pallas_call(partial(reduce_kernel, chunks), out_shape=(jax.ShapeDtypeS...  145 us
    pallas_call x1, Pallas kernels, finish(): pl.pallas_call(finish_kernel, grid=(chunks,), out_shape=(jax.ShapeDtypeSt...  14.6 us

profile of v6, /device:TPU:0, one launch (start us, length us, event | category | flops | bytes accessed | tf_op | source)
XLA Modules:
  0.0 345.4 jit_solution(16798303771307855031)
XLA Ops:
  0.6 1.3 copy.14.resets
  1.9 183.4 %shard_map.127 = (bf16[2,1024,768]{2,1,0:T(8,128)(2,1)}, bf16[2,1024,768]{2,1,0:T(8,128)(2,1)}, bf16[8,272,768]{2,1,0:T(8,128)(2,1)}, bf16[8,272,768]{2,1,0:T(8,...) custom-call(bf16[2,1024,768]{2,1,0:T(8,128)(2,1)} %tokens.1, ...), custom_call_target="tpu_custom_call" | custom-call | tf_op jit(solution)/shard_map/pallas_call | solution.py:719
  185.4 145.4 %shard_map.128 = (bf16[12,6,64,768]{3,2,1,0:T(8,128)(2,1)}, f32[2,768]{1,0:T(2,128)}) custom-call(bf16[2176,768]{1,0:T(8,128)(2,1)} %bitcast.13, bf16[2176,768]{1,0:T(8,128)(2,1)} %bitcast.14, bf16[2176,3072]{1,0:T(8,128)(2,1)} %bitcast.11, bf16[2176,1536]{1,0:T(8,128)(2,1)} %bitcast.12, bf16[2176,768]{1,0:T(8,128)(2,1)} %bitcast.15, ...), custom_call_target="tpu_custom_call" | custom-call | tf_op jit(solution)/shard_map/pallas_call | solution.py:1133
  330.7 14.6 %shard_map.129 = (f32[768,3072]{1,0:T(8,128)}, f32[2,768,768]{2,1,0:T(8,128)}, bf16[2048,768]{1,0:T(8,128)(2,1)}, bf16[2048,768]{1,0:T(8,128)(2,1)}, f32[1,768]{1,0:T(1,128)}, /*index=5*/f32[1,768]{1,0:T(1,128)}) custom-call(bf16[12,6,64,768]{3,2,1,0:T(8,128)(2,1)} %get-tuple-element.28.sums, bf16[2048,768]{1,0:T(8,128)(2,1)} %bitcast.16, ...), custom_call_target="tpu_custom_call" | custom-call | tf_op jit(solution)/shard_map/pallas_call | solution.py:1191

commit v7 on v6

--- a/solution.py
+++ b/solution.py
@@ -55,8 +55,8 @@
     tokens, cotangent, first, down, docs, resets, gain, shift,
     out, gin, sx1, sx2, sr, sg, sd, norm_grad, ptok, pmem,
     wf, wd, nrm, x0, xo, q, kv, ctx, natt, yatt, nff, yd, gy, g, gpb, gp, stats, qdoc, kdoc, keep,
-    memin, mgin, dkvs, dkvin, dhb, ctxb, acc, accp, tprob, mprob,
-    wl, ws, wr, tok_sem, cot_sem, gp_sem, pw_sem, pr_sem, fs_sem, fr_sem, xs_sem, xr_sem,
+    memin, mgin, dkvs, dkvin, dhb, kvb, acc, accp, tprob, mprob,
+    wl, ws, wr, tok_sem, cot_sem, gp_sem, qkv_sem, pw_sem, pr_sem, fs_sem, fr_sem, xs_sem, xr_sem,
     ms_sem, mr_sem, gs_sem, gr_sem, hs_sem, hr_sem, ds_sem, dr_sem, as_sem, ar_sem,
     lsem, ssem, rsem,
 ):
@@ -77,6 +77,8 @@
     quads = heads // 4
     mem_keys = 2 * MEM_PAD
     scale = head_dim ** (-0.5)
+    qb = gpb.at[:, 0:width]
+    ctxb = gpb.at[:, width : 2 * width]
     dqb = gpb.at[:, 0:width]
     gab = gpb.at[:, width : 2 * width]
     dctx = gpb.at[:, 2 * width : wide]
@@ -100,7 +102,7 @@
         if which == 0:
             src, dst = token_rows(tokens, i), x0.at[i, 0:toks, :]
         else:
-            src, dst = token_rows(tokens, i, 1 - c), xo.at[i, 0:toks, :]
+            src, dst = token_rows(tokens, i, 1 - c), xo.at[lax.rem(i, n), 0:toks, :]
         return pltpu.make_async_copy(src, dst, tok_sem.at[which, i])
 
     def cot_copy(i):
@@ -147,7 +149,8 @@
             @pl.when(x == 0)
             def _():
                 token_copy(0, i).start()
-                token_copy(1, i).start()
+                if i < n:
+                    token_copy(1, i).start()
 
         @pl.when(x == 1)
         def _():
@@ -166,12 +169,14 @@
 
     for i in range(items):
         seq, seg = i % n, i // n
-        kdoc[i] = docs[seq : seq + 1, seg * seg_len : (seg + 1) * seg_len].astype(F32)
         own = pl.ds(pl.multiple_of(seg * seg_len + c * toks, toks), toks)
+        others = pl.ds(pl.multiple_of(seg * seg_len + (1 - c) * toks, toks), toks)
         own_row = docs[seq : seq + 1, own].astype(F32)
+        kdoc[i, :, 0:toks] = own_row
+        kdoc[i, :, toks:] = docs[seq : seq + 1, others].astype(F32)
         qdoc[i] = jnp.transpose(jnp.broadcast_to(own_row, (128, toks)))
         if seg > 0:
-            flag = resets[seq : seq + 1, seg - 1 : seg].astype(F32)
+            flag = resets[seg - 1 : seg, seq : seq + 1].astype(F32)
             keep[i] = jnp.broadcast_to(1.0 - flag, (MEM_PAD, 128))
 
     def routed(kind, i):
@@ -192,7 +197,7 @@
         elif kind == S_DQ:
             src, dst = dqb, sr.at[block, :, 0:width]
         elif kind == S_DKV:
-            src, dst = kv.at[i, c], sr.at[block, :, width:wide]
+            src, dst = kv.at[i, 0], sr.at[block, :, width:wide]
         elif kind == S_DATT:
             src, dst = natt.at[i], sr.at[block, :, wide:]
         elif kind == S_GLO:
@@ -246,6 +251,12 @@
         def _():
             route_away(kind, i).wait_recv()
 
+    def qkv_copies(i):
+        return [
+            pltpu.make_async_copy(qb, q.at[i], qkv_sem.at[0, i]),
+            pltpu.make_async_copy(kvb, kv.at[i], qkv_sem.at[1, i]),
+        ]
+
     def gp_copy(i):
         return pltpu.make_async_copy(gpb, gp.at[i], gp_sem.at[i])
 
@@ -272,7 +283,8 @@
 
     def pass_copy(p, i):
         return remote(
-            x0.at[i, piece(p)], xo.at[i, piece(p)], fs_sem.at[p, i], fr_sem.at[p, i], core_peer
+            x0.at[i, piece(p)], xo.at[lax.rem(i, n), piece(p)],
+            fs_sem.at[p, i], fr_sem.at[p, i], core_peer,
         )
 
     def mem_copy(which, i):
@@ -291,7 +303,7 @@
 
     def dkv_copy(j, i, slot):
         return remote(
-            dkvs.at[1 - c, j], dkvin.at[slot, j], ds_sem.at[j, i], dr_sem.at[j, i], core_peer
+            dkvs.at[1, j], dkvin.at[slot, j], ds_sem.at[j, i], dr_sem.at[j, i], core_peer
         )
 
     head_lanes = group_of((rows, quad), 1, head_dim)
@@ -311,10 +323,10 @@
     def head_rows(block):
         return [block[h * rows : (h + 1) * rows] for h in range(4)]
 
-    def token_and_memory(i, low):
+    def token_and_memory(ref, low):
         cols = slice(low, low + quad)
-        tok = jnp.concatenate([kv[i, 0, 0:toks, cols], kv[i, 1, 0:toks, cols]], axis=0)
-        mem = jnp.concatenate([kv[i, 0, toks:, cols], kv[i, 1, toks:, cols]], axis=0)
+        tok = jnp.concatenate([ref[0, 0:toks, cols], ref[1, 0:toks, cols]], axis=0)
+        mem = jnp.concatenate([ref[0, toks:, cols], ref[1, toks:, cols]], axis=0)
         return tok, jnp.where(diagonal, jnp.concatenate([mem] * 4, axis=0), BF16(0))
 
     def only_same_document(s, i):
@@ -329,8 +341,8 @@
         own = [mem_lanes == h for h in range(4)]
 
         def scores(j):
-            q4 = q[i, :, j * quad : (j + 1) * quad]
-            tok_k, mem_k = token_and_memory(i, j * quad)
+            q4 = qb[:, j * quad : (j + 1) * quad]
+            tok_k, mem_k = token_and_memory(kvb, j * quad)
             return dot(stacked(q4), tok_k, 1, 1), memory_scores(q4, mem_k)
 
         st = jnp.zeros((rows, 128), F32)
@@ -357,7 +369,7 @@
                 both = jnp.concatenate([p, jnp.where(own[h], pm, 0.0)], axis=1)
                 totals.append(1.0 / jnp.sum(both, axis=1, keepdims=True))
                 st = jnp.where(stat_lane == 4 * j + h, totals[h], st)
-            tok_v, mem_v = token_and_memory(i, width + j * quad)
+            tok_v, mem_v = token_and_memory(kvb, width + j * quad)
             o = spread(head_rows(dot(jnp.concatenate(probs, axis=0), tok_v)), head_lanes)
             o = o + dot(pm.astype(BF16), mem_v)
             ctxb[:, j * quad : (j + 1) * quad] = (o * spread(totals, head_lanes)).astype(BF16)
@@ -371,17 +383,17 @@
         def _():
             @pl.when(x == 0)
             def _():
-                for which, rows_ref in enumerate((x0, xo)):
+                for which, rows_ref in enumerate((x0.at[i], xo.at[lax.rem(i, n)])):
                     token_copy(which, i).wait()
 
                     @pl.when(i < n)
                     def _():
-                        rows_ref[i, toks:rows, :] = jnp.zeros((MEM_PAD, width), BF16)
+                        rows_ref[toks:rows, :] = jnp.zeros((MEM_PAD, width), BF16)
 
                     @pl.when(i >= n)
                     def _():
                         mem_copy(which, i - n).wait_recv()
-                        rows_ref[i, toks:rows, :] = jnp.where(
+                        rows_ref[toks:rows, :] = jnp.where(
                             keep[i][:, 0:1] > 0.0, memin[which, i - n], jnp.zeros((), BF16)
                         )
 
@@ -395,20 +407,32 @@
             def _():
                 wait_first_of(0, (0,))
 
-            kv[i, c] = dot(x0[i], wf[0, :, width:wide]).astype(BF16)
+            @pl.when(i > 0)
+            def _():
+                qkv_copies(i - 1)[1].wait()
+                gp_copy(i - 1).wait()
+
+            kvb[0] = dot(x0[i], wf[0, :, width:wide]).astype(BF16)
 
             @pl.when(i == 0)
             def _():
                 wait_first_of(0, (1,))
 
-            q[i] = dot(x0[i], wf[0, :, 0:width]).astype(BF16) * BF16(scale)
+            qb[...] = dot(x0[i], wf[0, :, 0:width]).astype(BF16) * BF16(scale)
 
             @pl.when(x == 1)
             def _():
                 for p in range(2):
                     pass_copy(p, i).wait_recv()
 
-            kv[i, 1 - c] = dot(xo[i], wf[0, :, width:wide]).astype(BF16)
+            kvb[1] = dot(xo[lax.rem(i, n)], wf[0, :, width:wide]).astype(BF16)
+            for copy in qkv_copies(i):
+                copy.start()
+
+            @pl.when((x == 0) & (i < items - n))
+            def _():
+                token_copy(1, i + n).start()
+
             @pl.when(i > 0)
             def _():
                 for copy in prob_copies(i - 1, False):
@@ -417,8 +441,6 @@
             attend(i)
             for copy in prob_copies(i, False):
                 copy.start()
-            route(S_X0, i)
-            route(S_CTX, i)
 
             @pl.when(i == 0)
             def _():
@@ -438,7 +460,8 @@
             def _():
                 route_sent(S_GLO, i - 1)
                 route_sent(S_GHI, i - 1)
-                gp_copy(i - 1).wait()
+
+            qkv_copies(i)[0].wait()
 
             for part in range(2):
                 cols = slice(part * hidden_half, (part + 1) * hidden_half)
@@ -447,13 +470,6 @@
                 pdf = 0.3989422804014327 * jnp.exp(-0.5 * u * u)
                 g[:, cols] = (u * cdf).astype(BF16)
                 gpb[:, cols] = (cdf + u * pdf).astype(BF16)
-            gp_copy(i).start()
-            route(OUT_ATT, i)
-            route(S_Y1, i)
-            route(S_Y2, i)
-            route(S_GLO, i)
-            route(S_GHI, i)
-
             @pl.when(i == 0)
             def _():
                 wait_first_of(0, (3,))
@@ -476,9 +492,11 @@
                 for which in range(2):
                     mem_copy(which, i).start()
 
+            gp_copy(i).start()
+            for kind in (S_GLO, S_GHI, S_X0, S_CTX, OUT_ATT, S_Y1, S_Y2, OUT_FF):
+                route(kind, i)
             nff[i] = normed.astype(BF16)
             stats[i] = jnp.where(stat_lane == heads + 1, inv, stats[i])
-            route(OUT_FF, i)
 
         return carry
 
@@ -502,7 +520,7 @@
             for which in range(2):
                 mem_copy(which, i).wait_send()
 
-    for copy in prob_copies(items - 1, False):
+    for copy in prob_copies(items - 1, False) + qkv_copies(items - 1)[1:]:
         copy.wait()
     for copy in prob_copies(items - n, True):
         copy.start()
@@ -527,7 +545,7 @@
             inverse = [stats[i][:, 4 * j + h : 4 * j + h + 1] for h in range(4)]
             c4 = dctx[:, j * quad : (j + 1) * quad].astype(F32) * spread(inverse, head_lanes)
             c4 = c4.astype(BF16)
-            tok_v, mem_v = token_and_memory(i, width + j * quad)
+            tok_v, mem_v = token_and_memory(kv.at[i], width + j * quad)
             return c4, dot(stacked(c4), tok_v, 1, 1), dot(c4, mem_v, 1, 1)
 
         following = prob_grads(0)
@@ -537,7 +555,7 @@
                 following = prob_grads(j + 1)
             cols = slice(j * quad, (j + 1) * quad)
             q4 = q[i, :, cols]
-            tok_k, mem_k = token_and_memory(i, j * quad)
+            tok_k, mem_k = token_and_memory(kv.at[i], j * quad)
             products = c4.astype(F32) * ctx[i, :, cols].astype(F32)
             dp = head_rows(dp)
             inner = [
@@ -578,13 +596,13 @@
 
     def gather_dkv(j, i, slot):
         dkv_copy(j, i, slot).wait_recv()
-        both = (dkvs[c, j].astype(F32) + dkvin[slot, j].astype(F32)).astype(BF16)
-        kv[i, c, :, j * quad : (j + 1) * quad] = both[:, 0:quad]
-        kv[i, c, :, width + j * quad : width + (j + 1) * quad] = both[:, quad:]
+        both = (dkvs[0, j].astype(F32) + dkvin[slot, j].astype(F32)).astype(BF16)
+        kv[i, 0, :, j * quad : (j + 1) * quad] = both[:, 0:quad]
+        kv[i, 0, :, width + j * quad : width + (j + 1) * quad] = both[:, quad:]
 
     def dkv_back(i, low, high):
-        return dot(kv[i, c, :, low:high], wf[0, :, width + low : width + high], 1, 1) + dot(
-            kv[i, c, :, width + low : width + high],
+        return dot(kv[i, 0, :, low:high], wf[0, :, width + low : width + high], 1, 1) + dot(
+            kv[i, 0, :, width + low : width + high],
             wf[0, :, 2 * width + low : 2 * width + high], 1, 1,
         )
 
@@ -737,7 +755,7 @@
             pltpu.VMEM((2, hidden_half, width), BF16),
             pltpu.VMEM((2, 2, width), F32),
             item_rows,
-            item_rows,
+            pltpu.VMEM((n, rows, width), BF16),
             item_rows,
             pltpu.VMEM((items, 2, rows, 2 * width), BF16),
             item_rows,
@@ -758,13 +776,13 @@
             pltpu.VMEM((2, quads, rows, 2 * quad), BF16),
             pltpu.VMEM((2, quads, rows, 2 * quad), BF16),
             pltpu.VMEM((rows, width), F32),
-            pltpu.VMEM((rows, width), BF16),
+            pltpu.VMEM((2, rows, 2 * width), BF16),
             pltpu.VMEM((2, 2, width), F32),
             pltpu.VMEM((2, width), F32),
             pltpu.VMEM((quads, 4 * rows, 2 * toks), BF16),
             pltpu.VMEM((quads, rows, 8 * MEM_PAD), BF16),
             dma((4,)), dma((5,)), dma((5,)),
-            two, one, one, two, two,
+            two, one, one, two, two, two,
             two, two,
             two, two,
             two, two,
@@ -1171,11 +1189,13 @@
 
 
 def finish_kernel(sums, out, gin, norms, first_grad, down_grad, out_copy, gin_copy, gain, shift):
-    width = sums.shape[3]
-    for b in range(4):
-        first_grad[:, b * width : (b + 1) * width] = sums[0, b].astype(F32)
-    for b in range(2):
-        down_grad[b] = sums[0, 4 + b].astype(F32)
+    group, _, part, width = sums.shape
+    for e in range(group):
+        rows = slice(e * part, (e + 1) * part)
+        for b in range(4):
+            first_grad[rows, b * width : (b + 1) * width] = sums[e, b].astype(F32)
+        for b in range(2):
+            down_grad[b, rows] = sums[e, 4 + b].astype(F32)
     out_copy[...] = out[...]
     gin_copy[...] = gin[...]
     gain[...] = norms[0:1]
@@ -1185,12 +1205,12 @@
 def finish(sums, out, gin, norms):
     chunks, _, part, width = sums.shape
     total = out.shape[0]
-    blocks = 8
+    group, blocks = chunks // 3, 2
     tokens = pl.BlockSpec((total // blocks, width), lambda k: (jnp.minimum(k, blocks - 1), 0))
     whole = pl.BlockSpec((1, width), lambda k: (0, 0))
     return pl.pallas_call(
         finish_kernel,
-        grid=(chunks,),
+        grid=(chunks // group,),
         out_shape=(
             jax.ShapeDtypeStruct((width, 4 * width), F32),
             jax.ShapeDtypeStruct((2, width, width), F32),
@@ -1200,19 +1220,20 @@
             jax.ShapeDtypeStruct((1, width), F32),
         ),
         in_specs=[
-            pl.BlockSpec((1, 6, part, width), lambda k: (k, 0, 0, 0)),
+            pl.BlockSpec((group, 6, part, width), lambda k: (k, 0, 0, 0)),
             tokens,
             tokens,
             pl.BlockSpec((2, width), lambda k: (0, 0)),
         ],
         out_specs=[
-            pl.BlockSpec((part, 4 * width), lambda k: (k, 0)),
-            pl.BlockSpec((2, part, width), lambda k: (0, k, 0)),
+            pl.BlockSpec((group * part, 4 * width), lambda k: (k, 0)),
+            pl.BlockSpec((2, group * part, width), lambda k: (0, k, 0)),
             tokens,
             tokens,
             whole,
             whole,
         ],
+        compiler_params=pltpu.CompilerParams(vmem_limit_bytes=40 * 1024 * 1024),
     )(sums, out, gin, norms)
 
 
@@ -1224,7 +1245,7 @@
     rows = length // NSEG // 2 + MEM_PAD
     out, gin, sx1, sx2, sr, sg, sd, norm_grad, _, _ = run_layers(
         n, NSEG, H, tokens, cotangent, first_weights, down_halves,
-        doc_ids, reset_flags, norm_gain, norm_bias,
+        doc_ids, reset_flags.T, norm_gain, norm_bias,
     )
     total = 2 * items * rows
     sx1, sx2, sd = (a.reshape(total, width) for a in (sx1, sx2, sd))

time: 346 us -> 345 us (level)
  Pallas kernels: 343 us -> 338 us
  local copies, waits for them, and re-layouts: 1.3 us -> 5.59 us
    pallas_call x1, Pallas kernels: 14.6 us -> 7.46 us  [finish(): pl.pallas_call(finish_kernel, grid=(chunks // group,), out_shape=(jax.Sha...]
    unnamed x1 -> x8, local copies, waits for them, and re-layouts: 1.3 us -> 5.59 us
where the time goes in v7:
time: 345 us; the launch traced here: 344 us
  Pallas kernels  338 us (98%)
  local copies, waits for them, and re-layouts  5.59 us (2%)
    pallas_call x1, Pallas kernels, run_layers(): pl.pallas_call(partial(layers_kernel, n, nseg, heads), out_shape=(jax.Sha...  185 us
    pallas_call x1, Pallas kernels, sum_weights(): pl.pallas_call(partial(reduce_kernel, chunks), out_shape=(jax.ShapeDtypeS...  146 us
    pallas_call x1, Pallas kernels, finish(): pl.pallas_call(finish_kernel, grid=(chunks // group,), out_shape=(jax.Sha...  7.46 us

profile of v7, /device:TPU:0, one launch (start us, length us, event | category | flops | bytes accessed | tf_op | source)
XLA Modules:
  0.0 344.3 jit_solution(8052176294818029118)
XLA Ops:
  0.6 185.0 %shard_map.127 = (bf16[2,1024,768]{2,1,0:T(8,128)(2,1)}, bf16[2,1024,768]{2,1,0:T(8,128)(2,1)}, bf16[8,272,768]{2,1,0:T(8,128)(2,1)}, bf16[8,272,768]{2,1,0:T(8,...) custom-call(bf16[2,1024,768]{2,1,0:T(8,128)(2,1)} %tokens.1, ...), custom_call_target="tpu_custom_call" | custom-call | tf_op jit(solution)/shard_map/pallas_call | solution.py:737
  185.6 0.0 copy-start.1
  185.6 145.5 %shard_map.128 = (bf16[12,6,64,768]{3,2,1,0:T(8,128)(2,1)}, f32[2,768]{1,0:T(2,128)}) custom-call(bf16[2176,768]{1,0:T(8,128)(2,1)} %bitcast.16, bf16[2176,768]{1,0:T(8,128)(2,1)} %bitcast.17, bf16[2176,3072]{1,0:T(8,128)(2,1)} %bitcast.14, bf16[2176,1536]{1,0:T(8,128)(2,1)} %bitcast.15, bf16[2176,768]{1,0:T(8,128)(2,1)} %bitcast.18, ...), custom_call_target="tpu_custom_call" | custom-call | tf_op jit(solution)/shard_map/pallas_call | solution.py:1151
  331.2 0.0 copy-done.1
  331.2 0.0 copy-start
  331.2 3.0 copy-done
  334.2 0.0 copy-start.2
  334.2 1.9 copy-done.2
  336.1 0.0 copy-start.3
  336.1 0.7 copy-done.3
  336.8 7.5 %shard_map.129 = (f32[768,3072]{1,0:T(8,128)}, f32[2,768,768]{2,1,0:T(8,128)}, bf16[2048,768]{1,0:T(8,128)(2,1)}, bf16[2048,768]{1,0:T(8,128)(2,1)}, f32[1,768]{1,0:T(1,128)}, /*index=5*/f32[1,768]{1,0:T(1,128)}) custom-call(bf16[12,6,64,768]{3,2,1,0:T(8,128)(2,1)S(1)} %copy-done, bf16[2048,768]{1,0:T(8,128)(2,1)S(1)} %bitcast.12, ...), custom_call_target="tpu_custom_call" | custom-call | tf_op jit(solution)/shard_map/pallas_call | solution.py:1211
Async XLA Ops:
  185.6 145.5 %copy-start.1 = (bf16[2,1024,768]{2,1,0:T(8,128)(2,1)S(1)}, bf16[2,1024,768]{2,1,0:T(8,128)(2,1)}, u32[]{:S(2)}) copy-start(bf16[2,1024,768]{2,1,0:T(8,128)(2,1)} %get-tuple-element.29) | copy-start | bytes 9437188
  331.2 3.0 copy-start
  334.2 1.9 copy-start.2
  336.1 0.7 copy-start.3

commit v8 on v7

--- a/solution.py
+++ b/solution.py
@@ -592,7 +592,11 @@
                     dkvs[core, j, toks:rows, cols] = mem_part[
                         core * MEM_PAD : (core + 1) * MEM_PAD
                     ].astype(BF16)
-            dkv_copy(j, i, slot).start()
+            if j == quads - 1:
+                dkv_copy(j, i, slot).start()
+            elif j == quads - 2:
+                for ready in range(quads - 1):
+                    dkv_copy(ready, i, slot).start()
 
     def gather_dkv(j, i, slot):
         dkv_copy(j, i, slot).wait_recv()
@@ -851,12 +855,6 @@
     left_load(1, 0).start()
     left_load(2, 0).start()
     right_load(4).start()
-    left_load(3, 0).start()
-    for k in range(1, 4):
-        right_load(k).start()
-    for group in range(1, lane_groups):
-        for which in range(4):
-            left_load(which, group).start()
 
     norms[d] = norm_part[...]
     pl.semaphore_wait(barrier, dp - 1)
@@ -961,6 +959,12 @@
         @pl.when(r == 0)
         def _():
             right_load(4).wait()
+            left_load(3, 0).start()
+            for k in range(1, 4):
+                right_load(k).start()
+            for later in range(1, lane_groups):
+                for which in range(4):
+                    left_load(which, later).start()
 
         store_chunks(group, 3, dot(x2[:, cols], rr[:, 3 * width :], 0, 0).astype(BF16))
 
@@ -1233,7 +1237,7 @@
             whole,
             whole,
         ],
-        compiler_params=pltpu.CompilerParams(vmem_limit_bytes=40 * 1024 * 1024),
+        compiler_params=pltpu.CompilerParams(vmem_limit_bytes=61 * 1024 * 1024),
     )(sums, out, gin, norms)
 
 

time: 345 us -> 344 us (level)
  local copies, waits for them, and re-layouts: 5.59 us -> 0 us
  Pallas kernels: 338 us -> 343 us
    unnamed x8 -> x0, local copies, waits for them, and re-layouts: 5.59 us -> none
where the time goes in v8:
time: 344 us; the launch traced here: 343 us
  Pallas kernels  343 us (100%)
    pallas_call x1, Pallas kernels, run_layers(): pl.pallas_call(partial(layers_kernel, n, nseg, heads), out_shape=(jax.Sha...  185 us
    pallas_call x1, Pallas kernels, sum_weights(): pl.pallas_call(partial(reduce_kernel, chunks), out_shape=(jax.ShapeDtypeS...  147 us
    pallas_call x1, Pallas kernels, finish(): pl.pallas_call(finish_kernel, grid=(chunks // group,), out_shape=(jax.Sha...  10.5 us

profile of v8, /device:TPU:0, one launch (start us, length us, event | category | flops | bytes accessed | tf_op | source)
XLA Modules:
  0.0 343.4 jit_solution(5658693088242398330)
XLA Ops:
  0.6 184.7 %shard_map.127 = (bf16[2,1024,768]{2,1,0:T(8,128)(2,1)}, bf16[2,1024,768]{2,1,0:T(8,128)(2,1)}, bf16[8,272,768]{2,1,0:T(8,128)(2,1)}, bf16[8,272,768]{2,1,0:T(8,...) custom-call(bf16[2,1024,768]{2,1,0:T(8,128)(2,1)} %tokens.1, ...), custom_call_target="tpu_custom_call" | custom-call | tf_op jit(solution)/shard_map/pallas_call | solution.py:741
  185.3 147.4 %shard_map.128 = (bf16[12,6,64,768]{3,2,1,0:T(8,128)(2,1)}, f32[2,768]{1,0:T(2,128)}) custom-call(bf16[2176,768]{1,0:T(8,128)(2,1)} %bitcast.14, bf16[2176,768]{1,0:T(8,128)(2,1)} %bitcast.15, bf16[2176,3072]{1,0:T(8,128)(2,1)} %bitcast.12, bf16[2176,1536]{1,0:T(8,128)(2,1)} %bitcast.13, bf16[2176,768]{1,0:T(8,128)(2,1)} %bitcast.16, ...), custom_call_target="tpu_custom_call" | custom-call | tf_op jit(solution)/shard_map/pallas_call | solution.py:1155
  332.8 10.5 %shard_map.129 = (f32[768,3072]{1,0:T(8,128)}, f32[2,768,768]{2,1,0:T(8,128)}, bf16[2048,768]{1,0:T(8,128)(2,1)}, bf16[2048,768]{1,0:T(8,128)(2,1)}, f32[1,768]{1,0:T(1,128)}, /*index=5*/f32[1,768]{1,0:T(1,128)}) custom-call(bf16[12,6,64,768]{3,2,1,0:T(8,128)(2,1)} %get-tuple-element.28.sums, bf16[2048,768]{1,0:T(8,128)(2,1)} %bitcast.17, ...), custom_call_target="tpu_custom_call" | custom-call | tf_op jit(solution)/shard_map/pallas_call | solution.py:1215

commit v9 on v8

--- a/solution.py
+++ b/solution.py
@@ -21,7 +21,8 @@
 OUT_ATT, OUT_FF, GIN_ATT, GIN_FF = 0, 1, 2, 3
 S_X0, S_CTX, S_DQ, S_DKV, S_DATT, S_GLO, S_DFF0 = 4, 5, 6, 7, 8, 9, 10
 S_Y1, S_Y2, S_DU, S_GHI, S_DFF1 = 11, 12, 13, 14, 15
-KINDS = 16
+S_DV, S_LASTK, S_LASTV = 16, 17, 18
+KINDS = 19
 
 
 def dot(a, b, lhs_dim=1, rhs_dim=0):
@@ -196,8 +197,12 @@
             src, dst = ctx.at[i], sx2.at[block]
         elif kind == S_DQ:
             src, dst = dqb, sr.at[block, :, 0:width]
-        elif kind == S_DKV:
-            src, dst = kv.at[i, 0], sr.at[block, :, width:wide]
+        elif kind in (S_DKV, S_DV, S_LASTK, S_LASTV):
+            last = width - width // quads
+            low, high = (0, last) if kind in (S_DKV, S_DV) else (last, width)
+            if kind in (S_DV, S_LASTV):
+                low, high = low + width, high + width
+            src, dst = kv.at[i, 0, :, low:high], sr.at[block, :, width + low : width + high]
         elif kind == S_DATT:
             src, dst = natt.at[i], sr.at[block, :, wide:]
         elif kind == S_GLO:
@@ -376,15 +381,37 @@
         stats[i] = st
         ctx[i] = ctxb[...]
 
+    def to_queries(product):
+        return product.astype(BF16) * BF16(scale)
+
     def forward_tick(t, carry):
         i = t - x
 
         @pl.when((i >= 0) & (i < items))
         def _():
+            ahead = (x == 0) & (i >= n) & (lax.rem(i, n) == 0)
+
+            @pl.when(i > 0)
+            def _():
+                qkv_copies(i - 1)[1].wait()
+                gp_copy(i - 1).wait()
+
             @pl.when(x == 0)
             def _():
+                token_copy(0, i).wait()
+                token_copy(1, i).wait()
+
+            @pl.when(ahead)
+            def _():
+                kvb[0, 0:toks, :] = dot(x0[i, 0:toks, :], wf[0, :, width:wide]).astype(BF16)
+                kvb[1, 0:toks, :] = dot(
+                    xo[lax.rem(i, n), 0:toks, :], wf[0, :, width:wide]
+                ).astype(BF16)
+                qb[0:toks, :] = to_queries(dot(x0[i, 0:toks, :], wf[0, :, 0:width]))
+
+            @pl.when(x == 0)
+            def _():
                 for which, rows_ref in enumerate((x0.at[i], xo.at[lax.rem(i, n)])):
-                    token_copy(which, i).wait()
 
                     @pl.when(i < n)
                     def _():
@@ -407,25 +434,33 @@
             def _():
                 wait_first_of(0, (0,))
 
-            @pl.when(i > 0)
-            def _():
-                qkv_copies(i - 1)[1].wait()
-                gp_copy(i - 1).wait()
-
-            kvb[0] = dot(x0[i], wf[0, :, width:wide]).astype(BF16)
-
-            @pl.when(i == 0)
-            def _():
-                wait_first_of(0, (1,))
-
-            qb[...] = dot(x0[i], wf[0, :, 0:width]).astype(BF16) * BF16(scale)
-
-            @pl.when(x == 1)
-            def _():
-                for p in range(2):
-                    pass_copy(p, i).wait_recv()
-
-            kvb[1] = dot(xo[lax.rem(i, n)], wf[0, :, width:wide]).astype(BF16)
+            @pl.when(ahead)
+            def _():
+                memory = jnp.concatenate(
+                    [x0[i, toks:rows, :], xo[lax.rem(i, n), toks:rows, :]], axis=0
+                )
+                both = dot(memory, wf[0, :, width:wide]).astype(BF16)
+                kvb[0, toks:rows, :] = both[0:MEM_PAD]
+                kvb[1, toks:rows, :] = both[MEM_PAD:]
+                qb[toks:rows, :] = to_queries(dot(memory, wf[0, :, 0:width])[0:MEM_PAD])
+
+            @pl.when(jnp.logical_not(ahead))
+            def _():
+                kvb[0] = dot(x0[i], wf[0, :, width:wide]).astype(BF16)
+
+                @pl.when(i == 0)
+                def _():
+                    wait_first_of(0, (1,))
+
+                qb[...] = to_queries(dot(x0[i], wf[0, :, 0:width]))
+
+                @pl.when(x == 1)
+                def _():
+                    for p in range(2):
+                        pass_copy(p, i).wait_recv()
+
+                kvb[1] = dot(xo[lax.rem(i, n)], wf[0, :, width:wide]).astype(BF16)
+
             for copy in qkv_copies(i):
                 copy.start()
 
@@ -670,13 +705,17 @@
 
             for j in range(quads - 1):
                 gather_dkv(j, i, slot)
+            if quads > 1:
+                route(S_DKV, i)
+                route(S_DV, i)
             early = (quads - 1) * quad
             partial_sum = dot(dqb[...], wf[0, :, 0:width], 1, 1) + dhb[...]
             if early:
                 partial_sum = partial_sum + dkv_back(i, 0, early)
             dhb[...] = partial_sum
             gather_dkv(quads - 1, i, slot)
-            route(S_DKV, i)
+            route(S_LASTK, i)
+            route(S_LASTV, i)
             forward_sent(i)
             yd[i] = (dkv_back(i, early, width) + dhb[...]).astype(BF16)
 
@@ -709,6 +748,8 @@
             mg_copy(i).wait_send()
 
         for kind in range(KINDS):
+            if quads == 1 and kind in (S_DKV, S_DV):
+                continue
             if kind not in (OUT_FF, S_GLO, S_GHI, S_DQ, GIN_FF):
                 route_sent(kind, i)
             route_received(kind, i)

time: 344 us -> 344 us (level)
  no operation moved by 1% of the time
where the time goes in v9:
time: 344 us
  Pallas kernels  343 us (100%)
    pallas_call x1, Pallas kernels, run_layers(): pl.pallas_call(partial(layers_kernel, n, nseg, heads), out_shape=(jax.Sha...  185 us
    pallas_call x1, Pallas kernels, sum_weights(): pl.pallas_call(partial(reduce_kernel, chunks), out_shape=(jax.ShapeDtypeS...  147 us
    pallas_call x1, Pallas kernels, finish(): pl.pallas_call(finish_kernel, grid=(chunks // group,), out_shape=(jax.Sha...  10.5 us

profile of v9, /device:TPU:0, one launch (start us, length us, event | category | flops | bytes accessed | tf_op | source)
XLA Modules:
  0.0 343.8 jit_solution(11012092415751715061)
XLA Ops:
  0.6 185.1 %shard_map.127 = (bf16[2,1024,768]{2,1,0:T(8,128)(2,1)}, bf16[2,1024,768]{2,1,0:T(8,128)(2,1)}, bf16[8,272,768]{2,1,0:T(8,128)(2,1)}, bf16[8,272,768]{2,1,0:T(8,...) custom-call(bf16[2,1024,768]{2,1,0:T(8,128)(2,1)} %tokens.1, ...), custom_call_target="tpu_custom_call" | custom-call | tf_op jit(solution)/shard_map/pallas_call | solution.py:782
  185.7 147.4 %shard_map.128 = (bf16[12,6,64,768]{3,2,1,0:T(8,128)(2,1)}, f32[2,768]{1,0:T(2,128)}) custom-call(bf16[2176,768]{1,0:T(8,128)(2,1)} %bitcast.14, bf16[2176,768]{1,0:T(8,128)(2,1)} %bitcast.15, bf16[2176,3072]{1,0:T(8,128)(2,1)} %bitcast.12, bf16[2176,1536]{1,0:T(8,128)(2,1)} %bitcast.13, bf16[2176,768]{1,0:T(8,128)(2,1)} %bitcast.16, ...), custom_call_target="tpu_custom_call" | custom-call | tf_op jit(solution)/shard_map/pallas_call | solution.py:1196
  333.1 10.5 %shard_map.129 = (f32[768,3072]{1,0:T(8,128)}, f32[2,768,768]{2,1,0:T(8,128)}, bf16[2048,768]{1,0:T(8,128)(2,1)}, bf16[2048,768]{1,0:T(8,128)(2,1)}, f32[1,768]{1,0:T(1,128)}, /*index=5*/f32[1,768]{1,0:T(1,128)}) custom-call(bf16[12,6,64,768]{3,2,1,0:T(8,128)(2,1)} %get-tuple-element.28.sums, bf16[2048,768]{1,0:T(8,128)(2,1)} %bitcast.17, ...), custom_call_target="tpu_custom_call" | custom-call | tf_op jit(solution)/shard_map/pallas_call | solution.py:1256

commit v10 on v9

--- a/solution.py
+++ b/solution.py
@@ -510,17 +510,25 @@
                 wait_first_of(0, (3,))
                 wait_first_of(1, (3,))
 
-            normed, inv = normalize(
-                dot(g[:, 0:hidden_half], wd[0])
-                + dot(g[:, hidden_half:], wd[1])
-                + yatt[i].astype(F32)
-            )
-            yd[i] = (normed * nrm[1, 0:1, :] + nrm[1, 1:2, :]).astype(BF16)
+            def finish_rows(part):
+                normed, inv = normalize(
+                    dot(g[part, 0:hidden_half], wd[0])
+                    + dot(g[part, hidden_half:], wd[1])
+                    + yatt[i, part].astype(F32)
+                )
+                yd[i, part] = (normed * nrm[1, 0:1, :] + nrm[1, 1:2, :]).astype(BF16)
+                nff[i, part] = normed.astype(BF16)
+                stats[i, part] = jnp.where(stat_lane[part] == heads + 1, inv, stats[i, part])
 
             @pl.when(x == 0)
             def _():
                 for p in range(2):
+                    finish_rows(piece(p))
                     x_copy(p, i).start()
+
+            @pl.when(x == 1)
+            def _():
+                finish_rows(slice(0, rows))
 
             @pl.when((x == 1) & (i < items - n))
             def _():
@@ -530,8 +538,6 @@
             gp_copy(i).start()
             for kind in (S_GLO, S_GHI, S_X0, S_CTX, OUT_ATT, S_Y1, S_Y2, OUT_FF):
                 route(kind, i)
-            nff[i] = normed.astype(BF16)
-            stats[i] = jnp.where(stat_lane == heads + 1, inv, stats[i])
 
         return carry
 

time: 344 us -> 340 us (0.988)
  Pallas kernels: 343 us -> 339 us
    pallas_call x1, Pallas kernels: 185 us -> 181 us  [run_layers(): pl.pallas_call(partial(layers_kernel, n, nseg, heads), out_shape=(jax.Sha...]
where the time goes in v10:
time: 340 us
  Pallas kernels  339 us (100%)
    pallas_call x1, Pallas kernels, run_layers(): pl.pallas_call(partial(layers_kernel, n, nseg, heads), out_shape=(jax.Sha...  181 us
    pallas_call x1, Pallas kernels, sum_weights(): pl.pallas_call(partial(reduce_kernel, chunks), out_shape=(jax.ShapeDtypeS...  147 us
    pallas_call x1, Pallas kernels, finish(): pl.pallas_call(finish_kernel, grid=(chunks // group,), out_shape=(jax.Sha...  10.5 us

profile of v10, /device:TPU:0, one launch (start us, length us, event | category | flops | bytes accessed | tf_op | source)
XLA Modules:
  0.0 339.6 jit_solution(4772631948063351384)
XLA Ops:
  0.6 180.8 %shard_map.127 = (bf16[2,1024,768]{2,1,0:T(8,128)(2,1)}, bf16[2,1024,768]{2,1,0:T(8,128)(2,1)}, bf16[8,272,768]{2,1,0:T(8,128)(2,1)}, bf16[8,272,768]{2,1,0:T(8,...) custom-call(bf16[2,1024,768]{2,1,0:T(8,128)(2,1)} %tokens.1, ...), custom_call_target="tpu_custom_call" | custom-call | tf_op jit(solution)/shard_map/pallas_call | solution.py:788
  181.5 147.5 %shard_map.128 = (bf16[12,6,64,768]{3,2,1,0:T(8,128)(2,1)}, f32[2,768]{1,0:T(2,128)}) custom-call(bf16[2176,768]{1,0:T(8,128)(2,1)} %bitcast.14, bf16[2176,768]{1,0:T(8,128)(2,1)} %bitcast.15, bf16[2176,3072]{1,0:T(8,128)(2,1)} %bitcast.12, bf16[2176,1536]{1,0:T(8,128)(2,1)} %bitcast.13, bf16[2176,768]{1,0:T(8,128)(2,1)} %bitcast.16, ...), custom_call_target="tpu_custom_call" | custom-call | tf_op jit(solution)/shard_map/pallas_call | solution.py:1202
  329.0 10.5 %shard_map.129 = (f32[768,3072]{1,0:T(8,128)}, f32[2,768,768]{2,1,0:T(8,128)}, bf16[2048,768]{1,0:T(8,128)(2,1)}, bf16[2048,768]{1,0:T(8,128)(2,1)}, f32[1,768]{1,0:T(1,128)}, /*index=5*/f32[1,768]{1,0:T(1,128)}) custom-call(bf16[12,6,64,768]{3,2,1,0:T(8,128)(2,1)} %get-tuple-element.28.sums, bf16[2048,768]{1,0:T(8,128)(2,1)} %bitcast.17, ...), custom_call_target="tpu_custom_call" | custom-call | tf_op jit(solution)/shard_map/pallas_call | solution.py:1262

commit v11 on v10

--- a/solution.py
+++ b/solution.py
@@ -298,8 +298,10 @@
             mr_sem.at[which, i], cross_peer if which else chip_peer,
         )
 
-    def gy_copy(i):
-        return remote(yd.at[i], gy.at[i], gs_sem.at[i], gr_sem.at[i], chip_peer)
+    def gy_copy(p, i):
+        return remote(
+            yd.at[i, piece(p)], gy.at[i, piece(p)], gs_sem.at[p, i], gr_sem.at[p, i], chip_peer
+        )
 
     def mg_copy(i):
         return remote(
@@ -645,9 +647,9 @@
         kv[i, 0, :, j * quad : (j + 1) * quad] = both[:, 0:quad]
         kv[i, 0, :, width + j * quad : width + (j + 1) * quad] = both[:, quad:]
 
-    def dkv_back(i, low, high):
-        return dot(kv[i, 0, :, low:high], wf[0, :, width + low : width + high], 1, 1) + dot(
-            kv[i, 0, :, width + low : width + high],
+    def dkv_back(i, low, high, part):
+        return dot(kv[i, 0, part, low:high], wf[0, :, width + low : width + high], 1, 1) + dot(
+            kv[i, 0, part, width + low : width + high],
             wf[0, :, 2 * width + low : 2 * width + high], 1, 1,
         )
 
@@ -679,7 +681,8 @@
 
             @pl.when(x == 0)
             def _():
-                gy_copy(i).wait_recv()
+                for p in range(2):
+                    gy_copy(p, i).wait_recv()
 
             @pl.when(r > 0)
             def _():
@@ -717,17 +720,19 @@
             early = (quads - 1) * quad
             partial_sum = dot(dqb[...], wf[0, :, 0:width], 1, 1) + dhb[...]
             if early:
-                partial_sum = partial_sum + dkv_back(i, 0, early)
+                partial_sum = partial_sum + dkv_back(i, 0, early, slice(0, rows))
             dhb[...] = partial_sum
             gather_dkv(quads - 1, i, slot)
             route(S_LASTK, i)
             route(S_LASTV, i)
             forward_sent(i)
-            yd[i] = (dkv_back(i, early, width) + dhb[...]).astype(BF16)
-
-            @pl.when(x == 1)
-            def _():
-                gy_copy(i).start()
+            for p in range(2):
+                part = piece(p)
+                yd[i, part] = (dkv_back(i, early, width, part) + dhb[part, :]).astype(BF16)
+
+                @pl.when(x == 1)
+                def _():
+                    gy_copy(p, i).start()
 
             @pl.when((x == 0) & (i >= n))
             def _():
@@ -747,7 +752,8 @@
     def backward_drain(i, carry):
         @pl.when(x == 1)
         def _():
-            gy_copy(i).wait_send()
+            for p in range(2):
+                gy_copy(p, i).wait_send()
 
         @pl.when((x == 0) & (i >= n))
         def _():
@@ -837,7 +843,7 @@
             two, two,
             two, two,
             two, two,
-            one, one, one, one,
+            two, two, one, one,
             dma((quads, items)), dma((quads, items)),
             dma(()), dma(()),
         ]

time: 340 us -> 342 us (level)
  no operation moved by 1% of the time
where the time goes in v11:
time: 342 us; the launch traced here: 341 us
  Pallas kernels  341 us (100%)
    pallas_call x1, Pallas kernels, run_layers(): pl.pallas_call(partial(layers_kernel, n, nseg, heads), out_shape=(jax.Sha...  183 us
    pallas_call x1, Pallas kernels, sum_weights(): pl.pallas_call(partial(reduce_kernel, chunks), out_shape=(jax.ShapeDtypeS...  147 us
    pallas_call x1, Pallas kernels, finish(): pl.pallas_call(finish_kernel, grid=(chunks // group,), out_shape=(jax.Sha...  10.5 us

profile of v11, /device:TPU:0, one launch (start us, length us, event | category | flops | bytes accessed | tf_op | source)
XLA Modules:
  0.0 341.4 jit_solution(11044634119640914593)
XLA Ops:
  0.6 182.7 %shard_map.127 = (bf16[2,1024,768]{2,1,0:T(8,128)(2,1)}, bf16[2,1024,768]{2,1,0:T(8,128)(2,1)}, bf16[8,272,768]{2,1,0:T(8,128)(2,1)}, bf16[8,272,768]{2,1,0:T(8,...) custom-call(bf16[2,1024,768]{2,1,0:T(8,128)(2,1)} %tokens.1, ...), custom_call_target="tpu_custom_call" | custom-call | tf_op jit(solution)/shard_map/pallas_call | solution.py:794
  183.3 147.4 %shard_map.128 = (bf16[12,6,64,768]{3,2,1,0:T(8,128)(2,1)}, f32[2,768]{1,0:T(2,128)}) custom-call(bf16[2176,768]{1,0:T(8,128)(2,1)} %bitcast.14, bf16[2176,768]{1,0:T(8,128)(2,1)} %bitcast.15, bf16[2176,3072]{1,0:T(8,128)(2,1)} %bitcast.12, bf16[2176,1536]{1,0:T(8,128)(2,1)} %bitcast.13, bf16[2176,768]{1,0:T(8,128)(2,1)} %bitcast.16, ...), custom_call_target="tpu_custom_call" | custom-call | tf_op jit(solution)/shard_map/pallas_call | solution.py:1208
  330.8 10.5 %shard_map.129 = (f32[768,3072]{1,0:T(8,128)}, f32[2,768,768]{2,1,0:T(8,128)}, bf16[2048,768]{1,0:T(8,128)(2,1)}, bf16[2048,768]{1,0:T(8,128)(2,1)}, f32[1,768]{1,0:T(1,128)}, /*index=5*/f32[1,768]{1,0:T(1,128)}) custom-call(bf16[12,6,64,768]{3,2,1,0:T(8,128)(2,1)} %get-tuple-element.28.sums, bf16[2048,768]{1,0:T(8,128)(2,1)} %bitcast.17, ...), custom_call_target="tpu_custom_call" | custom-call | tf_op jit(solution)/shard_map/pallas_call | solution.py:1268
